TPU v7x, 32 devices: a whole 2x2x4 slice. The times are simulated.
32 devices in a mesh: dp: 8 (over y, x, core), tensor: 4 (over z).
Axes of the slice: x: 2, y: 2, z: 4, core: 2. Of those that a mesh axis runs over, the one named last changes fastest.
Arguments:
- block_in: bfloat16 [4096, 2048], P(('dp', 'tensor')), may hold values from -6 to 6
- attn_norm_gain: bfloat16 [2048], P(('dp', 'tensor')), may hold values from 0.5 to 1.5
- query_weight: bfloat16 [2048, 3072], P('dp', 'tensor'), may hold values from -0.125 to 0.125
- kv_down_weight: bfloat16 [2048, 576], P(('dp', 'tensor')), may hold values from -0.125 to 0.125
- latent_gain: bfloat16 [512], P(('dp', 'tensor')), may hold values from 0.5 to 1.5
- kv_up_weight: bfloat16 [512, 4096], P('dp', 'tensor'), may hold values from -0.25 to 0.25
- output_weight: bfloat16 [2048, 2048], P('tensor', 'dp'), may hold values from -0.5 to 0.5
- ffn_norm_gain: bfloat16 [2048], P(('dp', 'tensor')), may hold values from 0.5 to 1.5
- router_weight: bfloat16 [2048, 64], P(('dp', 'tensor')), may hold values from -0.125 to 0.125
- expert_ids: int32 [4096, 6], P('dp'), may hold values from 0 to 63, all different within a row; in each aligned block of 512 rows (0 to 511, 512 to 1023, ...) at most 96 rows name the same one
- shared_gate_weight: bfloat16 [2048, 2816], P('dp', 'tensor'), may hold values from -0.125 to 0.125
- shared_up_weight: bfloat16 [2048, 2816], P('dp', 'tensor'), may hold values from -0.125 to 0.125
- shared_down_weight: bfloat16 [2816, 2048], P('tensor', 'dp'), may hold values from -0.109375 to 0.109375
- expert_gate_weight: bfloat16 [8, 2048, 1408], P(None, 'dp', 'tensor'), may hold values from -0.125 to 0.125
- expert_up_weight: bfloat16 [8, 2048, 1408], P(None, 'dp', 'tensor'), may hold values from -0.125 to 0.125
- expert_down_weight: bfloat16 [8, 1408, 2048], P(None, 'tensor', 'dp'), may hold values from -2.5 to 2.5
- out_grad: bfloat16 [4096, 2048], P(('dp', 'tensor')), may hold values from -6 to 6
Outputs:
- block_out: bfloat16 [4096, 2048], P(('dp', 'tensor'))
- input_grad: float32 [4096, 2048], P(('dp', 'tensor'))
- attn_norm_gain_grad: float32 [2048], P(('dp', 'tensor'))
- query_weight_grad: float32 [2048, 3072], P('dp', 'tensor')
- kv_down_weight_grad: float32 [2048, 576], P(('dp', 'tensor'))
- latent_gain_grad: float32 [512], P(('dp', 'tensor'))
- kv_up_weight_grad: float32 [512, 4096], P('dp', 'tensor')
- output_weight_grad: float32 [2048, 2048], P('tensor', 'dp')
- ffn_norm_gain_grad: float32 [2048], P(('dp', 'tensor'))
- router_weight_grad: float32 [2048, 64], P(('dp', 'tensor'))
- shared_gate_weight_grad: float32 [2048, 2816], P('dp', 'tensor')
- shared_up_weight_grad: float32 [2048, 2816], P('dp', 'tensor')
- shared_down_weight_grad: float32 [2816, 2048], P('tensor', 'dp')
- expert_gate_weight_grad: float32 [8, 2048, 1408], P(None, 'dp', 'tensor')
- expert_up_weight_grad: float32 [8, 2048, 1408], P(None, 'dp', 'tensor')
- expert_down_weight_grad: float32 [8, 1408, 2048], P(None, 'tensor', 'dp')
Inputs may be any that keep to these rules, and one draw needn't show every extreme that they name: `expert_ids`: each row names 6 different experts. Of the 512 rows of one index of dp, at most 96 name the same expert, a bound that some block reaches of them.
All inputs are finite; a program needn't handle non-finite values.
Results may differ from a plain program's by a relative error of at most 0.02.
Values may be sent and summed in bfloat16 or wider, within the bound.
No kernel may reach another device: no remote copies, remote signals or barrier semaphores. Data moves between devices by JAX's collectives and lax.ppermute only.
A program may use at most 192 MiB of HBM per device.

v0:
```python
import jax
import jax.numpy as jnp
from jax import lax
from jax.sharding import PartitionSpec as P

NOPE = 128
ROPE = 64
VDIM = 128
LATENT = 512
ACTIVE = 8
SEQ = 512
CAP = 96


EPSILON = 1e-06
NEGATIVE = -1e30


def matmul(left, right):
    return jnp.dot(left, right, preferred_element_type=jnp.float32)


def left_dot(left, right):
    return lax.dot_general(
        left, right, (((0,), (0,)), ((), ())), preferred_element_type=jnp.float32
    )


def right_dot(left, right):
    return lax.dot_general(
        left, right, (((left.ndim - 1,), (1,)), ((), ())), preferred_element_type=jnp.float32
    )


def einsum32(form, left, right):
    return jnp.einsum(form, left, right, preferred_element_type=jnp.float32)


def rms_scale(values):
    return lax.rsqrt(jnp.mean(values * values, axis=-1, keepdims=True) + EPSILON)


def norm_back(grad_normed, normed, scale):
    return scale * (grad_normed - normed * jnp.mean(grad_normed * normed, axis=-1, keepdims=True))


def silu_grad(values):
    sigma = jax.nn.sigmoid(values)
    return sigma * (1.0 + values * (1.0 - sigma))


def rope_tables(count):
    position = (jnp.arange(count) % SEQ).astype(jnp.float32)
    halfway = ROPE // 2
    inverse = jnp.exp(-jnp.log(10000.0) * jnp.arange(halfway).astype(jnp.float32) / halfway)
    angles = position[:, None] * inverse[None, :]
    return (jnp.cos(angles), jnp.sin(angles))


def rotate(values, cosine, sine):
    halfway = ROPE // 2
    first, second = (values[..., :halfway], values[..., halfway:])
    return jnp.concatenate(
        [first * cosine - second * sine, first * sine + second * cosine], axis=-1
    )


def unrotate(grads, cosine, sine):
    halfway = ROPE // 2
    first, second = (grads[..., :halfway], grads[..., halfway:])
    return jnp.concatenate(
        [first * cosine + second * sine, second * cosine - first * sine], axis=-1
    )


def causal_scores(query_nope, query_rope, key_nope, key_rope):
    scores = einsum32("qhd,khd->hqk", query_nope, key_nope)
    scores = scores + einsum32("qhd,kd->hqk", query_rope, key_rope)
    length = query_nope.shape[0]
    causal = jnp.arange(length)[:, None] >= jnp.arange(length)[None, :]
    return jnp.where(causal[None], scores * (NOPE + ROPE) ** (-0.5), NEGATIVE)


def attend_forward(blocks):
    query_nope, query_rope, key_nope, key_rope, values = blocks
    scores = causal_scores(query_nope, query_rope, key_nope, key_rope)
    logsum = jax.nn.logsumexp(scores, axis=-1)
    probs = jnp.exp(scores - logsum[..., None]).astype(jnp.bfloat16)
    return (einsum32("hqk,khd->qhd", probs, values).astype(jnp.bfloat16), logsum)


def attend_backward(blocks):
    query_nope, query_rope, key_nope, key_rope, values, mixed, mixed_grad, logsum = blocks
    scores = causal_scores(query_nope, query_rope, key_nope, key_rope)
    probs_full = jnp.exp(scores - logsum[..., None])
    probs = probs_full.astype(jnp.bfloat16)
    values_grad = einsum32("hqk,qhd->khd", probs, mixed_grad)
    probs_grad = einsum32("qhd,khd->hqk", mixed_grad, values)
    delta = einsum32("qhd,qhd->hq", mixed_grad, mixed)
    score_grad = (probs_full * (probs_grad - delta[..., None]) * (NOPE + ROPE) ** (-0.5)).astype(
        jnp.bfloat16
    )
    query_nope_grad = einsum32("hqk,khd->qhd", score_grad, key_nope)
    query_rope_grad = einsum32("hqk,kd->qhd", score_grad, key_rope)
    key_nope_grad = einsum32("hqk,qhd->khd", score_grad, query_nope)
    key_rope_grad = einsum32("hqk,qhd->kd", score_grad, query_rope)
    return (query_nope_grad, query_rope_grad, key_nope_grad, key_rope_grad, values_grad)


def fetch_dense(
    query_weight,
    kv_up_weight,
    output_weight,
    shared_gate_weight,
    shared_up_weight,
    shared_down_weight,
):
    return (
        lax.all_gather(query_weight, "dp", axis=0, tiled=True),
        lax.all_gather(kv_up_weight, "dp", axis=0, tiled=True),
        lax.all_gather(output_weight, "dp", axis=1, tiled=True),
        lax.all_gather(shared_gate_weight, "dp", axis=0, tiled=True),
        lax.all_gather(shared_up_weight, "dp", axis=0, tiled=True),
        lax.all_gather(shared_down_weight, "dp", axis=1, tiled=True),
    )


def to_owner(slot_rows, slot_weight, gate_slab, up_slab, down_slab):
    return (
        lax.all_to_all(slot_rows, "dp", split_axis=0, concat_axis=0, tiled=True),
        lax.all_to_all(slot_weight, "dp", split_axis=0, concat_axis=0, tiled=True),
        lax.all_to_all(gate_slab, "dp", split_axis=0, concat_axis=0, tiled=True),
        lax.all_to_all(up_slab, "dp", split_axis=0, concat_axis=0, tiled=True),
        lax.all_to_all(down_slab, "dp", split_axis=0, concat_axis=0, tiled=True),
    )


def from_owner(slot_rows, slot_values):
    return (
        lax.all_to_all(slot_rows, "dp", split_axis=0, concat_axis=0, tiled=True),
        lax.all_to_all(slot_values, "dp", split_axis=0, concat_axis=0, tiled=True),
    )


def per_device(
    block_in,
    attn_norm_gain,
    query_weight,
    kv_down_weight,
    latent_gain,
    kv_up_weight,
    output_weight,
    ffn_norm_gain,
    router_weight,
    expert_ids,
    shared_gate_weight,
    shared_up_weight,
    shared_down_weight,
    expert_gate_weight,
    expert_up_weight,
    expert_down_weight,
    out_grad,
):
    wide = jnp.float32
    narrow = jnp.bfloat16
    own_rows = block_in.shape[0]
    width = block_in.shape[1]
    group = own_rows * lax.axis_size("tensor")
    nseqs = group // SEQ
    dp_count = lax.axis_size("dp")
    owner_count = dp_count // ACTIVE
    slot_piece = CAP // owner_count
    gain_one, gain_two, gain_lat, kv_down, router = (
        lax.all_gather(attn_norm_gain, ("dp", "tensor"), axis=0, tiled=True),
        lax.all_gather(ffn_norm_gain, ("dp", "tensor"), axis=0, tiled=True),
        lax.all_gather(latent_gain, ("dp", "tensor"), axis=0, tiled=True),
        lax.all_gather(kv_down_weight, ("dp", "tensor"), axis=0, tiled=True),
        lax.all_gather(router_weight, ("dp", "tensor"), axis=0, tiled=True),
    )
    gain_one = gain_one.astype(wide)
    gain_two = gain_two.astype(wide)
    gain_lat = gain_lat.astype(wide)
    dense_all = fetch_dense(
        query_weight,
        kv_up_weight,
        output_weight,
        shared_gate_weight,
        shared_up_weight,
        shared_down_weight,
    )
    query_full, kv_up_full, output_full, shared_gate, shared_up, shared_down = dense_all
    heads = query_full.shape[1] // (NOPE + ROPE)
    residual_in = block_in.astype(wide)
    scale_one = rms_scale(residual_in)
    normed_one = residual_in * scale_one
    hidden_own = (normed_one * gain_one).astype(narrow)
    latent_own = matmul(hidden_own, kv_down).astype(narrow)
    hidden_one, latent_in = (
        lax.all_gather(hidden_own, "tensor", axis=0, tiled=True),
        lax.all_gather(latent_own, "tensor", axis=0, tiled=True),
    )
    compressed = latent_in[:, :LATENT].astype(wide)
    scale_lat = rms_scale(compressed)
    normed_lat = compressed * scale_lat
    latent = (normed_lat * gain_lat).astype(narrow)
    cosine, sine = rope_tables(group)
    key_rope = rotate(latent_in[:, LATENT:].astype(wide), cosine, sine).astype(narrow)
    query = matmul(hidden_one, query_full).reshape(group, heads, NOPE + ROPE)
    query_nope = query[..., :NOPE].astype(narrow)
    query_rope = rotate(query[..., NOPE:], cosine[:, None, :], sine[:, None, :]).astype(narrow)
    keyvalue = matmul(latent, kv_up_full).astype(narrow).reshape(group, heads, NOPE + VDIM)
    key_nope = keyvalue[..., :NOPE]
    values = keyvalue[..., NOPE:]

    def by_seq(array):
        return array.reshape((nseqs, SEQ) + array.shape[1:])

    def to_pieces(slots):
        return slots.reshape((dp_count, slot_piece) + slots.shape[2:])

    mixed, logsum = lax.map(
        attend_forward,
        (
            by_seq(query_nope),
            by_seq(query_rope),
            by_seq(key_nope),
            by_seq(key_rope),
            by_seq(values),
        ),
    )
    mixed = mixed.reshape(group, heads * VDIM)
    attn_share = matmul(mixed, output_full)
    attn_own = lax.psum_scatter(attn_share, "tensor", scatter_dimension=0, tiled=True)
    after_attn = residual_in + attn_own
    scale_two = rms_scale(after_attn)
    normed_two = after_attn * scale_two
    hidden_two_own = (normed_two * gain_two).astype(narrow)
    hidden_two, grad_all = (
        lax.all_gather(hidden_two_own, "tensor", axis=0, tiled=True),
        lax.all_gather(out_grad, "tensor", axis=0, tiled=True),
    )
    route_prob = jax.nn.softmax(matmul(hidden_two, router), axis=-1)
    chosen = jnp.any(
        expert_ids[:, :, None] == jnp.arange(ACTIVE, dtype=jnp.int32)[None, None, :], axis=1
    )
    gate = jnp.where(chosen, route_prob[:, :ACTIVE], 0.0)
    ranks = jnp.cumsum(chosen.astype(jnp.int32), axis=0) - 1
    slot_of = jnp.arange(ACTIVE, dtype=jnp.int32)[None, :] * CAP + ranks
    slot_of = jnp.where(chosen, slot_of, ACTIVE * CAP).reshape(-1)
    row_of = jnp.broadcast_to(jnp.arange(group, dtype=jnp.int32)[:, None], (group, ACTIVE)).reshape(
        -1
    )
    source = jnp.zeros((ACTIVE * CAP,), jnp.int32).at[slot_of].set(row_of, mode="drop")
    filled = jnp.zeros((ACTIVE * CAP,), wide).at[slot_of].set(1.0, mode="drop")
    expert_of = jnp.arange(ACTIVE * CAP, dtype=jnp.int32) // CAP
    weight = (gate[source, expert_of] * filled).reshape(ACTIVE, CAP)
    tokens_in = hidden_two[source].reshape(ACTIVE, CAP, width)
    shared_a = matmul(hidden_two, shared_gate)
    shared_b = matmul(hidden_two, shared_up)
    shared_hidden = (jax.nn.silu(shared_a) * shared_b).astype(narrow)
    gate_slab = jnp.repeat(expert_gate_weight, owner_count, axis=0).astype(wide)
    up_slab = jnp.repeat(expert_up_weight, owner_count, axis=0).astype(wide)
    down_slab = jnp.repeat(expert_down_weight, owner_count, axis=0).astype(wide)
    arrived = to_owner(
        to_pieces(tokens_in.astype(wide)), to_pieces(weight), gate_slab, up_slab, down_slab
    )
    rows_here = arrived[0].reshape(-1, width).astype(narrow)
    weight_here = arrived[1].reshape(-1)
    gate_here = arrived[2].astype(narrow).reshape(width, -1)
    up_here = arrived[3].astype(narrow).reshape(width, -1)
    down_here = arrived[4].astype(narrow)
    owned_a = matmul(rows_here, gate_here)
    owned_b = matmul(rows_here, up_here)
    owned_hidden = (jax.nn.silu(owned_a) * owned_b).astype(narrow)
    owned_out = (
        einsum32("rf,sfd->rsd", owned_hidden, down_here).reshape(-1, width) * weight_here[:, None]
    )
    returned = from_owner(
        owned_out.reshape(dp_count, slot_piece, width), jnp.zeros((dp_count, slot_piece), wide)
    )
    routed_flat = returned[0].reshape(-1, width)
    moe_share = matmul(shared_hidden, shared_down).at[source].add(routed_flat)
    moe_own = lax.psum_scatter(
        moe_share.astype(jnp.bfloat16), "tensor", scatter_dimension=0, tiled=True
    ).astype(jnp.float32)
    block_out = (after_attn + moe_own).astype(narrow)
    dense_all = fetch_dense(
        query_weight,
        kv_up_weight,
        output_weight,
        shared_gate_weight,
        shared_up_weight,
        shared_down_weight,
    )
    query_full, kv_up_full, output_full, shared_gate, shared_up, shared_down = dense_all
    shared_up_grad = right_dot(grad_all, shared_down)
    shared_a_grad = (shared_up_grad * shared_b * silu_grad(shared_a)).astype(narrow)
    shared_b_grad = (shared_up_grad * jax.nn.silu(shared_a)).astype(narrow)
    shared_down_grad = left_dot(shared_hidden, grad_all)
    shared_gate_grad = left_dot(hidden_two, shared_a_grad)
    shared_up_wgrad = left_dot(hidden_two, shared_b_grad)
    hidden_two_share = right_dot(shared_a_grad, shared_gate) + right_dot(shared_b_grad, shared_up)
    grad_in = grad_all[source].reshape(ACTIVE, CAP, width)
    arrived = to_owner(
        to_pieces(grad_in.astype(wide)), to_pieces(weight), gate_slab, up_slab, down_slab
    )
    grad_here = arrived[0].reshape(-1, width).astype(narrow)
    weight_here = arrived[1].reshape(-1)
    gate_here = arrived[2].astype(narrow).reshape(width, -1)
    up_here = arrived[3].astype(narrow).reshape(width, -1)
    down_here = arrived[4].astype(narrow)
    grad_split = grad_here.reshape(grad_here.shape[0], dp_count, -1)
    owned_up_grad = einsum32("rsd,sfd->rf", grad_split, down_here)
    owned_slot = jnp.sum(owned_up_grad * owned_hidden.astype(wide), axis=-1)
    owned_hidden_grad = weight_here[:, None] * owned_up_grad
    owned_a_grad = (owned_hidden_grad * owned_b * silu_grad(owned_a)).astype(narrow)
    owned_b_grad = (owned_hidden_grad * jax.nn.silu(owned_a)).astype(narrow)
    owned_scaled = (weight_here[:, None] * owned_hidden.astype(wide)).astype(narrow)
    down_term = einsum32("rf,rsd->sfd", owned_scaled, grad_split)
    gate_term = left_dot(rows_here, owned_a_grad).reshape(dp_count, -1, owned_a_grad.shape[1])
    up_term = left_dot(rows_here, owned_b_grad).reshape(dp_count, -1, owned_b_grad.shape[1])
    owned_back = right_dot(owned_a_grad, gate_here) + right_dot(owned_b_grad, up_here)
    returned = from_owner(
        owned_back.reshape(dp_count, slot_piece, width), owned_slot.reshape(dp_count, slot_piece)
    )
    back_flat = returned[0].reshape(-1, width)
    per_slot = returned[1].reshape(-1) * filled
    summed = (
        lax.all_to_all(
            gate_term.astype(jnp.bfloat16), "dp", split_axis=0, concat_axis=0, tiled=True
        ).astype(gate_term.dtype),
        lax.all_to_all(
            up_term.astype(jnp.bfloat16), "dp", split_axis=0, concat_axis=0, tiled=True
        ).astype(up_term.dtype),
        lax.all_to_all(
            down_term.astype(jnp.bfloat16), "dp", split_axis=0, concat_axis=0, tiled=True
        ).astype(down_term.dtype),
    )
    expert_gate_grad = jnp.sum(
        summed[0].reshape((ACTIVE, owner_count) + summed[0].shape[1:]), axis=1
    )
    expert_up_wgrad = jnp.sum(
        summed[1].reshape((ACTIVE, owner_count) + summed[1].shape[1:]), axis=1
    )
    expert_down_grad = jnp.sum(
        summed[2].reshape((ACTIVE, owner_count) + summed[2].shape[1:]), axis=1
    )
    gate_share = jnp.zeros((group, ACTIVE), wide).at[source, expert_of].add(per_slot)
    hidden_two_share = hidden_two_share.at[source].add(back_flat)
    hidden_two_grad, gate_grad = (
        lax.psum_scatter(
            hidden_two_share.astype(jnp.bfloat16), "tensor", scatter_dimension=0, tiled=True
        ).astype(jnp.float32),
        lax.psum_scatter(
            gate_share.astype(jnp.bfloat16), "tensor", scatter_dimension=0, tiled=True
        ).astype(jnp.float32),
    )
    prob_own = jax.nn.softmax(matmul(hidden_two_own, router), axis=-1)
    prob_grad = jnp.concatenate(
        [gate_grad, jnp.zeros((own_rows, prob_own.shape[1] - ACTIVE), wide)], axis=-1
    )
    logit_grad = (
        prob_own * (prob_grad - jnp.sum(prob_own * prob_grad, axis=-1, keepdims=True))
    ).astype(narrow)
    router_grad = left_dot(hidden_two_own, logit_grad)
    hidden_two_grad = hidden_two_grad + right_dot(logit_grad, router)
    gain_two_grad = jnp.sum(hidden_two_grad * normed_two, axis=0)
    after_attn_grad = out_grad.astype(wide) + norm_back(
        hidden_two_grad * gain_two, normed_two, scale_two
    )
    residual_low = lax.all_gather(after_attn_grad.astype(narrow), "tensor", axis=0, tiled=True)
    output_grad = left_dot(mixed, residual_low)
    mixed_grad = right_dot(residual_low, output_full).astype(narrow).reshape(group, heads, VDIM)
    grads = lax.map(
        attend_backward,
        (
            by_seq(query_nope),
            by_seq(query_rope),
            by_seq(key_nope),
            by_seq(key_rope),
            by_seq(values),
            by_seq(mixed.reshape(group, heads, VDIM)),
            by_seq(mixed_grad),
            logsum,
        ),
    )
    query_nope_grad, query_rope_grad, key_nope_grad, key_rope_grad, values_grad = [
        part.reshape((group,) + part.shape[2:]) for part in grads
    ]
    query_rope_back = unrotate(query_rope_grad, cosine[:, None, :], sine[:, None, :])
    query_grad = (
        jnp.concatenate([query_nope_grad, query_rope_back], axis=-1)
        .astype(narrow)
        .reshape(group, heads * (NOPE + ROPE))
    )
    keyvalue_grad = (
        jnp.concatenate([key_nope_grad, values_grad], axis=-1)
        .astype(narrow)
        .reshape(group, heads * (NOPE + VDIM))
    )
    kv_up_grad = left_dot(latent, keyvalue_grad)
    latent_grad = right_dot(keyvalue_grad, kv_up_full)
    gain_lat_grad = jnp.sum(latent_grad * normed_lat, axis=0)
    compressed_grad = norm_back(latent_grad * gain_lat, normed_lat, scale_lat)
    key_rope_back = unrotate(key_rope_grad, cosine, sine)
    latent_in_share = jnp.concatenate([compressed_grad, key_rope_back], axis=-1)
    query_wgrad = left_dot(hidden_one, query_grad)
    hidden_one_share = right_dot(query_grad, query_full)
    dense_grads = (
        lax.psum_scatter(
            query_wgrad.astype(jnp.bfloat16), "dp", scatter_dimension=0, tiled=True
        ).astype(jnp.float32),
        lax.psum_scatter(
            kv_up_grad.astype(jnp.bfloat16), "dp", scatter_dimension=0, tiled=True
        ).astype(jnp.float32),
        lax.psum_scatter(
            output_grad.astype(jnp.bfloat16), "dp", scatter_dimension=1, tiled=True
        ).astype(jnp.float32),
        lax.psum_scatter(
            shared_gate_grad.astype(jnp.bfloat16), "dp", scatter_dimension=0, tiled=True
        ).astype(jnp.float32),
        lax.psum_scatter(
            shared_up_wgrad.astype(jnp.bfloat16), "dp", scatter_dimension=0, tiled=True
        ).astype(jnp.float32),
        lax.psum_scatter(
            shared_down_grad.astype(jnp.bfloat16), "dp", scatter_dimension=1, tiled=True
        ).astype(jnp.float32),
    )
    hidden_one_grad, latent_in_grad = (
        lax.psum_scatter(
            hidden_one_share.astype(jnp.bfloat16), "tensor", scatter_dimension=0, tiled=True
        ).astype(jnp.float32),
        lax.psum_scatter(
            latent_in_share.astype(jnp.bfloat16), "tensor", scatter_dimension=0, tiled=True
        ).astype(jnp.float32),
    )
    latent_in_low = latent_in_grad.astype(narrow)
    kv_down_grad = left_dot(hidden_own, latent_in_low)
    hidden_one_grad = hidden_one_grad + right_dot(latent_in_low, kv_down)
    gain_one_grad = jnp.sum(hidden_one_grad * normed_one, axis=0)
    input_grad = after_attn_grad + norm_back(hidden_one_grad * gain_one, normed_one, scale_one)
    small_grads = (
        lax.psum_scatter(gain_one_grad, ("dp", "tensor"), scatter_dimension=0, tiled=True),
        lax.psum_scatter(gain_two_grad, ("dp", "tensor"), scatter_dimension=0, tiled=True),
        lax.psum_scatter(gain_lat_grad, ("dp", "tensor"), scatter_dimension=0, tiled=True),
        lax.psum_scatter(kv_down_grad, ("dp", "tensor"), scatter_dimension=0, tiled=True),
        lax.psum_scatter(router_grad, ("dp", "tensor"), scatter_dimension=0, tiled=True),
    )
    return (
        block_out,
        input_grad,
        small_grads[0],
        dense_grads[0],
        small_grads[3],
        small_grads[2],
        dense_grads[1],
        dense_grads[2],
        small_grads[1],
        small_grads[4],
        dense_grads[3],
        dense_grads[4],
        dense_grads[5],
        expert_gate_grad,
        expert_up_wgrad,
        expert_down_grad,
    )


def solution(mesh):
    in_specs = (
        P(("dp", "tensor"), None),
        P(("dp", "tensor")),
        P("dp", "tensor"),
        P(("dp", "tensor"), None),
        P(("dp", "tensor")),
        P("dp", "tensor"),
        P("tensor", "dp"),
        P(("dp", "tensor")),
        P(("dp", "tensor"), None),
        P("dp", None),
        P("dp", "tensor"),
        P("dp", "tensor"),
        P("tensor", "dp"),
        P(None, "dp", "tensor"),
        P(None, "dp", "tensor"),
        P(None, "tensor", "dp"),
        P(("dp", "tensor"), None),
    )
    out_specs = (
        P(("dp", "tensor"), None),
        P(("dp", "tensor"), None),
        P(("dp", "tensor")),
        P("dp", "tensor"),
        P(("dp", "tensor"), None),
        P(("dp", "tensor")),
        P("dp", "tensor"),
        P("tensor", "dp"),
        P(("dp", "tensor")),
        P(("dp", "tensor"), None),
        P("dp", "tensor"),
        P("dp", "tensor"),
        P("tensor", "dp"),
        P(None, "dp", "tensor"),
        P(None, "dp", "tensor"),
        P(None, "tensor", "dp"),
    )
    return jax.shard_map(
        per_device, mesh=mesh, in_specs=in_specs, out_specs=out_specs, check_vma=False
    )
```

profile of v0, /device:TPU:0, one launch (start us, length us, event | category | flops | bytes accessed | tf_op | source)
XLA Modules:
  0.0 1490.6 jit_solution(15080583595471268522)
XLA Ops:
  11.3 42.3 %all-reduce.8 = (bf16[512]{0:T(512)(128)(2,1)S(1)}, bf16[2048]{0:T(1024)(128)(2,1)S(1)}, bf16[2048]{0:T(1024)(128)(2,1)S(1)}) all-reduce(bf16[512]{0:T(512)(128)(2,1)S(1)} %dynamic-update-slice.1, bf16[2048]{0:T(1024)(128)(2,1)S(1)} %dynamic-update-slice, ...), channel_id=1, replica_groups=mesh['dp'=8,'tensor'=4] {'dp','tensor'}, use_global_device_ids=true, to_apply=%add.2 | all-reduce | flops 4608 | bytes 18432
  74.5 15.9 %all_gather.56 = bf16[512,576]{0,1:T(8,128)(2,1)S(1)} all-gather(bf16[128,576]{0,1:T(8,128)(2,1)S(1)} %convolution_convert_fusion.15), channel_id=1, replica_groups=mesh['dp'=8,'tensor'=4] {'tensor'}, dimensions={0}, use_global_device_ids=true | all-gather | bytes 737280 | tf_op jit(solution)/shard_map/all_gather | solution.py:200
  99.5 43.9 %all-gather.16.cloned.1.call-done = bf16[512,2048]{1,0:T(8,128)(2,1)} async-done(((bf16[128,2048]{1,0:T(8,128)(2,1)}), bf16[512,2048]{1,0:T(8,128)(2,1)}) %all-gather.16.cloned.1.call-update) | async-done | bytes 2097168 | tf_op jit(solution)/shard_map/all_gather | solution.py:199
  143.4 32.8 %all-gather.18.cloned.1.call-done = bf16[2048,768]{1,0:T(8,128)(2,1)} async-done(((bf16[256,768]{1,0:T(8,128)(2,1)}), bf16[2048,768]{1,0:T(8,128)(2,1)}) %all-gather.18.cloned.1.call-update) | async-done | bytes 3145744 | tf_op jit(solution)/shard_map/all_gather | solution.py:119
  185.8 20.2 %all-gather.20.cloned.1.call-done = bf16[512,2048]{1,0:T(8,128)(2,1)} async-done(((bf16[512,256]{1,0:T(8,128)(2,1)}), bf16[512,2048]{1,0:T(8,128)(2,1)}) %all-gather.20.cloned.1.call-update) | async-done | bytes 2097168 | tf_op jit(solution)/shard_map/all_gather | solution.py:121
  211.9 75.9 %reduce-scatter.19.cloned.1.call-done = f32[128,2048]{1,0:T(8,128)} async-done(((f32[512,2048]{1,0:T(8,128)}), f32[128,2048]{1,0:T(8,128)}) %reduce-scatter.19.cloned.1.call-update) | async-done | bytes 1048592 | tf_op jit(solution)/shard_map/reduce_scatter | solution.py:233
  296.2 18.1 %all-to-all-done.1 = bf16[8,256,352]{1,2,0:T(8,128)(2,1)S(1)} async-done(((bf16[8,256,352]{1,2,0:T(8,128)(2,1)}), bf16[8,256,352]{1,2,0:T(8,128)(2,1)S(1)}, u32[]{:S(2)}, u32[]{:S(2)}) %all-to-all-start.1) | async-done | bytes 1441824 | tf_op jit(solution)/shard_map/all_to_all | solution.py:132
  365.3 73.4 %all_gather.67 = bf16[2048,64]{1,0:T(8,128)(2,1)S(1)} all-gather(bf16[64,64]{1,0:T(8,128)(2,1)S(1)} %copy-done.50), channel_id=1, replica_groups=mesh['dp'=8,'tensor'=4] {'dp','tensor'}, dimensions={0}, use_global_device_ids=true | all-gather | bytes 270336 | tf_op jit(solution)/shard_map/all_gather | solution.py:178
  454.7 42.2 %all_to_all.72 = bf16[8,96,2048]{2,1,0:T(8,128)(2,1)} all-to-all(bf16[8,96,2048]{2,1,0:T(8,128)(2,1)} %bitcast.160), channel_id=1, replica_groups=mesh['dp'=8,'tensor'=4] {'dp'}, dimensions={0} | all-to-all | bytes 6291456 | tf_op jit(solution)/shard_map/all_to_all | solution.py:130
  569.6 36.2 %scatter_fusion.2 = f32[512,8]{0,1:T(8,128)S(1)} fusion(f32[512,8]{0,1:T(8,128)S(1)} %broadcast_in_dim.84, s32[768]{0:T(1024)S(1)} %get-tuple-element.88, f32[768]{0:T(1024)S(1)} %mul.498), kind=kCustom, calls=%fused_computation.7 | custom fusion | flops 768 | bytes 15360 | tf_op jit(solution)/shard_map/scatter-add | solution.py:348
  619.5 18.8 %scatter_fusion.1 = f32[512,2048]{1,0:T(8,128)} fusion(f32[512,2048]{1,0:T(8,128)} %convolution_add_fusion.1, s32[768]{0:T(1024)S(1)} %compare_select_fusion.2, f32[768,2048]{1,0:T(8,128)} %bitcast.20), kind=kCustom, calls=%fused_computation.6 | custom fusion | flops 1572864 | bytes 18877440 | tf_op jit(solution)/shard_map/scatter-add | solution.py:349
  644.7 37.6 %reduce-scatter.23.cloned.1.call-done = bf16[128,2048]{1,0:T(8,128)(2,1)} async-done(((bf16[512,2048]{1,0:T(8,128)(2,1)}), bf16[128,2048]{1,0:T(8,128)(2,1)}) %reduce-scatter.23.cloned.1.call-update) | async-done | bytes 524304 | tf_op jit(solution)/shard_map/reduce_scatter | solution.py:351
  686.8 44.6 %all-gather.32.cloned.1.call-done = bf16[512,2048]{1,0:T(8,128)(2,1)} async-done(((bf16[128,2048]{1,0:T(8,128)(2,1)}), bf16[512,2048]{1,0:T(8,128)(2,1)}) %all-gather.32.cloned.1.call-update) | async-done | bytes 2097168 | tf_op jit(solution)/shard_map/all_gather | solution.py:371
  807.9 65.1 %all-to-all-done.5 = f32[8,96,2048]{2,1,0:T(8,128)} async-done(((f32[8,96,2048]{2,1,0:T(8,128)}), f32[8,96,2048]{2,1,0:T(8,128)}, u32[]{:S(2)}, u32[]{:S(2)}) %all-to-all-start.5) | async-done | bytes 6291488 | tf_op jit(solution)/shard_map/all_to_all | solution.py:140
  873.0 18.8 %scatter_fusion = f32[512,2048]{1,0:T(8,128)} fusion(f32[512,2048]{1,0:T(8,128)} %fusion.112, s32[768]{0:T(1024)S(1)} %compare_select_fusion.2, f32[768,2048]{1,0:T(8,128)} %bitcast.16), kind=kCustom, calls=%fused_computation.5 | custom fusion | flops 1572864 | bytes 18877440 | tf_op jit(solution)/shard_map/scatter-add | solution.py:282
  925.9 15.9 %all-to-all-done.11 = bf16[8,352,256]{2,1,0:T(8,128)(2,1)S(1)} async-done(((bf16[8,352,256]{2,1,0:T(8,128)(2,1)}), bf16[8,352,256]{2,1,0:T(8,128)(2,1)S(1)}, u32[]{:S(2)}, u32[]{:S(2)}) %all-to-all-start.11) | async-done | bytes 1441824 | tf_op jit(solution)/shard_map/all_to_all | solution.py:335
  950.4 17.6 %all-to-all-done.10 = bf16[8,256,352]{1,2,0:T(8,128)(2,1)} async-done(((bf16[8,256,352]{1,2,0:T(8,128)(2,1)}), bf16[8,256,352]{1,2,0:T(8,128)(2,1)}, u32[]{:S(2)}, u32[]{:S(2)}) %all-to-all-start.10) | async-done | bytes 1441824 | tf_op jit(solution)/shard_map/all_to_all | solution.py:332
  977.4 17.3 %all-to-all-done.9 = bf16[8,256,352]{1,2,0:T(8,128)(2,1)} async-done(((bf16[8,256,352]{1,2,0:T(8,128)(2,1)}), bf16[8,256,352]{1,2,0:T(8,128)(2,1)}, u32[]{:S(2)}, u32[]{:S(2)}) %all-to-all-start.9) | async-done | bytes 1441824 | tf_op jit(solution)/shard_map/all_to_all | solution.py:329
  1005.5 42.7 %reduce-scatter.33.cloned.1.call-done = bf16[512,256]{1,0:T(8,128)(2,1)} async-done(((bf16[512,2048]{1,0:T(8,128)(2,1)}), bf16[512,256]{1,0:T(8,128)(2,1)}) %reduce-scatter.33.cloned.1.call-update) | async-done | bytes 262160 | tf_op jit(solution)/shard_map/reduce_scatter | solution.py:416
  1049.9 44.2 %reduce-scatter.25.cloned.1.call-done = bf16[128,2048]{1,0:T(8,128)(2,1)} async-done(((bf16[512,2048]{1,0:T(8,128)(2,1)}), bf16[128,2048]{1,0:T(8,128)(2,1)}) %reduce-scatter.25.cloned.1.call-update) | async-done | bytes 524304 | tf_op jit(solution)/shard_map/reduce_scatter | solution.py:430
  1097.9 42.8 %all-reduce.7 = (f32[2048]{0:T(1024)S(1)}, f32[512]{0:T(512)S(1)}, f32[2048]{0:T(1024)S(1)}) all-reduce(f32[2048]{0:T(1024)S(1)} %get-tuple-element.72, f32[512]{0:T(512)S(1)} %get-tuple-element.70, f32[2048]{0:T(1024)S(1)} %get-tuple-element.68), channel_id=8, replica_groups=mesh['dp'=8,'tensor'=4] {'dp','tensor'}, use_global_device_ids=true, to_apply=%region_29.30.clone | all-reduce | flops 4608 | bytes 36864
  1145.5 43.5 %reduce-scatter.27.cloned.1.call-done = bf16[256,768]{1,0:T(8,128)(2,1)} async-done(((bf16[2048,768]{1,0:T(8,128)(2,1)}), bf16[256,768]{1,0:T(8,128)(2,1)}) %reduce-scatter.27.cloned.1.call-update) | async-done | bytes 393232 | tf_op jit(solution)/shard_map/reduce_scatter | solution.py:410
  1190.9 137.9 %reduce-scatter.35.cloned.1.call-done = f32[64,64]{1,0:T(8,128)} async-done(((f32[2048,64]{1,0:T(8,128)}), f32[64,64]{1,0:T(8,128)}) %reduce-scatter.35.cloned.1.call-update) | async-done | bytes 16400 | tf_op jit(solution)/shard_map/reduce_scatter | solution.py:447
  1328.8 154.9 %reduce-scatter.29.cloned.1.call-done = f32[64,576]{1,0:T(8,128)} async-done(((f32[2048,576]{1,0:T(8,128)}), f32[64,576]{1,0:T(8,128)}) %reduce-scatter.29.cloned.1.call-update) | async-done | bytes 147472 | tf_op jit(solution)/shard_map/reduce_scatter | solution.py:446
  (341 shorter events, 372.6 us)
Async XLA Ops:
  7.9 87.6 %all-gather.14.cloned.1.call-start = ((), (), s32[]{:S(2)}) async-start(), calls=%async_computation.27 | async-start | bytes 1179648 | tf_op jit(solution)/shard_map/all_gather | solution.py:120
  8.7 134.7 %all-gather.16.cloned.1.call-start = ((), (), s32[]{:S(2)}) async-start(), calls=%async_computation.28 | async-start | bytes 2621440 | tf_op jit(solution)/shard_map/all_gather | solution.py:199
  57.4 118.7 %all-gather.18.cloned.1.call-start = ((), (), s32[]{:S(2)}) async-start(), calls=%async_computation.29 | async-start | bytes 3538944 | tf_op jit(solution)/shard_map/all_gather | solution.py:119
  58.0 148.0 %all-gather.20.cloned.1.call-start = ((), (), s32[]{:S(2)}) async-start(), calls=%async_computation.30 | async-start | bytes 2359296 | tf_op jit(solution)/shard_map/all_gather | solution.py:121
  58.6 229.2 %reduce-scatter.19.cloned.1.call-start = ((), (), s32[]{:S(2)}) async-start(), calls=%async_computation.31 | async-start | bytes 5242880 | tf_op jit(solution)/shard_map/reduce_scatter | solution.py:233
  210.9 124.8 %all-gather.30.cloned.1.call-start = ((), (), s32[]{:S(2)}) async-start(), calls=%async_computation.37 | async-start | bytes 2621440 | tf_op jit(solution)/shard_map/all_gather | solution.py:240
  211.6 227.1 %all-gather.22.cloned.1.call-start = ((), (), s32[]{:S(2)}) async-start(), calls=%async_computation.32 | async-start | bytes 2621440 | tf_op jit(solution)/shard_map/all_gather | solution.py:239
  290.3 257.9 %all-gather.26.cloned.1.call-start = ((), (), s32[]{:S(2)}) async-start(), calls=%async_computation.34 | async-start | bytes 3244032 | tf_op jit(solution)/shard_map/all_gather | solution.py:123
  344.6 102.2 %all-to-all-start.6 = ((bf16[8,96,2048]{2,1,0:T(8,128)(2,1)}), bf16[8,96,2048]{2,1,0:T(8,128)(2,1)}, u32[]{:S(2)}, u32[]{:S(2)}) async-start(bf16[8,96,2048]{2,1,0:T(8,128)(2,1)} %bitcast.159), calls=%async_computation.8 | async-start | bytes 6291456 | tf_op jit(solution)/shard_map/all_to_all | solution.py:130
  349.1 203.7 %all-gather.24.cloned.1.call-start = ((), (), s32[]{:S(2)}) async-start(), calls=%async_computation.33 | async-start | bytes 3244032 | tf_op jit(solution)/shard_map/all_gather | solution.py:122
  547.9 95.9 %reduce-scatter.43.cloned.1.call-start = ((), (), s32[]{:S(2)}) async-start(), calls=%async_computation.49 | async-start | bytes 163840
  642.1 89.2 %all-gather.32.cloned.1.call-start = ((), (), s32[]{:S(2)}) async-start(), calls=%async_computation.39 | async-start | bytes 2621440 | tf_op jit(solution)/shard_map/all_gather | solution.py:371
  686.3 217.3 %reduce-scatter.45.cloned.1.call-start = ((), (), s32[]{:S(2)}) async-start(), calls=%async_computation.50 | async-start | bytes 819200
  743.9 254.0 %reduce-scatter.41.cloned.1.call-start = ((), (), s32[]{:S(2)}) async-start(), calls=%async_computation.48 | async-start | bytes 3244032 | tf_op jit(solution)/shard_map/reduce_scatter | solution.py:425
  749.1 250.9 %reduce-scatter.39.cloned.1.call-start = ((), (), s32[]{:S(2)}) async-start(), calls=%async_computation.47 | async-start | bytes 3244032 | tf_op jit(solution)/shard_map/reduce_scatter | solution.py:422
  753.5 248.4 %reduce-scatter.37.cloned.1.call-start = ((), (), s32[]{:S(2)}) async-start(), calls=%async_computation.46 | async-start | bytes 3244032 | tf_op jit(solution)/shard_map/reduce_scatter | solution.py:419
  757.9 245.9 %reduce-scatter.31.cloned.1.call-start = ((), (), s32[]{:S(2)}) async-start(), calls=%async_computation.43 | async-start | bytes 1179648 | tf_op jit(solution)/shard_map/reduce_scatter | solution.py:413
  762.0 286.1 %reduce-scatter.33.cloned.1.call-start = ((), (), s32[]{:S(2)}) async-start(), calls=%async_computation.44 | async-start | bytes 2359296 | tf_op jit(solution)/shard_map/reduce_scatter | solution.py:416
  790.1 83.0 %all-to-all-start.5 = ((f32[8,96,2048]{2,1,0:T(8,128)}), f32[8,96,2048]{2,1,0:T(8,128)}, u32[]{:S(2)}, u32[]{:S(2)}) async-start(f32[8,96,2048]{2,1,0:T(8,128)} %broadcast_multiply_fusion), calls=%async_computation.6 | async-start | bytes 12582912 | tf_op jit(solution)/shard_map/all_to_all | solution.py:140
  795.0 299.1 %reduce-scatter.25.cloned.1.call-start = ((), (), s32[]{:S(2)}) async-start(), calls=%async_computation.40 | async-start | bytes 2621440 | tf_op jit(solution)/shard_map/reduce_scatter | solution.py:430
  801.2 341.2 %reduce-scatter.21.cloned.1.call-start = ((), (), s32[]{:S(2)}) async-start(), calls=%async_computation.36 | async-start | bytes 2621440 | tf_op jit(solution)/shard_map/reduce_scatter | solution.py:283
  895.7 293.3 %reduce-scatter.27.cloned.1.call-start = ((), (), s32[]{:S(2)}) async-start(), calls=%async_computation.41 | async-start | bytes 3538944 | tf_op jit(solution)/shard_map/reduce_scatter | solution.py:410
  900.9 427.9 %reduce-scatter.35.cloned.1.call-start = ((), (), s32[]{:S(2)}) async-start(), calls=%async_computation.45 | async-start | bytes 1081344 | tf_op jit(solution)/shard_map/reduce_scatter | solution.py:447
  903.4 580.3 %reduce-scatter.29.cloned.1.call-start = ((), (), s32[]{:S(2)}) async-start(), calls=%async_computation.42 | async-start | bytes 5406720 | tf_op jit(solution)/shard_map/reduce_scatter | solution.py:446
  (70 other events, 1810.3 us)
Sparse Core Ops, SparseCore 0:
  10.8 60.5 all-gather.11
  73.3 22.1 all-gather.13
  97.7 45.6 all-gather.15
  145.1 30.9 all-gather.17
  177.9 28.0 all-gather.19
  211.0 76.7 reduce-scatter.18
  289.4 46.1 all-gather.29
  337.2 46.5 all-gather.21
  385.6 30.8 all-gather.25
  418.3 31.7 all-gather.23
  503.9 34.3 all-gather.27
  642.3 40.0 reduce-scatter.22
  686.5 44.8 all-gather.31
  744.1 21.3 reduce-scatter.44
  768.7 73.2 reduce-scatter.40
  845.2 45.8 reduce-scatter.38
  894.4 60.7 reduce-scatter.36
  958.3 45.4 reduce-scatter.30
  1007.0 41.1 reduce-scatter.32
  1050.4 43.5 reduce-scatter.24
  1096.3 43.9 reduce-scatter.20
  1143.7 45.2 reduce-scatter.26
  1191.7 137.0 reduce-scatter.34
  1331.7 151.9 reduce-scatter.28
  (1 shorter events, 18.1 us)
where the time goes:
time: 1500 us; the launch traced here: 1490 us
  waiting for transfers between devices  845 us (56%)
  blocking collectives  217 us (14%)
  matrix products  141 us (9%)
  other arithmetic  123 us (8%)
  local copies, waits for them, and re-layouts  101 us (7%)
  starting transfers between devices  48.2 us (3%)
  between operations  15.5 us (1%)
    reduce_scatter x1, waiting for transfers between devices, per_device(): lax.psum_scatter(kv_down_grad, ('dp', 'tensor'), scatter_dimension=0, til...  155 us
    reduce_scatter x1, waiting for transfers between devices, per_device(): lax.psum_scatter(router_grad, ('dp', 'tensor'), scatter_dimension=0, tile...  138 us
    unnamed x2, blocking collectives  85.1 us
    reduce_scatter x1, waiting for transfers between devices, per_device(): lax.psum_scatter(attn_share, 'tensor', scatter_dimension=0, tiled=True)  75.9 us
    all_gather x1, blocking collectives, per_device(): lax.all_gather(router_weight, ('dp', 'tensor'), axis=0, tiled=True)  73.4 us
    all_to_all x2, waiting for transfers between devices, from_owner(): lax.all_to_all(slot_rows, 'dp', split_axis=0, concat_axis=0, tiled=True)  70.7 us
    all_gather x1, waiting for transfers between devices, per_device(): lax.all_gather(after_attn_grad.astype(narrow), 'tensor', axis=0, tiled=True)  44.6 us
    reduce_scatter x1, waiting for transfers between devices, per_device(): lax.psum_scatter(hidden_one_share.astype(jnp.bfloat16), 'tensor', scatter...  44.2 us
  transfers between devices with their start and end apart: 36, of which 23 were waited for; matrix products, arithmetic and copies ran while one was open for 22% of the time, Pallas kernels for 0%

commit v1 on v0

v1 whole, which is shorter than its diff:
```python
import jax
import jax.numpy as jnp
from jax import lax
from jax.sharding import PartitionSpec as P

NOPE = 128
ROPE = 64
VDIM = 128
LATENT = 512
ACTIVE = 8
SEQ = 512
CAP = 96


EPSILON = 1e-06
NEGATIVE = -1e30


def matmul(left, right):
    return jnp.dot(left, right, preferred_element_type=jnp.float32)


def left_dot(left, right):
    return lax.dot_general(
        left, right, (((0,), (0,)), ((), ())), preferred_element_type=jnp.float32
    )


def right_dot(left, right):
    return lax.dot_general(
        left, right, (((left.ndim - 1,), (1,)), ((), ())), preferred_element_type=jnp.float32
    )


def einsum32(form, left, right):
    return jnp.einsum(form, left, right, preferred_element_type=jnp.float32)


def rms_scale(values):
    return lax.rsqrt(jnp.mean(values * values, axis=-1, keepdims=True) + EPSILON)


def norm_back(grad_normed, normed, scale):
    return scale * (grad_normed - normed * jnp.mean(grad_normed * normed, axis=-1, keepdims=True))


def silu_grad(values):
    sigma = jax.nn.sigmoid(values)
    return sigma * (1.0 + values * (1.0 - sigma))


def rope_tables(position):
    halfway = ROPE // 2
    inverse = jnp.exp(-jnp.log(10000.0) * jnp.arange(halfway).astype(jnp.float32) / halfway)
    angles = position[:, None] * inverse[None, :]
    return (jnp.cos(angles), jnp.sin(angles))


def rotate(values, cosine, sine):
    halfway = ROPE // 2
    first, second = (values[..., :halfway], values[..., halfway:])
    return jnp.concatenate(
        [first * cosine - second * sine, first * sine + second * cosine], axis=-1
    )


def unrotate(grads, cosine, sine):
    halfway = ROPE // 2
    first, second = (grads[..., :halfway], grads[..., halfway:])
    return jnp.concatenate(
        [first * cosine + second * sine, second * cosine - first * sine], axis=-1
    )


def send_tensor(values, step):
    count = lax.axis_size("tensor")
    return lax.ppermute(values, "tensor", [(i, (i + step) % count) for i in range(count)])


def halves(values):
    middle = values.shape[0] // 2
    return [values[:middle], values[middle:]]


def gather_tensor(own):
    pieces = halves(own)
    found = [list(pieces)]
    for _ in range(lax.axis_size("tensor") - 1):
        pieces = [send_tensor(piece, -1) for piece in pieces]
        found.append(list(pieces))
    return jnp.concatenate([piece for row in found for piece in row], axis=0)


def scatter_tensor(share):
    count = lax.axis_size("tensor")
    blocks = share.reshape((count, share.shape[0] // count) + share.shape[1:])
    sums = [piece.astype(jnp.bfloat16) for piece in halves(blocks[count - 1])]
    for step in range(count - 2, -1, -1):
        sums = [send_tensor(piece.astype(jnp.bfloat16), 1) for piece in sums]
        sums = [
            piece.astype(jnp.float32) + more.astype(jnp.float32)
            for piece, more in zip(sums, halves(blocks[step]))
        ]
    return jnp.concatenate(sums, axis=0)


def shift_blocks(share):
    count = lax.axis_size("tensor")
    index = lax.axis_index("tensor")
    twice = share.reshape((count, share.shape[0] // count) + share.shape[1:])
    twice = jnp.concatenate([twice, twice], axis=0)
    return exchange(lax.dynamic_slice_in_dim(twice, (count - index) % count, count, 0), "tensor")


def exchange(values, axes):
    return lax.all_to_all(values, axes, split_axis=0, concat_axis=0, tiled=True)


def dp_orders():
    count = lax.axis_size("dp")
    masks = [1 << k for k in range(count.bit_length() - 1)]
    return (masks[1:] + masks[:1], masks[:0:-1] + masks[:1])


def swap_dp(values, mask):
    count = lax.axis_size("dp")
    return lax.ppermute(values, "dp", [(i, i ^ mask) for i in range(count)])


def axis_of(mask):
    return lax.axis_size("dp").bit_length() - 1 - mask.bit_length()


def gather_dp(own, order):
    count = lax.axis_size("dp")
    index = lax.axis_index("dp")
    current = own.reshape((1,) * (count.bit_length() - 1) + own.shape)
    for mask in order:
        other = swap_dp(current, mask)
        high = (index & mask) > 0
        current = jnp.concatenate(
            [jnp.where(high, other, current), jnp.where(high, current, other)], axis=axis_of(mask)
        )
    return current.reshape((count,) + own.shape)


def scatter_dp(blocks, order):
    count = lax.axis_size("dp")
    index = lax.axis_index("dp")
    own = blocks.shape[1:]
    current = blocks.reshape((2,) * (count.bit_length() - 1) + own)
    for mask in order[::-1]:
        high = ((index & mask) > 0).astype(jnp.int32)
        axis = axis_of(mask)
        keep = lax.dynamic_slice_in_dim(current, high, 1, axis)
        give = lax.dynamic_slice_in_dim(current, 1 - high, 1, axis)
        got = swap_dp(give.astype(jnp.bfloat16), mask)
        current = keep.astype(jnp.float32) + got.astype(jnp.float32)
    return current.reshape(own)


def causal_scores(query_nope, query_rope, key_nope, key_rope, seen):
    scores = einsum32("qhd,khd->hqk", query_nope, key_nope)
    scores = scores + einsum32("qhd,kd->hqk", query_rope, key_rope)
    return jnp.where(seen[None], scores * (NOPE + ROPE) ** (-0.5), NEGATIVE)


def attend_forward(query_nope, query_rope, key_nope, key_rope, values, seen):
    scores = causal_scores(query_nope, query_rope, key_nope, key_rope, seen)
    logsum = jax.nn.logsumexp(scores, axis=-1)
    probs = jnp.exp(scores - logsum[..., None]).astype(jnp.bfloat16)
    return (einsum32("hqk,khd->qhd", probs, values).astype(jnp.bfloat16), logsum)


def attend_backward(
    query_nope, query_rope, key_nope, key_rope, values, mixed, mixed_grad, logsum, seen
):
    scores = causal_scores(query_nope, query_rope, key_nope, key_rope, seen)
    probs_full = jnp.exp(scores - logsum[..., None])
    probs = probs_full.astype(jnp.bfloat16)
    values_grad = einsum32("hqk,qhd->khd", probs, mixed_grad)
    probs_grad = einsum32("qhd,khd->hqk", mixed_grad, values)
    delta = einsum32("qhd,qhd->hq", mixed_grad, mixed)
    score_grad = (probs_full * (probs_grad - delta[..., None]) * (NOPE + ROPE) ** (-0.5)).astype(
        jnp.bfloat16
    )
    query_nope_grad = einsum32("hqk,khd->qhd", score_grad, key_nope)
    query_rope_grad = einsum32("hqk,kd->qhd", score_grad, key_rope)
    key_nope_grad = einsum32("hqk,qhd->khd", score_grad, query_nope)
    key_rope_grad = einsum32("hqk,qhd->kd", score_grad, query_rope)
    return (query_nope_grad, query_rope_grad, key_nope_grad, key_rope_grad, values_grad)


def per_device(
    block_in,
    attn_norm_gain,
    query_weight,
    kv_down_weight,
    latent_gain,
    kv_up_weight,
    output_weight,
    ffn_norm_gain,
    router_weight,
    expert_ids,
    shared_gate_weight,
    shared_up_weight,
    shared_down_weight,
    expert_gate_weight,
    expert_up_weight,
    expert_down_weight,
    out_grad,
):
    wide = jnp.float32
    narrow = jnp.bfloat16
    own_rows = block_in.shape[0]
    width = block_in.shape[1]
    dp_count = lax.axis_size("dp")
    tensor_count = lax.axis_size("tensor")
    tensor_index = lax.axis_index("tensor")
    group = own_rows * tensor_count
    owner_count = dp_count // ACTIVE
    slot_piece = CAP // owner_count
    slots = ACTIVE * CAP
    both = ("dp", "tensor")
    first_order, second_order = dp_orders()

    gains = jnp.concatenate([attn_norm_gain, ffn_norm_gain, latent_gain])
    gains = exchange(
        jnp.broadcast_to(gains[None], (dp_count * tensor_count, gains.shape[0])), both
    ).astype(wide)
    split_one = attn_norm_gain.shape[0]
    gain_one = gains[:, :split_one].reshape(-1)
    gain_two = gains[:, split_one : 2 * split_one].reshape(-1)
    gain_lat = gains[:, 2 * split_one :].reshape(-1)

    all_in = gather_tensor(block_in)
    small = jnp.concatenate([kv_down_weight, router_weight], axis=1)
    small = exchange(jnp.broadcast_to(small[None], (tensor_count,) + small.shape), "tensor")
    query_full = gather_dp(query_weight, first_order).reshape(width, -1)
    kv_up_full = gather_dp(kv_up_weight, second_order).reshape(LATENT, -1)
    small = gather_dp(small, second_order).reshape(width, -1)
    kv_down = small[:, : LATENT + ROPE]
    router = small[:, LATENT + ROPE :]
    output_full = jnp.moveaxis(gather_dp(output_weight, second_order), 0, 1).reshape(
        output_weight.shape[0], width
    )
    grad_all = gather_tensor(out_grad)

    heads = query_full.shape[1] // (NOPE + ROPE)
    residual_all = all_in.astype(wide)
    scale_all = rms_scale(residual_all)
    hidden_one = (residual_all * scale_all * gain_one).astype(narrow)
    latent_in = matmul(hidden_one, kv_down).astype(narrow)
    compressed = latent_in[:, :LATENT].astype(wide)
    scale_lat = rms_scale(compressed)
    normed_lat = compressed * scale_lat
    latent = (normed_lat * gain_lat).astype(narrow)
    place = (jnp.arange(group) + tensor_index * own_rows) % group
    position = (place % SEQ).astype(wide)
    sequence = place // SEQ
    seen = (place[:, None] >= place[None, :]) & (sequence[:, None] == sequence[None, :])
    cosine, sine = rope_tables(position)
    key_rope = rotate(latent_in[:, LATENT:].astype(wide), cosine, sine).astype(narrow)
    query = matmul(hidden_one, query_full).reshape(group, heads, NOPE + ROPE)
    query_nope = query[..., :NOPE].astype(narrow)
    query_rope = rotate(query[..., NOPE:], cosine[:, None, :], sine[:, None, :]).astype(narrow)
    keyvalue = matmul(latent, kv_up_full).astype(narrow).reshape(group, heads, NOPE + VDIM)
    key_nope = keyvalue[..., :NOPE]
    values = keyvalue[..., NOPE:]
    mixed, logsum = attend_forward(query_nope, query_rope, key_nope, key_rope, values, seen)
    mixed_flat = mixed.reshape(group, heads * VDIM)
    attn_own = scatter_tensor(matmul(mixed_flat, output_full))

    residual_in = block_in.astype(wide)
    after_attn = residual_in + attn_own
    scale_two = rms_scale(after_attn)
    normed_two = after_attn * scale_two
    hidden_two_own = (normed_two * gain_two).astype(narrow)
    hidden_two = gather_tensor(hidden_two_own)

    shared_gate = gather_dp(shared_gate_weight, first_order).reshape(width, -1)
    shared_up = gather_dp(shared_up_weight, second_order).reshape(width, -1)
    shared_down = jnp.moveaxis(gather_dp(shared_down_weight, first_order), 0, 1).reshape(
        shared_down_weight.shape[0], width
    )
    slabs = jnp.concatenate(
        [expert_gate_weight, expert_up_weight, jnp.swapaxes(expert_down_weight, 1, 2)], axis=1
    )
    slabs = exchange(jnp.repeat(slabs, owner_count, axis=0), "dp")
    rows_dp = expert_gate_weight.shape[1]
    gate_here = slabs[:, :rows_dp].reshape(width, -1)
    up_here = slabs[:, rows_dp : 2 * rows_dp].reshape(width, -1)
    down_here = slabs[:, 2 * rows_dp :].reshape(width, -1)

    ids = jnp.concatenate([expert_ids, expert_ids], axis=0)
    ids = lax.dynamic_slice_in_dim(ids, tensor_index * own_rows, group, 0)
    chosen = jnp.any(ids[:, :, None] == jnp.arange(ACTIVE, dtype=jnp.int32)[None, None, :], axis=1)
    ranks = jnp.cumsum(chosen.astype(jnp.int32), axis=0) - 1
    places = (ranks[:, :, None] == jnp.arange(CAP, dtype=jnp.int32)[None, None, :]) & chosen[
        :, :, None
    ]
    pick = places.astype(narrow).reshape(group, slots)
    grad_in = left_dot(pick, grad_all).astype(narrow)
    grad_here = exchange(grad_in.reshape(dp_count, slot_piece, width), "dp").reshape(-1, width)
    tokens_in = left_dot(pick, hidden_two).astype(narrow)
    rows_here = exchange(tokens_in.reshape(dp_count, slot_piece, width), "dp").reshape(-1, width)
    route_prob = jax.nn.softmax(matmul(hidden_two, router), axis=-1)
    gate = jnp.where(chosen, route_prob[:, :ACTIVE], 0.0)
    weight = jnp.sum(jnp.where(places, gate[:, :, None], 0.0), axis=0)
    weight_here = exchange(weight.reshape(dp_count, slot_piece), "dp").reshape(-1)

    shared_a = matmul(hidden_two, shared_gate)
    shared_b = matmul(hidden_two, shared_up)
    shared_hidden = (jax.nn.silu(shared_a) * shared_b).astype(narrow)
    shared_up_grad = right_dot(grad_all, shared_down)
    shared_a_grad = (shared_up_grad * shared_b * silu_grad(shared_a)).astype(narrow)
    shared_b_grad = (shared_up_grad * jax.nn.silu(shared_a)).astype(narrow)
    hidden_two_share = right_dot(shared_a_grad, shared_gate) + right_dot(shared_b_grad, shared_up)
    moe_share = matmul(shared_hidden, shared_down)
    shared_down_grad = left_dot(shared_hidden, grad_all)
    shared_gate_grad = left_dot(hidden_two, shared_a_grad)
    shared_up_wgrad = left_dot(hidden_two, shared_b_grad)

    owned_a = matmul(rows_here, gate_here)
    owned_b = matmul(rows_here, up_here)
    owned_hidden = (jax.nn.silu(owned_a) * owned_b).astype(narrow)
    owned_up_grad = matmul(grad_here, down_here)
    owned_slot = jnp.sum(owned_up_grad * owned_hidden.astype(wide), axis=-1)
    owned_hidden_grad = weight_here[:, None] * owned_up_grad
    owned_a_grad = (owned_hidden_grad * owned_b * silu_grad(owned_a)).astype(narrow)
    owned_b_grad = (owned_hidden_grad * jax.nn.silu(owned_a)).astype(narrow)
    owned_scaled = (weight_here[:, None] * owned_hidden.astype(wide)).astype(narrow)
    owned_back = (right_dot(owned_a_grad, gate_here) + right_dot(owned_b_grad, up_here)).astype(
        narrow
    )
    back_flat = exchange(owned_back.reshape(dp_count, slot_piece, width), "dp").reshape(
        -1, width
    )
    per_slot = exchange(owned_slot.reshape(dp_count, slot_piece), "dp").reshape(1, ACTIVE, CAP)
    owned_out = (weight_here[:, None] * right_dot(owned_hidden, down_here)).astype(narrow)
    routed_flat = exchange(owned_out.reshape(dp_count, slot_piece, width), "dp").reshape(
        -1, width
    )
    terms = jnp.concatenate(
        [
            left_dot(rows_here, owned_a_grad).astype(narrow).reshape(dp_count, rows_dp, -1),
            left_dot(rows_here, owned_b_grad).astype(narrow).reshape(dp_count, rows_dp, -1),
            left_dot(grad_here, owned_scaled).astype(narrow).reshape(dp_count, rows_dp, -1),
        ],
        axis=1,
    )
    terms = exchange(terms, "dp").astype(wide)
    terms = jnp.sum(terms.reshape((ACTIVE, owner_count) + terms.shape[1:]), axis=1)
    expert_gate_grad = terms[:, :rows_dp]
    expert_up_wgrad = terms[:, rows_dp : 2 * rows_dp]
    expert_down_grad = jnp.swapaxes(terms[:, 2 * rows_dp :], 1, 2)

    hidden_two_share = hidden_two_share + matmul(pick, back_flat)
    gate_share = jnp.sum(jnp.where(places, per_slot, 0.0), axis=-1)
    gate_grad = jnp.sum(shift_blocks(gate_share), 0)
    hidden_two_grad = scatter_tensor(hidden_two_share)
    prob_own = jax.nn.softmax(matmul(hidden_two_own, router), axis=-1)
    prob_grad = jnp.concatenate(
        [gate_grad, jnp.zeros((own_rows, prob_own.shape[1] - ACTIVE), wide)], axis=-1
    )
    logit_grad = (
        prob_own * (prob_grad - jnp.sum(prob_own * prob_grad, axis=-1, keepdims=True))
    ).astype(narrow)
    router_grad = left_dot(hidden_two_own, logit_grad)
    hidden_two_grad = hidden_two_grad + right_dot(logit_grad, router)
    gain_two_grad = jnp.sum(hidden_two_grad * normed_two, axis=0)
    after_attn_grad = out_grad.astype(wide) + norm_back(
        hidden_two_grad * gain_two, normed_two, scale_two
    )
    residual_low = gather_tensor(after_attn_grad.astype(narrow))
    moe_own = scatter_tensor(moe_share + matmul(pick, routed_flat))
    block_out = (after_attn + moe_own).astype(narrow)

    mixed_grad = right_dot(residual_low, output_full).astype(narrow).reshape(group, heads, VDIM)
    output_grad = left_dot(mixed_flat, residual_low)
    query_nope_grad, query_rope_grad, key_nope_grad, key_rope_grad, values_grad = attend_backward(
        query_nope, query_rope, key_nope, key_rope, values, mixed, mixed_grad, logsum, seen
    )
    keyvalue_grad = (
        jnp.concatenate([key_nope_grad, values_grad], axis=-1)
        .astype(narrow)
        .reshape(group, heads * (NOPE + VDIM))
    )
    latent_grad = right_dot(keyvalue_grad, kv_up_full)
    gain_lat_grad = jnp.sum(latent_grad * normed_lat, axis=0)
    compressed_grad = norm_back(latent_grad * gain_lat, normed_lat, scale_lat)
    key_rope_back = unrotate(key_rope_grad, cosine, sine)
    latent_in_share = jnp.concatenate([compressed_grad, key_rope_back], axis=-1)
    latent_in_low = jnp.sum(
        shift_blocks(latent_in_share.astype(narrow)).astype(wide), axis=0
    ).astype(narrow)
    query_rope_back = unrotate(query_rope_grad, cosine[:, None, :], sine[:, None, :])
    query_grad = (
        jnp.concatenate([query_nope_grad, query_rope_back], axis=-1)
        .astype(narrow)
        .reshape(group, heads * (NOPE + ROPE))
    )
    hidden_one_share = right_dot(query_grad, query_full)
    hidden_one_grad = scatter_tensor(hidden_one_share)
    query_wgrad = left_dot(hidden_one, query_grad)
    kv_up_grad = left_dot(latent, keyvalue_grad)
    latent_back = right_dot(latent_in_low, kv_down)
    hidden_one_grad = hidden_one_grad + latent_back
    scale_one = rms_scale(residual_in)
    normed_one = residual_in * scale_one
    input_grad = after_attn_grad + norm_back(hidden_one_grad * gain_one, normed_one, scale_one)

    def by_dp(values, axis):
        shape = values.shape
        values = values.reshape(
            shape[:axis] + (dp_count, shape[axis] // dp_count) + shape[axis + 1 :]
        )
        return jnp.moveaxis(values, axis, 0).astype(narrow)

    dense_grads = (
        scatter_dp(by_dp(query_wgrad, 0), first_order),
        scatter_dp(by_dp(kv_up_grad, 0), second_order),
        scatter_dp(by_dp(output_grad, 1), second_order),
        scatter_dp(by_dp(shared_gate_grad, 0), first_order),
        scatter_dp(by_dp(shared_up_wgrad, 0), second_order),
        scatter_dp(by_dp(shared_down_grad, 1), first_order),
    )

    hidden_own = hidden_one[:own_rows]
    tall = jnp.concatenate([left_dot(hidden_own, latent_in_low), router_grad], axis=1)
    tall = tall.reshape(dp_count, tensor_count, -1, tall.shape[1])
    tall = jnp.sum(exchange(jnp.swapaxes(tall, 0, 1).astype(narrow), "tensor").astype(wide), 0)
    tall = jnp.sum(exchange(tall.astype(narrow), "dp").astype(wide), 0)
    kv_down_grad = tall[:, : LATENT + ROPE]
    router_grad = tall[:, LATENT + ROPE :]
    gain_one_grad = jnp.sum(hidden_one_share * (residual_all * scale_all), axis=0) + jnp.sum(
        latent_back * normed_one, axis=0
    )
    devices = dp_count * tensor_count
    gain_grads = jnp.concatenate(
        [
            gain_one_grad.reshape(devices, -1),
            gain_two_grad.reshape(devices, -1),
            gain_lat_grad.reshape(devices, -1),
        ],
        axis=1,
    )
    gain_grads = jnp.sum(exchange(gain_grads, both), axis=0)
    return (
        block_out,
        input_grad,
        gain_grads[:split_one],
        dense_grads[0],
        kv_down_grad,
        gain_grads[2 * split_one :],
        dense_grads[1],
        dense_grads[2],
        gain_grads[split_one : 2 * split_one],
        router_grad,
        dense_grads[3],
        dense_grads[4],
        dense_grads[5],
        expert_gate_grad,
        expert_up_wgrad,
        expert_down_grad,
    )


def solution(mesh):
    in_specs = (
        P(("dp", "tensor"), None),
        P(("dp", "tensor")),
        P("dp", "tensor"),
        P(("dp", "tensor"), None),
        P(("dp", "tensor")),
        P("dp", "tensor"),
        P("tensor", "dp"),
        P(("dp", "tensor")),
        P(("dp", "tensor"), None),
        P("dp", None),
        P("dp", "tensor"),
        P("dp", "tensor"),
        P("tensor", "dp"),
        P(None, "dp", "tensor"),
        P(None, "dp", "tensor"),
        P(None, "tensor", "dp"),
        P(("dp", "tensor"), None),
    )
    out_specs = (
        P(("dp", "tensor"), None),
        P(("dp", "tensor"), None),
        P(("dp", "tensor")),
        P("dp", "tensor"),
        P(("dp", "tensor"), None),
        P(("dp", "tensor")),
        P("dp", "tensor"),
        P("tensor", "dp"),
        P(("dp", "tensor")),
        P(("dp", "tensor"), None),
        P("dp", "tensor"),
        P("dp", "tensor"),
        P("tensor", "dp"),
        P(None, "dp", "tensor"),
        P(None, "dp", "tensor"),
        P(None, "tensor", "dp"),
    )
    return jax.shard_map(
        per_device, mesh=mesh, in_specs=in_specs, out_specs=out_specs, check_vma=False
    )
```

time: 1500 us -> 928 us (0.62)
  waiting for transfers between devices: 845 us -> 314 us
  blocking collectives: 217 us -> 0 us
  starting transfers between devices: 48.2 us -> 174 us
  local copies, waits for them, and re-layouts: 101 us -> 170 us
    reduce_scatter x12 -> x0, waiting for transfers between devices: 537 us -> none  [the longest x1 155 us: per_device(): lax.psum_scatter(kv_down_grad, ('dp', 'tensor'), scatter_dimension=0, til...]
    ppermute x0 -> x87, waiting for transfers between devices: none -> 262 us  [the longest x39 138 us: swap_dp(): return lax.ppermute(values, 'dp', [(i, i ^ mask) for i in range(count)])]
    all_gather x11 -> x0, waiting for transfers between devices: 159 us -> none  [the longest x1 44.6 us: per_device(): lax.all_gather(after_attn_grad.astype(narrow), 'tensor', axis=0, tiled=True)]
    ppermute x0 -> x87, starting transfers between devices: none -> 106 us  [the longest x48 73.3 us: send_tensor(): lax.ppermute(values, 'tensor', [(i, (i + step) % count) for i in range(co...]
    all_to_all x11 -> x15, waiting for transfers between devices: 144 us -> 52.3 us  [exchange(): return lax.all_to_all(values, axes, split_axis=0, concat_axis=0, tiled=True)]
    all_gather x2 -> x0, blocking collectives: 89.3 us -> none  [the longest x1 73.4 us: per_device(): lax.all_gather(router_weight, ('dp', 'tensor'), axis=0, tiled=True)]
    unnamed x2 -> x0, blocking collectives: 85.1 us -> none
    scatter-add x3 -> x0, other arithmetic: 73.8 us -> none  [the longest x1 36.2 us: per_device(): jnp.zeros((group, ACTIVE), wide).at[source, expert_of].add(per_slot)]
  transfers between devices with their start and end apart: 36 -> 102, of which waited for: 23 -> 47; matrix products, arithmetic and copies ran while one was open for 22% -> 42% of each run, Pallas kernels for 0% -> 0%
where the time goes in v1:
time: 928 us; the launch traced here: 917 us
  waiting for transfers between devices  314 us (34%)
  starting transfers between devices  174 us (19%)
  local copies, waits for them, and re-layouts  170 us (18%)
  matrix products  130 us (14%)
  other arithmetic  126 us (14%)
    ppermute x39, waiting for transfers between devices, swap_dp(): return lax.ppermute(values, 'dp', [(i, i ^ mask) for i in range(count)])  138 us
    ppermute x48, waiting for transfers between devices, send_tensor(): lax.ppermute(values, 'tensor', [(i, (i + step) % count) for i in range(co...  123 us
    ppermute x48, starting transfers between devices, send_tensor(): lax.ppermute(values, 'tensor', [(i, (i + step) % count) for i in range(co...  73.3 us
    all_to_all x15, starting transfers between devices, exchange(): return lax.all_to_all(values, axes, split_axis=0, concat_axis=0, tiled=True)  68.3 us
    all_to_all x15, waiting for transfers between devices, exchange(): return lax.all_to_all(values, axes, split_axis=0, concat_axis=0, tiled=True)  52.3 us
    dot_general x14, matrix products, matmul(): return jnp.dot(left, right, preferred_element_type=jnp.float32)  49.9 us
    unnamed x385, local copies, waits for them, and re-layouts  42.6 us
    dot_general x13, matrix products, left_dot(): lax.dot_general(left, right, (((0,), (0,)), ((), ())), preferred_element_...  37.6 us
  transfers between devices with their start and end apart: 102, of which 47 were waited for; matrix products, arithmetic and copies ran while one was open for 42% of the time, Pallas kernels for 0%

profile of v1, /device:TPU:0, one launch (start us, length us, event | category | flops | bytes accessed | tf_op | source)
XLA Modules:
  0.0 916.6 jit_solution(6643752192992975888)
XLA Ops:
  2.1 7.3 all-to-all-start
  125.1 53.1 %collective-permute-done.6 = bf16[1,1,1,4,64,640]{5,4,3,2,1,0:T(8,128)(2,1)S(1)} collective-permute-done((bf16[1,1,1,4,64,640]{5,4,3,2,1,0:T(8,128)(2,1)}, bf16[1,1,1,4,64,640]{5,4,3,2,1,0:T(8,128)(2,1)S(1)}, u32[]{:S(2)}, u32[]{:S(2)}) %collective-permute-start.6) | collective-permute-done | bytes 327712 | tf_op jit(solution)/shard_map/ppermute | solution.py:127
  186.2 11.1 %collective-permute-done.13 = bf16[1,2,1,256,768]{4,3,2,1,0:T(8,128)(2,1)S(1)} collective-permute-done((bf16[1,2,1,256,768]{4,3,2,1,0:T(8,128)(2,1)S(1)}, bf16[1,2,1,256,768]{4,3,2,1,0:T(8,128)(2,1)S(1)}, u32[]{:S(2)}, u32[]{:S(2)}) %collective-permute-start.13) | collective-permute-done | bytes 786464 | tf_op jit(solution)/shard_map/ppermute | solution.py:127
  243.0 7.3 collective-permute-done.18
  258.8 7.6 collective-permute-done.19
  276.3 7.8 reshape_reshape.18
  288.6 7.6 reshape_reshape.19
  361.9 7.9 convert_element_type.579
  369.9 10.2 %constant_dynamic-slice_fusion.4 = (bf16[2,2,1,256,704]{3,2,1,0,4:T(2,128)(2,1)}, bf16[2,2,1,256,704]{3,2,1,0,4:T(2,128)(2,1)S(1)}) fusion(bf16[2,2,2,256,704]{3,2,1,0,4:T(2,128)(2,1)} %convert_element_type.579, s32[]{:T(128)S(6)} %select_n.454, s32[]{:T(128)S(6)} %select_n.455), kind=kLoop, calls=%fused_computation.369 | loop fusion | bytes 5767176 | tf_op jit(solution)/shard_map/dynamic_slice | solution.py:155
  385.7 8.2 convert_element_type.587
  393.9 10.3 %constant_dynamic-slice_fusion.2 = (bf16[2,2,1,256,704]{3,2,1,0,4:T(2,128)(2,1)}, bf16[2,2,1,256,704]{3,2,1,0,4:T(2,128)(2,1)S(1)}) fusion(bf16[2,2,2,256,704]{3,2,1,0,4:T(2,128)(2,1)} %convert_element_type.587, s32[]{:T(128)S(6)} %select_n.454, s32[]{:T(128)S(6)} %select_n.455), kind=kLoop, calls=%fused_computation.367 | loop fusion | bytes 5767176 | tf_op jit(solution)/shard_map/dynamic_slice | solution.py:155
  426.0 6.0 fusion.155
  452.9 9.7 %all-to-all-done.6 = bf16[8,96,2048]{2,1,0:T(8,128)(2,1)} async-done(((bf16[8,96,2048]{2,1,0:T(8,128)(2,1)}), bf16[8,96,2048]{2,1,0:T(8,128)(2,1)}, u32[]{:S(2)}, u32[]{:S(2)}) %all-to-all-start.6) | async-done | bytes 3145760 | tf_op jit(solution)/shard_map/all_to_all | solution.py:116
  462.6 6.0 fusion.32
  485.7 10.2 %all-to-all-done.2 = f32[8,1,96]{2,1,0:T(1,128)} async-done(((f32[8,1,96]{2,1,0:T(1,128)}), f32[8,1,96]{2,1,0:T(1,128)}, u32[]{:S(2)}, u32[]{:S(2)}) %all-to-all-start.2) | async-done | bytes 3104 | tf_op jit(solution)/shard_map/all_to_all | solution.py:116
  526.5 43.3 %collective-permute-done.85 = bf16[1,2,1,704,256]{4,3,2,1,0:T(8,128)(2,1)S(1)} collective-permute-done((bf16[1,2,1,704,256]{4,3,2,1,0:T(8,128)(2,1)S(1)}, bf16[1,2,1,704,256]{4,3,2,1,0:T(8,128)(2,1)S(1)}, u32[]{:S(2)}, u32[]{:S(2)}) %collective-permute-start.85) | collective-permute-done | bytes 720928 | tf_op jit(solution)/shard_map/ppermute | solution.py:127
  604.8 8.3 fusion.146
  616.8 10.2 %all-to-all-done.5 = bf16[8,96,2048]{2,1,0:T(8,128)(2,1)} async-done(((bf16[8,96,2048]{2,1,0:T(8,128)(2,1)}), bf16[8,96,2048]{2,1,0:T(8,128)(2,1)}, u32[]{:S(2)}, u32[]{:S(2)}) %all-to-all-start.5) | async-done | bytes 3145760 | tf_op jit(solution)/shard_map/all_to_all | solution.py:116
  705.7 6.5 convert_element_type.607
  715.0 6.4 collective-permute-done.59
  798.1 6.6 collective-permute-done.65
  867.0 10.9 %collective-permute-done.70 = bf16[1,2,1,256,768]{4,3,2,1,0:T(8,128)(2,1)} collective-permute-done((bf16[1,2,1,256,768]{4,3,2,1,0:T(8,128)(2,1)}, bf16[1,2,1,256,768]{4,3,2,1,0:T(8,128)(2,1)}, u32[]{:S(2)}, u32[]{:S(2)}) %collective-permute-start.70) | collective-permute-done | bytes 786464 | tf_op jit(solution)/shard_map/ppermute | solution.py:127
  882.6 14.7 %all-to-all-done.12 = bf16[4,8,64,640]{3,2,1,0:T(8,128)(2,1)} async-done(((bf16[4,8,64,640]{3,2,1,0:T(8,128)(2,1)}), bf16[4,8,64,640]{3,2,1,0:T(8,128)(2,1)}, u32[]{:S(2)}, u32[]{:S(2)}) %all-to-all-start.12) | async-done | bytes 2621472 | tf_op jit(solution)/shard_map/all_to_all | solution.py:116
  908.3 7.2 all-to-all-done.13
  (819 shorter events, 628.4 us)
Async XLA Ops:
  17.0 55.7 %collective-permute-start.12 = (bf16[1,1,1,256,768]{4,3,2,1,0:T(8,128)(2,1)}, bf16[1,1,1,256,768]{4,3,2,1,0:T(8,128)(2,1)}, u32[]{:S(2)}, u32[]{:S(2)}) collective-permute-start(bf16[1,1,1,256,768]{4,3,2,1,0:T(8,128)(2,1)} %bitcast.319), channel_id=1, source_target_pairs={{0,8},{4,12},{8,0},{12,4},{16,24},{20,28},{24,16},{28,20},{1,9},{5... | collective-permute-start | bytes 1179656 | tf_op jit(solution)/shard_map/ppermute | solution.py:127
  31.3 85.7 %all-to-all-start.1 = ((bf16[4,64,640]{2,1,0:T(8,128)(2,1)}), bf16[4,64,640]{2,1,0:T(8,128)(2,1)}, u32[]{:S(2)}, u32[]{:S(2)}) async-start(bf16[4,64,640]{2,1,0:T(8,128)(2,1)} %broadcast_in_dim.43), calls=%async_computation.1 | async-start | bytes 655360 | tf_op jit(solution)/shard_map/all_to_all | solution.py:116
  56.4 65.4 %collective-permute-start.16 = (bf16[2,1,1,512,256]{4,3,2,1,0:T(8,128)(2,1)}, bf16[2,1,1,512,256]{4,3,2,1,0:T(8,128)(2,1)}, u32[]{:S(2)}, u32[]{:S(2)}) collective-permute-start(bf16[2,1,1,512,256]{4,3,2,1,0:T(8,128)(2,1)} %pad_maximum_fusion.24), channel_id=1, source_target_pairs={{0,8},{4,12},{8,0},{12,4},{16,24},{20,28},{24,16},{28,20},{1,9},{5... | collective-permute-start | bytes 1572872 | tf_op jit(solution)/shard_map/ppermute | solution.py:127
  77.1 105.1 %collective-permute-start.34 = (bf16[2,1,1,256,704]{3,4,2,1,0:T(8,128)(2,1)}, bf16[2,1,1,256,704]{3,4,2,1,0:T(8,128)(2,1)}, u32[]{:S(2)}, u32[]{:S(2)}) collective-permute-start(bf16[2,1,1,256,704]{3,4,2,1,0:T(8,128)(2,1)} %pad_maximum_fusion.20), channel_id=1, source_target_pairs={{0,8},{4,12},{8,0},{12,4},{16,24},{20,28},{24,16},{28,20},{1,9},{5... | collective-permute-start | bytes 2162696 | tf_op jit(solution)/shard_map/ppermute | solution.py:127
  77.7 121.0 %collective-permute-start.31 = (bf16[1,2,1,256,704]{3,4,2,1,0:T(8,128)(2,1)}, bf16[1,2,1,256,704]{3,4,2,1,0:T(8,128)(2,1)}, u32[]{:S(2)}, u32[]{:S(2)}) collective-permute-start(bf16[1,2,1,256,704]{3,4,2,1,0:T(8,128)(2,1)} %pad_maximum_fusion.19), channel_id=1, source_target_pairs={{0,16},{4,20},{8,24},{12,28},{16,0},{20,4},{24,8},{28,12},{1,17},{... | collective-permute-start | bytes 2162696 | tf_op jit(solution)/shard_map/ppermute | solution.py:127
  106.2 95.6 %collective-permute-start.37 = (bf16[1,2,1,704,256]{4,3,2,1,0:T(8,128)(2,1)}, bf16[1,2,1,704,256]{4,3,2,1,0:T(8,128)(2,1)}, u32[]{:S(2)}, u32[]{:S(2)}) collective-permute-start(bf16[1,2,1,704,256]{4,3,2,1,0:T(8,128)(2,1)} %pad_maximum_fusion.21), channel_id=1, source_target_pairs={{0,16},{4,20},{8,24},{12,28},{16,0},{20,4},{24,8},{28,12},{1,17},{... | collective-permute-start | bytes 2162696 | tf_op jit(solution)/shard_map/ppermute | solution.py:127
  108.4 71.5 %collective-permute-start.11 = (bf16[2,2,1,64,1024]{4,3,2,1,0:T(8,128)(2,1)}, bf16[2,2,1,64,1024]{4,3,2,1,0:T(8,128)(2,1)}, u32[]{:S(2)}, u32[]{:S(2)}) collective-permute-start(bf16[2,2,1,64,1024]{4,3,2,1,0:T(8,128)(2,1)} %pad_maximum_fusion.23), channel_id=1, source_target_pairs={{0,4},{4,0},{8,12},{12,8},{16,20},{20,16},{24,28},{28,24},{1,5},{5... | collective-permute-start | bytes 1572872 | tf_op jit(solution)/shard_map/ppermute | solution.py:127
  117.0 194.5 %all-to-all-start.4 = ((bf16[8,768,352]{1,2,0:T(8,128)(2,1)}), bf16[8,768,352]{1,2,0:T(8,128)(2,1)}, u32[]{:S(2)}, u32[]{:S(2)}) async-start(bf16[8,768,352]{1,2,0:T(8,128)(2,1)} %pad_maximum_fusion), calls=%async_computation.4 | async-start | bytes 8650752 | tf_op jit(solution)/shard_map/all_to_all | solution.py:116
  121.9 56.4 %collective-permute-start.6 = (bf16[1,1,1,4,64,640]{5,4,3,2,1,0:T(8,128)(2,1)}, bf16[1,1,1,4,64,640]{5,4,3,2,1,0:T(8,128)(2,1)S(1)}, u32[]{:S(2)}, u32[]{:S(2)}) collective-permute-start(bf16[1,1,1,4,64,640]{5,4,3,2,1,0:T(8,128)(2,1)} %bitcast.2), channel_id=1, source_target_pairs={{0,16},{4,20},{8,24},{12,28},{16,0},{20,4},{24,8},{28,12},{1,17},{... | collective-permute-start | bytes 983048 | tf_op jit(solution)/shard_map/ppermute | solution.py:127
  204.9 50.7 %collective-permute-start.38 = (bf16[2,2,1,704,256]{4,3,2,1,0:T(8,128)(2,1)}, bf16[2,2,1,704,256]{4,3,2,1,0:T(8,128)(2,1)}, u32[]{:S(2)}, u32[]{:S(2)}) collective-permute-start(bf16[2,2,1,704,256]{4,3,2,1,0:T(8,128)(2,1)} %pad_maximum_fusion.12), channel_id=1, source_target_pairs={{0,4},{4,0},{8,12},{12,8},{16,20},{20,16},{24,28},{28,24},{1,5},{5... | collective-permute-start | bytes 4325384 | tf_op jit(solution)/shard_map/ppermute | solution.py:127
  343.1 77.0 %all-to-all-start.3 = ((bf16[8,96,2048]{2,1,0:T(8,128)(2,1)}), bf16[8,96,2048]{2,1,0:T(8,128)(2,1)}, u32[]{:S(2)}, u32[]{:S(2)}) async-start(bf16[8,96,2048]{2,1,0:T(8,128)(2,1)} %bitcast.294), calls=%async_computation.3 | async-start | bytes 6291456 | tf_op jit(solution)/shard_map/all_to_all | solution.py:116
  381.7 54.2 %collective-permute-start.78 = (bf16[2,2,1,256,704]{3,4,2,1,0:T(8,128)(2,1)}, bf16[2,2,1,256,704]{3,4,2,1,0:T(8,128)(2,1)}, u32[]{:S(2)}, u32[]{:S(2)}) collective-permute-start(bf16[2,2,1,256,704]{3,4,2,1,0:T(8,128)(2,1)} %copy.212), channel_id=1, source_target_pairs={{0,4},{4,0},{8,12},{12,8},{16,20},{20,16},{24,28},{28,24},{1,5},{5... | collective-permute-start | bytes 4325384 | tf_op jit(solution)/shard_map/ppermute | solution.py:127
  418.5 98.5 %collective-permute-start.84 = (bf16[2,2,1,704,256]{4,3,2,1,0:T(8,128)(2,1)}, bf16[2,2,1,704,256]{4,3,2,1,0:T(8,128)(2,1)}, u32[]{:S(2)}, u32[]{:S(2)}) collective-permute-start(bf16[2,2,1,704,256]{4,3,2,1,0:T(8,128)(2,1)} %constant_dynamic-slice_fusion), channel_id=1, source_target_pairs={{0,4},{4,0},{8,12},{12,8},{16,20},{20,16},{24,28},{28,24},{1,5},{5... | collective-permute-start | bytes 4325384 | tf_op jit(solution)/shard_map/ppermute | solution.py:127
  439.0 82.4 %collective-permute-start.79 = (bf16[1,2,1,256,704]{3,4,2,1,0:T(8,128)(2,1)}, bf16[1,2,1,256,704]{3,4,2,1,0:T(8,128)(2,1)}, u32[]{:S(2)}, u32[]{:S(2)}) collective-permute-start(bf16[1,2,1,256,704]{3,4,2,1,0:T(8,128)(2,1)} %dynamic-slice_convert_fusion.3), channel_id=1, source_target_pairs={{0,16},{4,20},{8,24},{12,28},{16,0},{20,4},{24,8},{28,12},{1,17},{... | collective-permute-start | bytes 2162696 | tf_op jit(solution)/shard_map/ppermute | solution.py:127
  476.2 48.1 %collective-permute-start.82 = (bf16[2,1,1,256,704]{3,4,2,1,0:T(8,128)(2,1)}, bf16[2,1,1,256,704]{3,4,2,1,0:T(8,128)(2,1)}, u32[]{:S(2)}, u32[]{:S(2)}) collective-permute-start(bf16[2,1,1,256,704]{3,4,2,1,0:T(8,128)(2,1)} %dynamic-slice_convert_fusion.2), channel_id=1, source_target_pairs={{0,8},{4,12},{8,0},{12,4},{16,24},{20,28},{24,16},{28,20},{1,9},{5... | collective-permute-start | bytes 2162696 | tf_op jit(solution)/shard_map/ppermute | solution.py:127
  512.5 71.5 %all-to-all-start.7 = ((bf16[8,96,2048]{2,1,0:T(8,128)(2,1)}), bf16[8,96,2048]{2,1,0:T(8,128)(2,1)}, u32[]{:S(2)}, u32[]{:S(2)}) async-start(bf16[8,96,2048]{2,1,0:T(8,128)(2,1)} %bitcast.266), calls=%async_computation.7 | async-start | bytes 6291456 | tf_op jit(solution)/shard_map/all_to_all | solution.py:116
  519.4 50.4 %collective-permute-start.85 = (bf16[1,2,1,704,256]{4,3,2,1,0:T(8,128)(2,1)S(1)}, bf16[1,2,1,704,256]{4,3,2,1,0:T(8,128)(2,1)S(1)}, u32[]{:S(2)}, u32[]{:S(2)}) collective-permute-start(bf16[1,2,1,704,256]{4,3,2,1,0:T(8,128)(2,1)S(1)} %dynamic-slice_convert_fusion.1), channel_id=1, source_target_pairs={{0,16},{4,20},{8,24},{12,28},{16,0},{20,4},{24,8},{28,12},{1,17},{... | collective-permute-start | bytes 2162696 | tf_op jit(solution)/shard_map/ppermute | solution.py:127
  522.7 48.3 %collective-permute-start.80 = (bf16[1,1,1,256,704]{3,4,2,1,0:T(8,128)(2,1)S(1)}, bf16[1,1,1,256,704]{3,4,2,1,0:T(8,128)(2,1)S(1)}, u32[]{:S(2)}, u32[]{:S(2)}) collective-permute-start(bf16[1,1,1,256,704]{3,4,2,1,0:T(8,128)(2,1)S(1)} %dynamic-slice_convert_fusion.8), channel_id=1, source_target_pairs={{0,8},{4,12},{8,0},{12,4},{16,24},{20,28},{24,16},{28,20},{1,9},{5... | collective-permute-start | bytes 1081352 | tf_op jit(solution)/shard_map/ppermute | solution.py:127
  525.6 51.3 %collective-permute-start.83 = (bf16[1,1,1,256,704]{3,4,2,1,0:T(8,128)(2,1)S(1)}, bf16[1,1,1,256,704]{3,4,2,1,0:T(8,128)(2,1)S(1)}, u32[]{:S(2)}, u32[]{:S(2)}) collective-permute-start(bf16[1,1,1,256,704]{3,4,2,1,0:T(8,128)(2,1)S(1)} %dynamic-slice_convert_fusion.7), channel_id=1, source_target_pairs={{0,16},{4,20},{8,24},{12,28},{16,0},{20,4},{24,8},{28,12},{1,17},{... | collective-permute-start | bytes 1081352 | tf_op jit(solution)/shard_map/ppermute | solution.py:127
  626.9 73.8 %all-to-all-start.14 = ((bf16[8,768,352]{1,2,0:T(8,128)(2,1)}), bf16[8,768,352]{1,2,0:T(8,128)(2,1)}, u32[]{:S(2)}, u32[]{:S(2)}) async-start(bf16[8,768,352]{1,2,0:T(8,128)(2,1)} %pad_maximum_fusion.1), calls=%async_computation.14 | async-start | bytes 8650752 | tf_op jit(solution)/shard_map/all_to_all | solution.py:116
  761.0 50.5 %all-to-all-start.10 = ((bf16[4,128,576]{1,2,0:T(8,128)(2,1)}), bf16[4,128,576]{1,2,0:T(8,128)(2,1)S(1)}, u32[]{:S(2)}, u32[]{:S(2)}) async-start(bf16[4,128,576]{1,2,0:T(8,128)(2,1)} %fusion.57), calls=%async_computation.10 | async-start | bytes 1179648 | tf_op jit(solution)/shard_map/all_to_all | solution.py:116
  774.2 78.5 %collective-permute-start.69 = (bf16[2,2,1,256,768]{4,3,2,1,0:T(8,128)(2,1)}, bf16[2,2,1,256,768]{4,3,2,1,0:T(8,128)(2,1)}, u32[]{:S(2)}, u32[]{:S(2)}) collective-permute-start(bf16[2,2,1,256,768]{4,3,2,1,0:T(8,128)(2,1)} %constant_dynamic-slice_fusion.7), channel_id=1, source_target_pairs={{0,4},{4,0},{8,12},{12,8},{16,20},{20,16},{24,28},{28,24},{1,5},{5... | collective-permute-start | bytes 4718600 | tf_op jit(solution)/shard_map/ppermute | solution.py:127
  781.8 55.8 %collective-permute-start.72 = (bf16[2,2,1,64,1024]{4,3,2,1,0:T(8,128)(2,1)}, bf16[2,2,1,64,1024]{4,3,2,1,0:T(8,128)(2,1)}, u32[]{:S(2)}, u32[]{:S(2)}) collective-permute-start(bf16[2,2,1,64,1024]{4,3,2,1,0:T(8,128)(2,1)} %constant_dynamic-slice_fusion.6), channel_id=1, source_target_pairs={{0,4},{4,0},{8,12},{12,8},{16,20},{20,16},{24,28},{28,24},{1,5},{5... | collective-permute-start | bytes 1572872 | tf_op jit(solution)/shard_map/ppermute | solution.py:127
  832.4 64.9 %all-to-all-start.12 = ((bf16[4,8,64,640]{3,2,1,0:T(8,128)(2,1)}), bf16[4,8,64,640]{3,2,1,0:T(8,128)(2,1)}, u32[]{:S(2)}, u32[]{:S(2)}) async-start(bf16[4,8,64,640]{3,2,1,0:T(8,128)(2,1)} %copy.171), calls=%async_computation.12 | async-start | bytes 5242880 | tf_op jit(solution)/shard_map/all_to_all | solution.py:116
  (256 other events, 2544.6 us)

commit v2 on v1

v2 whole, which is shorter than its diff:
```python
import jax
import jax.numpy as jnp
from jax import lax
from jax.experimental import pallas as pl
from jax.experimental.pallas import tpu as pltpu
from jax.sharding import PartitionSpec as P

NOPE = 128
ROPE = 64
VDIM = 128
LATENT = 512
ACTIVE = 8
SEQ = 512
CAP = 96


LANES = 128
EPSILON = 1e-06
NEGATIVE = -1e30


def matmul(left, right):
    return jnp.dot(left, right, preferred_element_type=jnp.float32)


def left_dot(left, right):
    return lax.dot_general(
        left, right, (((0,), (0,)), ((), ())), preferred_element_type=jnp.float32
    )


def right_dot(left, right):
    return lax.dot_general(
        left, right, (((left.ndim - 1,), (1,)), ((), ())), preferred_element_type=jnp.float32
    )


def einsum32(form, left, right):
    return jnp.einsum(form, left, right, preferred_element_type=jnp.float32)


def rms_scale(values):
    return lax.rsqrt(jnp.mean(values * values, axis=-1, keepdims=True) + EPSILON)


def norm_back(grad_normed, normed, scale):
    return scale * (grad_normed - normed * jnp.mean(grad_normed * normed, axis=-1, keepdims=True))


def rope_tables(position):
    halfway = ROPE // 2
    inverse = jnp.exp(-jnp.log(10000.0) * jnp.arange(halfway).astype(jnp.float32) / halfway)
    angles = position[:, None] * inverse[None, :]
    return (jnp.cos(angles), jnp.sin(angles))


def rotate(values, cosine, sine):
    halfway = ROPE // 2
    first, second = (values[..., :halfway], values[..., halfway:])
    return jnp.concatenate(
        [first * cosine - second * sine, first * sine + second * cosine], axis=-1
    )


def unrotate(grads, cosine, sine):
    halfway = ROPE // 2
    first, second = (grads[..., :halfway], grads[..., halfway:])
    return jnp.concatenate(
        [first * cosine + second * sine, second * cosine - first * sine], axis=-1
    )


def send_tensor(values, step):
    count = lax.axis_size("tensor")
    return lax.ppermute(values, "tensor", [(i, (i + step) % count) for i in range(count)])


def pieces_of(values, parts):
    rows = values.shape[0] // parts
    return [values[i * rows : (i + 1) * rows] for i in range(parts)]


def gather_tensor(own, parts=2):
    pieces = pieces_of(own, parts)
    found = [list(pieces)]
    for _ in range(1, lax.axis_size("tensor")):
        pieces = [send_tensor(piece, -1) for piece in pieces]
        found.append(list(pieces))
    return jnp.concatenate([piece for row in found for piece in row], axis=0)


def scatter_tensor(share, parts=2):
    count = lax.axis_size("tensor")
    blocks = share.reshape((count, share.shape[0] // count) + share.shape[1:])
    sums = [piece.astype(jnp.bfloat16) for piece in pieces_of(blocks[count - 1], parts)]
    for step in range(1, count):
        sums = [send_tensor(piece.astype(jnp.bfloat16), 1) for piece in sums]
        sums = [
            piece.astype(jnp.float32) + more.astype(jnp.float32)
            for piece, more in zip(sums, pieces_of(blocks[count - 1 - step], parts))
        ]
    return jnp.concatenate(sums, axis=0)


def with_column(rows, column):
    high = column.astype(jnp.bfloat16)
    low = (column - high.astype(jnp.float32)).astype(jnp.bfloat16)
    return jnp.concatenate(
        [rows, jnp.pad(jnp.stack([high, low], axis=1), ((0, 0), (0, LANES - 2)))], axis=1
    )


def column_of(rows, place):
    return jnp.sum(rows[:, place : place + 2].astype(jnp.float32), axis=1)


def exchange(values, axes):
    return lax.all_to_all(values, axes, split_axis=0, concat_axis=0, tiled=True)


def dp_orders():
    count = lax.axis_size("dp")
    masks = [1 << k for k in range(count.bit_length() - 1)]
    return (masks[1:] + masks[:1], masks[:0:-1] + masks[:1])


def swap_dp(values, mask):
    count = lax.axis_size("dp")
    return lax.ppermute(values, "dp", [(i, i ^ mask) for i in range(count)])


def axis_of(mask):
    return lax.axis_size("dp").bit_length() - 1 - mask.bit_length()


def gather_dp(own, order):
    count = lax.axis_size("dp")
    index = lax.axis_index("dp")
    current = own.reshape((1,) * (count.bit_length() - 1) + own.shape)
    for mask in order:
        other = swap_dp(current, mask)
        high = (index & mask) > 0
        current = jnp.concatenate(
            [jnp.where(high, other, current), jnp.where(high, current, other)],
            axis=axis_of(mask),
        )
    return current.reshape((count,) + own.shape)


def scatter_dp(blocks, order):
    count = lax.axis_size("dp")
    index = lax.axis_index("dp")
    own = blocks.shape[1:]
    current = blocks.reshape((2,) * (count.bit_length() - 1) + own)
    for mask in order[::-1]:
        high = ((index & mask) > 0).astype(jnp.int32)
        axis = axis_of(mask)
        keep = lax.dynamic_slice_in_dim(current, high, 1, axis)
        give = lax.dynamic_slice_in_dim(current, 1 - high, 1, axis).astype(jnp.bfloat16)
        got = swap_dp(give, mask)
        current = keep.astype(jnp.float32) + got.astype(jnp.float32)
    return current.reshape(own)


def wide_rows(blocks):
    return jnp.moveaxis(blocks, 0, 1).reshape(blocks.shape[1], -1)


def tall_blocks(values):
    count = lax.axis_size("dp")
    values = values.reshape(values.shape[0], count, -1)
    return jnp.moveaxis(values, 1, 0).astype(jnp.bfloat16)


def causal_scores(query_nope, query_rope, key_nope, key_rope, seen):
    scores = einsum32("qhd,khd->hqk", query_nope, key_nope)
    scores = scores + einsum32("qhd,kd->hqk", query_rope, key_rope)
    return jnp.where(seen[None], scores * (NOPE + ROPE) ** (-0.5), NEGATIVE)


def attend_forward(query_nope, query_rope, key_nope, key_rope, values, seen):
    scores = causal_scores(query_nope, query_rope, key_nope, key_rope, seen)
    logsum = jax.nn.logsumexp(scores, axis=-1)
    probs = jnp.exp(scores - logsum[..., None]).astype(jnp.bfloat16)
    return (einsum32("hqk,khd->qhd", probs, values).astype(jnp.bfloat16), logsum)


def attend_backward(
    query_nope, query_rope, key_nope, key_rope, values, mixed, mixed_grad, logsum, seen
):
    scores = causal_scores(query_nope, query_rope, key_nope, key_rope, seen)
    probs_full = jnp.exp(scores - logsum[..., None])
    probs = probs_full.astype(jnp.bfloat16)
    values_grad = einsum32("hqk,qhd->khd", probs, mixed_grad)
    probs_grad = einsum32("qhd,khd->hqk", mixed_grad, values)
    delta = einsum32("qhd,qhd->hq", mixed_grad, mixed)
    score_grad = (probs_full * (probs_grad - delta[..., None]) * (NOPE + ROPE) ** (-0.5)).astype(
        jnp.bfloat16
    )
    query_nope_grad = einsum32("hqk,khd->qhd", score_grad, key_nope)
    query_rope_grad = einsum32("hqk,kd->qhd", score_grad, key_rope)
    key_nope_grad = einsum32("hqk,qhd->khd", score_grad, query_nope)
    key_rope_grad = einsum32("hqk,qhd->kd", score_grad, query_rope)
    return (query_nope_grad, query_rope_grad, key_nope_grad, key_rope_grad, values_grad)


def regroup(blocks, count):
    if blocks.shape[0] == count:
        return blocks
    values = jnp.moveaxis(blocks, 0, 1).reshape(blocks.shape[1], count, -1)
    return jnp.moveaxis(values, 1, 0)


def lane_count(blocks):
    return min(blocks.shape[0], blocks.shape[0] * blocks.shape[2] // LANES)


def dot_of(left, right, dims):
    return lax.dot_general(left, right, ((dims[:1], dims[1:]), ((), ())), preferred_element_type=jnp.float32)


def swiglu_parts(first, second, grad):
    sigma = 1.0 / (1.0 + jnp.exp(-first))
    gated = first * sigma
    return (gated * second, grad * second * (sigma * (1.0 + first * (1.0 - sigma))), grad * gated)


def call_kernel(body, outs, scratch, *arguments):
    return pl.pallas_call(
        body,
        out_shape=[jax.ShapeDtypeStruct(shape, dtype) for shape, dtype in outs],
        scratch_shapes=[pltpu.VMEM(shape, dtype) for shape, dtype in scratch],
    )(*arguments)


def shared_experts(hidden, grad, first, second, units):
    narrow = jnp.bfloat16
    rows, width = hidden.shape
    given = first.shape[0]
    first, second = [regroup(blocks, lane_count(blocks)) for blocks in (first, second)]
    count, _, part = first.shape
    half = units // 2

    def body(x_ref, g_ref, first_ref, second_ref, out_ref, back_ref, dfirst_ref, dsecond_ref,
             gate_ref, up_ref, down_ref):
        for j in range(count):
            lanes = slice(j * part, (j + 1) * part)
            gate_ref[:, lanes] = first_ref[j, :units]
            up_ref[:, lanes] = second_ref[j, :units]
            down_ref[:half, lanes] = first_ref[j, units:]
            down_ref[half:, lanes] = second_ref[j, units:]
        a = dot_of(x_ref[...], gate_ref[...], (1, 1))
        b = dot_of(x_ref[...], up_ref[...], (1, 1))
        u = dot_of(g_ref[...], down_ref[...], (1, 1))
        h, da, db = [v.astype(narrow) for v in swiglu_parts(a, b, u)]
        out_ref[...] = dot_of(h, down_ref[...], (1, 0)).astype(narrow)
        back_ref[...] = dot_of(da, gate_ref[...], (1, 0)) + dot_of(db, up_ref[...], (1, 0))
        dgate = dot_of(da, x_ref[...], (0, 0)).astype(narrow)
        dup = dot_of(db, x_ref[...], (0, 0)).astype(narrow)
        ddown = dot_of(h, g_ref[...], (0, 0)).astype(narrow)
        for j in range(count):
            lanes = slice(j * part, (j + 1) * part)
            dfirst_ref[j, :units] = dgate[:, lanes]
            dsecond_ref[j, :units] = dup[:, lanes]
            dfirst_ref[j, units:] = ddown[:half, lanes]
            dsecond_ref[j, units:] = ddown[half:, lanes]

    wide_scratch = ((units, width), narrow)
    out, back, dfirst, dsecond = call_kernel(
        body,
        [((rows, width), narrow), ((rows, width), jnp.float32), (first.shape, narrow), (second.shape, narrow)],
        [wide_scratch] * 3,
        hidden, grad, first, second,
    )
    return out, back, regroup(dfirst, given), regroup(dsecond, given)


def load_slab(slab_ref, wide_ref, place, units):
    part = slab_ref.shape[2]
    for j in range(slab_ref.shape[0]):
        wide_ref[:, j * part : (j + 1) * part] = slab_ref[j, place * units : (place + 1) * units]


def owned_first(rows, grads, slabs):
    narrow = jnp.bfloat16
    slots, width = grads.shape
    units = slabs.shape[1] // 3
    slabs = regroup(slabs, lane_count(slabs))

    def body(x_ref, g_ref, slab_ref, back_ref, da_ref, db_ref, scaled_ref, gate_ref, up_ref, down_ref):
        load_slab(slab_ref, gate_ref, 0, units)
        load_slab(slab_ref, up_ref, 1, units)
        load_slab(slab_ref, down_ref, 2, units)
        x = x_ref[:, :width]
        extra = x_ref[:, width:].astype(jnp.float32)
        weight = extra[:, 0:1] + extra[:, 1:2]
        a = dot_of(x, gate_ref[...], (1, 1))
        b = dot_of(x, up_ref[...], (1, 1))
        u = dot_of(g_ref[...], down_ref[...], (1, 1))
        h, da, db = swiglu_parts(a, b, u)
        h = h.astype(narrow).astype(jnp.float32)
        slot = jnp.sum(u * h, axis=1, keepdims=True)
        da = (weight * da).astype(narrow)
        db = (weight * db).astype(narrow)
        da_ref[...] = da
        db_ref[...] = db
        scaled_ref[...] = (weight * h).astype(narrow)
        back_ref[:, :width] = (
            dot_of(da, gate_ref[...], (1, 0)) + dot_of(db, up_ref[...], (1, 0))
        ).astype(narrow)
        lane = lax.broadcasted_iota(jnp.int32, (slots, LANES), 1)
        high = slot.astype(narrow).astype(jnp.float32)
        column = jnp.where(lane == 0, high, jnp.where(lane == 1, slot - high, 0.0))
        back_ref[:, width:] = column.astype(narrow)

    inner = ((slots, units), narrow)
    return call_kernel(
        body, [(rows.shape, narrow), inner, inner, inner], [((units, width), narrow)] * 3,
        rows, grads, slabs,
    )


def owned_second(rows, grads, slabs, da, db, scaled):
    narrow = jnp.bfloat16
    slots, width = grads.shape
    units = slabs.shape[1] // 3
    given = slabs.shape[0]
    slabs = regroup(slabs, lane_count(slabs))

    def body(x_ref, g_ref, slab_ref, da_ref, db_ref, scaled_ref, out_ref, term_ref, down_ref):
        part = slab_ref.shape[2]
        load_slab(slab_ref, down_ref, 2, units)
        out_ref[...] = dot_of(scaled_ref[...], down_ref[...], (1, 0)).astype(narrow)
        x = x_ref[:, :width]
        for place, value in enumerate(
            (dot_of(da_ref[...], x, (0, 0)), dot_of(db_ref[...], x, (0, 0)),
             dot_of(scaled_ref[...], g_ref[...], (0, 0)))
        ):
            for j in range(slab_ref.shape[0]):
                term_ref[j, place * units : (place + 1) * units] = value[
                    :, j * part : (j + 1) * part
                ].astype(narrow)

    out, terms = call_kernel(
        body, [((slots, width), narrow), (slabs.shape, narrow)], [((units, width), narrow)],
        rows, grads, slabs, da, db, scaled,
    )
    return out, regroup(terms, given)


def block(
    block_in,
    attn_norm_gain,
    query_weight,
    kv_down_weight,
    latent_gain,
    kv_up_weight,
    output_weight,
    ffn_norm_gain,
    router_weight,
    expert_ids,
    shared_gate_weight,
    shared_up_weight,
    shared_down_weight,
    expert_gate_weight,
    expert_up_weight,
    expert_down_weight,
    out_grad,
):
    wide = jnp.float32
    narrow = jnp.bfloat16
    own_rows = block_in.shape[0]
    width = block_in.shape[1]
    dp_count = lax.axis_size("dp")
    tensor_count = lax.axis_size("tensor")
    tensor_index = lax.axis_index("tensor")
    group = own_rows * tensor_count
    owner_count = dp_count // ACTIVE
    slot_piece = CAP // owner_count
    slots = ACTIVE * CAP
    both = ("dp", "tensor")
    first_order, second_order = dp_orders()

    all_in = gather_tensor(block_in)
    small = jnp.concatenate([kv_down_weight, router_weight], axis=1)
    small = exchange(jnp.broadcast_to(small[None], (tensor_count,) + small.shape), "tensor")
    gains = jnp.concatenate([attn_norm_gain, ffn_norm_gain, latent_gain])
    gains = exchange(
        jnp.broadcast_to(gains[None], (dp_count * tensor_count, gains.shape[0])), both
    ).astype(wide)
    split_one = attn_norm_gain.shape[0]
    gain_one = gains[:, :split_one].reshape(-1)
    gain_two = gains[:, split_one : 2 * split_one].reshape(-1)
    gain_lat = gains[:, 2 * split_one :].reshape(-1)

    query_full = gather_dp(query_weight, first_order).reshape(width, -1)
    small = gather_dp(small, second_order).reshape(width, -1)
    kv_up_full = gather_dp(kv_up_weight, second_order).reshape(LATENT, -1)
    kv_down = small[:, : LATENT + ROPE]
    router = small[:, LATENT + ROPE :]
    output_full = wide_rows(gather_dp(output_weight, second_order))
    grad_all = gather_tensor(out_grad, 1)

    shared_units = shared_down_weight.shape[0]
    half = shared_units // 2
    shared = (
        gather_dp(jnp.concatenate([shared_gate_weight.T, shared_down_weight[:half]]), first_order),
        gather_dp(jnp.concatenate([shared_up_weight.T, shared_down_weight[half:]]), second_order),
    )
    units = expert_down_weight.shape[1]
    slabs = jnp.concatenate(
        [
            jnp.swapaxes(expert_gate_weight, 1, 2),
            jnp.swapaxes(expert_up_weight, 1, 2),
            expert_down_weight,
        ],
        axis=1,
    )
    slabs = exchange(jnp.repeat(slabs, owner_count, axis=0), "dp")

    heads = query_full.shape[1] // (NOPE + ROPE)
    residual_all = all_in.astype(wide)
    scale_all = rms_scale(residual_all)
    hidden_one = (residual_all * scale_all * gain_one).astype(narrow)
    latent_in = matmul(hidden_one, kv_down).astype(narrow)
    compressed = latent_in[:, :LATENT].astype(wide)
    scale_lat = rms_scale(compressed)
    normed_lat = compressed * scale_lat
    latent = (normed_lat * gain_lat).astype(narrow)
    place = (jnp.arange(group) + tensor_index * own_rows) % group
    position = (place % SEQ).astype(wide)
    sequence = place // SEQ
    seen = (place[:, None] >= place[None, :]) & (sequence[:, None] == sequence[None, :])
    cosine, sine = rope_tables(position)
    key_rope = rotate(latent_in[:, LATENT:].astype(wide), cosine, sine).astype(narrow)
    query = matmul(hidden_one, query_full).reshape(group, heads, NOPE + ROPE)
    query_nope = query[..., :NOPE].astype(narrow)
    query_rope = rotate(query[..., NOPE:], cosine[:, None, :], sine[:, None, :]).astype(narrow)
    keyvalue = matmul(latent, kv_up_full).astype(narrow).reshape(group, heads, NOPE + VDIM)
    key_nope = keyvalue[..., :NOPE]
    values = keyvalue[..., NOPE:]
    mixed, logsum = attend_forward(query_nope, query_rope, key_nope, key_rope, values, seen)
    mixed_flat = mixed.reshape(group, heads * VDIM)
    attn_share = matmul(mixed_flat, output_full)
    attn_own = scatter_tensor(attn_share)

    residual_in = block_in.astype(wide)
    after_attn = residual_in + attn_own
    scale_two = rms_scale(after_attn)
    normed_two = after_attn * scale_two
    hidden_two_own = (normed_two * gain_two).astype(narrow)
    hidden_two = gather_tensor(hidden_two_own)

    ids = jnp.concatenate([expert_ids, expert_ids], axis=0)
    ids = lax.dynamic_slice_in_dim(ids, tensor_index * own_rows, group, 0)
    chosen = jnp.any(ids[:, :, None] == jnp.arange(ACTIVE, dtype=jnp.int32)[None, None, :], axis=1)
    ranks = jnp.cumsum(chosen.astype(jnp.int32), axis=0) - 1
    places = (ranks[:, :, None] == jnp.arange(CAP, dtype=jnp.int32)[None, None, :]) & chosen[
        :, :, None
    ]
    pick = places.astype(narrow).reshape(group, slots)
    grad_in = left_dot(pick, grad_all).astype(narrow)
    grad_here = exchange(grad_in.reshape(dp_count, slot_piece, width), "dp").reshape(-1, width)
    route_prob = jax.nn.softmax(matmul(hidden_two, router), axis=-1)
    gate = jnp.where(chosen, route_prob[:, :ACTIVE], 0.0)
    weight = jnp.sum(jnp.where(places, gate[:, :, None], 0.0), axis=0).reshape(slots)
    tokens_in = with_column(left_dot(pick, hidden_two).astype(narrow), weight)
    rows_here = exchange(tokens_in.reshape(dp_count, slot_piece, -1), "dp")
    rows_here = rows_here.reshape(slots, -1)

    moe_share, hidden_two_share, shared_first, shared_second = shared_experts(
            hidden_two, grad_all, shared[0], shared[1], shared_units
    )

    owned_back, owned_a_grad, owned_b_grad, owned_scaled = owned_first(rows_here, grad_here, slabs)
    back_flat = exchange(owned_back.reshape(dp_count, slot_piece, -1), "dp")
    back_flat = back_flat.reshape(slots, -1)
    per_slot = column_of(back_flat, width).reshape(1, ACTIVE, CAP)
    back_flat = back_flat[:, :width]
    owned_out, terms = owned_second(
            rows_here, grad_here, slabs, owned_a_grad, owned_b_grad, owned_scaled
    )
    routed_flat = exchange(owned_out.reshape(dp_count, slot_piece, width), "dp").reshape(-1, width)
    terms = exchange(terms, "dp")
    terms = terms.reshape((ACTIVE, owner_count) + terms.shape[1:])

    def summed(first):
        return jnp.sum(terms[:, :, first : first + units].astype(wide), axis=1)

    expert_gate_grad = jnp.swapaxes(summed(0), 1, 2)
    expert_up_wgrad = jnp.swapaxes(summed(units), 1, 2)
    expert_down_grad = summed(2 * units)

    hidden_two_share = hidden_two_share + matmul(pick, back_flat)
    gate_share = jnp.sum(jnp.where(places, per_slot, 0.0), axis=-1)
    hidden_two_share = jnp.concatenate(
            [hidden_two_share, jnp.pad(gate_share, ((0, 0), (0, LANES - ACTIVE)))], axis=1
    )
    hidden_two_grad = scatter_tensor(hidden_two_share)
    gate_grad = hidden_two_grad[:, width : width + ACTIVE]
    hidden_two_grad = hidden_two_grad[:, :width]
    prob_own = jax.nn.softmax(matmul(hidden_two_own, router), axis=-1)
    prob_grad = jnp.concatenate(
        [gate_grad, jnp.zeros((own_rows, prob_own.shape[1] - ACTIVE), wide)], axis=-1
    )
    logit_grad = (
        prob_own * (prob_grad - jnp.sum(prob_own * prob_grad, axis=-1, keepdims=True))
    ).astype(narrow)
    router_grad = left_dot(hidden_two_own, logit_grad)
    hidden_two_grad = hidden_two_grad + right_dot(logit_grad, router)
    gain_two_grad = jnp.sum(hidden_two_grad * normed_two, axis=0)
    after_attn_grad = out_grad.astype(wide) + norm_back(
            hidden_two_grad * gain_two, normed_two, scale_two
    )
    residual_low = gather_tensor(after_attn_grad.astype(narrow))
    moe_share = moe_share.astype(wide) + matmul(pick, routed_flat)
    moe_own = scatter_tensor(moe_share, 1)
    block_out = (after_attn + moe_own).astype(narrow)

    mixed_grad = right_dot(residual_low, output_full).astype(narrow).reshape(group, heads, VDIM)
    output_grad = left_dot(mixed_flat, residual_low)
    query_nope_grad, query_rope_grad, key_nope_grad, key_rope_grad, values_grad = attend_backward(
            query_nope, query_rope, key_nope, key_rope, values, mixed, mixed_grad, logsum, seen
    )
    keyvalue_grad = (
        jnp.concatenate([key_nope_grad, values_grad], axis=-1)
        .astype(narrow)
        .reshape(group, heads * (NOPE + VDIM))
    )
    latent_grad = right_dot(keyvalue_grad, kv_up_full)
    gain_lat_grad = jnp.sum(latent_grad * normed_lat, axis=0)
    compressed_grad = norm_back(latent_grad * gain_lat, normed_lat, scale_lat)
    key_rope_back = unrotate(key_rope_grad, cosine, sine)
    latent_in_share = jnp.concatenate([compressed_grad, key_rope_back], axis=-1)
    latent_in_low = latent_in_share.astype(narrow)
    query_rope_back = unrotate(query_rope_grad, cosine[:, None, :], sine[:, None, :])
    query_grad = (
        jnp.concatenate([query_nope_grad, query_rope_back], axis=-1)
        .astype(narrow)
        .reshape(group, heads * (NOPE + ROPE))
    )
    hidden_one_share = right_dot(query_grad, query_full) + right_dot(latent_in_low, kv_down)
    hidden_one_grad = scatter_tensor(hidden_one_share)
    query_wgrad = left_dot(hidden_one, query_grad)
    kv_up_grad = left_dot(latent, keyvalue_grad)
    scale_one = rms_scale(residual_in)
    normed_one = residual_in * scale_one
    input_grad = after_attn_grad + norm_back(hidden_one_grad * gain_one, normed_one, scale_one)

    tall = jnp.concatenate(
        [left_dot(hidden_one, latent_in_low), router_grad], axis=1
    ).astype(narrow)
    tall = tall.reshape(dp_count, -1, tall.shape[1])
    shared_first = scatter_dp(shared_first, first_order)
    shared_second = scatter_dp(shared_second, second_order)
    shared_grads = (
        shared_first[:shared_units].T,
        shared_second[:shared_units].T,
        jnp.concatenate([shared_first[shared_units:], shared_second[shared_units:]]),
    )
    output_grad = scatter_dp(tall_blocks(output_grad), second_order)
    query_wgrad = query_wgrad.astype(narrow).reshape(dp_count, -1, query_wgrad.shape[1])
    query_wgrad = scatter_dp(query_wgrad, first_order)
    kv_up_grad = kv_up_grad.astype(narrow).reshape(dp_count, -1, kv_up_grad.shape[1])
    kv_up_grad = scatter_dp(kv_up_grad, second_order)
    tall = scatter_dp(tall, second_order).astype(narrow)
    tall = exchange(tall.reshape(tensor_count, -1, tall.shape[1]), "tensor")
    tall = jnp.sum(tall.astype(wide), axis=0)
    kv_down_grad = tall[:, : LATENT + ROPE]
    router_grad = tall[:, LATENT + ROPE :]
    gain_one_grad = jnp.sum(hidden_one_share * (residual_all * scale_all), axis=0)
    devices = dp_count * tensor_count
    gain_grads = jnp.concatenate(
        [
            gain_one_grad.reshape(devices, -1),
            gain_two_grad.reshape(devices, -1),
            gain_lat_grad.reshape(devices, -1),
        ],
        axis=1,
    )
    gain_grads = jnp.sum(exchange(gain_grads, both), axis=0)
    return (
        block_out,
        input_grad,
        gain_grads[:split_one],
        query_wgrad,
        kv_down_grad,
        gain_grads[2 * split_one :],
        kv_up_grad,
        output_grad,
        gain_grads[split_one : 2 * split_one],
        router_grad,
        shared_grads[0],
        shared_grads[1],
        shared_grads[2],
        expert_gate_grad,
        expert_up_wgrad,
        expert_down_grad,
    )


def solution(mesh):
    in_specs = (
        P(("dp", "tensor"), None),
        P(("dp", "tensor")),
        P("dp", "tensor"),
        P(("dp", "tensor"), None),
        P(("dp", "tensor")),
        P("dp", "tensor"),
        P("tensor", "dp"),
        P(("dp", "tensor")),
        P(("dp", "tensor"), None),
        P("dp", None),
        P("dp", "tensor"),
        P("dp", "tensor"),
        P("tensor", "dp"),
        P(None, "dp", "tensor"),
        P(None, "dp", "tensor"),
        P(None, "tensor", "dp"),
        P(("dp", "tensor"), None),
    )
    out_specs = (
        P(("dp", "tensor"), None),
        P(("dp", "tensor"), None),
        P(("dp", "tensor")),
        P("dp", "tensor"),
        P(("dp", "tensor"), None),
        P(("dp", "tensor")),
        P("dp", "tensor"),
        P("tensor", "dp"),
        P(("dp", "tensor")),
        P(("dp", "tensor"), None),
        P("dp", "tensor"),
        P("dp", "tensor"),
        P("tensor", "dp"),
        P(None, "dp", "tensor"),
        P(None, "dp", "tensor"),
        P(None, "tensor", "dp"),
    )
    return jax.shard_map(block, mesh=mesh, in_specs=in_specs, out_specs=out_specs, check_vma=False)
```

time: 928 us -> 859 us (0.926)
  waiting for transfers between devices: 314 us -> 419 us
  local copies, waits for them, and re-layouts: 170 us -> 85.7 us
  matrix products: 130 us -> 68.2 us
  Pallas kernels: 0 us -> 48.5 us
  starting transfers between devices: 174 us -> 126 us
  other arithmetic: 126 us -> 98 us
    ppermute x39 -> x36, waiting for transfers between devices: 138 us -> 215 us  [swap_dp(): return lax.ppermute(values, 'dp', [(i, i ^ mask) for i in range(count)])]
    ppermute x48 -> x42, waiting for transfers between devices: 123 us -> 172 us  [send_tensor(): lax.ppermute(values, 'tensor', [(i, (i + step) % count) for i in range(co...]
    pallas_call x0 -> x3, Pallas kernels: none -> 48.5 us  [call_kernel(): pl.pallas_call(body, out_shape=[jax.ShapeDtypeStruct(shape, dtype) for sh...]
    ppermute x48 -> x42, starting transfers between devices: 73.3 us -> 47 us  [send_tensor(): lax.ppermute(values, 'tensor', [(i, (i + step) % count) for i in range(co...]
    dot_general x14 -> x8, matrix products: 49.9 us -> 26.1 us  [matmul(): return jnp.dot(left, right, preferred_element_type=jnp.float32)]
    dot_general x11 -> x5, matrix products: 34.8 us -> 12.8 us  [right_dot(): lax.dot_general(left, right, (((left.ndim - 1,), (1,)), ((), ())), prefer...]
    convert_element_type x16 -> x12, local copies, waits for them, and re-layouts: 27.2 us -> 6.17 us  [scatter_dp(): lax.dynamic_slice_in_dim(current, 1 - high, 1, axis).astype(jnp.bfloat16)]
    all_to_all x15 -> x10, waiting for transfers between devices: 52.3 us -> 31.6 us  [exchange(): return lax.all_to_all(values, axes, split_axis=0, concat_axis=0, tiled=True)]
  transfers between devices with their start and end apart: 102 -> 88, of which waited for: 47 -> 44; matrix products, arithmetic and copies ran while one was open for 42% -> 27% of each run, Pallas kernels for 0% -> 6%
where the time goes in v2:
time: 859 us; the launch traced here: 849 us
  waiting for transfers between devices  419 us (49%)
  starting transfers between devices  126 us (15%)
  other arithmetic  98 us (11%)
  local copies, waits for them, and re-layouts  85.7 us (10%)
  matrix products  68.2 us (8%)
  Pallas kernels  48.5 us (6%)
    ppermute x36, waiting for transfers between devices, swap_dp(): return lax.ppermute(values, 'dp', [(i, i ^ mask) for i in range(count)])  215 us
    ppermute x42, waiting for transfers between devices, send_tensor(): lax.ppermute(values, 'tensor', [(i, (i + step) % count) for i in range(co...  172 us
    all_to_all x10, starting transfers between devices, exchange(): return lax.all_to_all(values, axes, split_axis=0, concat_axis=0, tiled=True)  48.9 us
    pallas_call x3, Pallas kernels, call_kernel(): pl.pallas_call(body, out_shape=[jax.ShapeDtypeStruct(shape, dtype) for sh...  48.5 us
    ppermute x42, starting transfers between devices, send_tensor(): lax.ppermute(values, 'tensor', [(i, (i + step) % count) for i in range(co...  47 us
    unnamed x293, local copies, waits for them, and re-layouts  33.9 us
    all_to_all x10, waiting for transfers between devices, exchange(): return lax.all_to_all(values, axes, split_axis=0, concat_axis=0, tiled=True)  31.6 us
    ppermute x36, starting transfers between devices, swap_dp(): return lax.ppermute(values, 'dp', [(i, i ^ mask) for i in range(count)])  30.5 us
  transfers between devices with their start and end apart: 88, of which 44 were waited for; matrix products, arithmetic and copies ran while one was open for 27% of the time, Pallas kernels for 6%

profile of v2, /device:TPU:0, one launch (start us, length us, event | category | flops | bytes accessed | tf_op | source)
XLA Modules:
  0.0 849.0 jit_solution(3241880751860036816)
XLA Ops:
  53.1 8.6 %collective-permute-done.10 = bf16[2,1,1,64,1024]{4,3,2,1,0:T(8,128)(2,1)S(1)} collective-permute-done((bf16[2,1,1,64,1024]{4,3,2,1,0:T(8,128)(2,1)S(1)}, bf16[2,1,1,64,1024]{4,3,2,1,0:T(8,128)(2,1)S(1)}, u32[]{:S(2)}, u32[]{:S(2)}) %collective-permute-start.10) | collective-permute-done | bytes 262176 | tf_op jit(solution)/shard_map/ppermute | solution.py:129
  101.2 52.0 %collective-permute-done.6 = bf16[1,1,1,4,64,640]{5,4,3,2,1,0:T(8,128)(2,1)S(1)} collective-permute-done((bf16[1,1,1,4,64,640]{5,4,3,2,1,0:T(8,128)(2,1)}, bf16[1,1,1,4,64,640]{5,4,3,2,1,0:T(8,128)(2,1)S(1)}, u32[]{:S(2)}, u32[]{:S(2)}) %collective-permute-start.6) | collective-permute-done | bytes 327712 | tf_op jit(solution)/shard_map/ppermute | solution.py:129
  163.6 27.0 %collective-permute-done.7 = bf16[2,1,1,4,64,640]{5,4,3,2,1,0:T(8,128)(2,1)S(1)} collective-permute-done((bf16[2,1,1,4,64,640]{5,4,3,2,1,0:T(8,128)(2,1)S(1)}, bf16[2,1,1,4,64,640]{5,4,3,2,1,0:T(8,128)(2,1)S(1)}, u32[]{:S(2)}, u32[]{:S(2)}) %collective-permute-start.7) | collective-permute-done | bytes 655392 | tf_op jit(solution)/shard_map/ppermute | solution.py:129
  234.3 8.9 %collective-permute-done.18 = bf16[64,2048]{1,0:T(8,128)(2,1)S(1)} collective-permute-done((bf16[64,2048]{1,0:T(8,128)(2,1)S(1)}, bf16[64,2048]{1,0:T(8,128)(2,1)S(1)}, u32[]{:S(2)}, u32[]{:S(2)}) %collective-permute-start.18) | collective-permute-done | bytes 262176 | tf_op jit(solution)/shard_map/ppermute | solution.py:75
  249.7 9.2 %collective-permute-done.19 = bf16[64,2048]{1,0:T(8,128)(2,1)S(1)} collective-permute-done((bf16[64,2048]{1,0:T(8,128)(2,1)S(1)}, bf16[64,2048]{1,0:T(8,128)(2,1)S(1)}, u32[]{:S(2)}, u32[]{:S(2)}) %collective-permute-start.19) | collective-permute-done | bytes 262176 | tf_op jit(solution)/shard_map/ppermute | solution.py:75
  263.3 10.6 %collective-permute-done.20 = bf16[64,2048]{1,0:T(8,128)(2,1)S(1)} collective-permute-done((bf16[64,2048]{1,0:T(8,128)(2,1)S(1)}, bf16[64,2048]{1,0:T(8,128)(2,1)S(1)}, u32[]{:S(2)}, u32[]{:S(2)}) %collective-permute-start.20) | collective-permute-done | bytes 262176 | tf_op jit(solution)/shard_map/ppermute | solution.py:75
  309.5 12.4 %all-to-all-start.3 = ((bf16[8,96,2048]{2,1,0:T(8,128)(2,1)}), bf16[8,96,2048]{2,1,0:T(8,128)(2,1)S(1)}, u32[]{:S(2)}, u32[]{:S(2)}) async-start(bf16[8,96,2048]{2,1,0:T(8,128)(2,1)} %bitcast.220), calls=%async_computation.3 | async-start | bytes 6291456 | tf_op jit(solution)/shard_map/all_to_all | solution.py:118
  325.2 22.5 %shard_map.288 = (bf16[512,2048]{1,0:T(8,128)(2,1)}, f32[512,2048]{1,0:T(8,128)}, bf16[8,1056,256]{2,1,0:T(8,128)(2,1)}, bf16[8,1056,256]{2,1,0:T(8,128)(2,1)}) custom-call(bf16[512,2048]{1,0:T(8,128)(2,1)} %constant_dynamic-update-slice_fusion.7.x_ref, bf16[512,2048]{1,0:T(8,128)(2,1)} %copy-done.55, bf16[8,1056,256]{2,1,0:T(8,128)(2,1)} %bitcast.196, ...), custom_call_target="tpu_custom_call" | custom-call | tf_op jit(solution)/shard_map/pallas_call | solution.py:229
  379.3 26.6 %all-to-all-done.2 = bf16[8,96,2176]{2,1,0:T(8,128)(2,1)S(1)} async-done(((bf16[8,96,2176]{2,1,0:T(8,128)(2,1)}), bf16[8,96,2176]{2,1,0:T(8,128)(2,1)S(1)}, u32[]{:S(2)}, u32[]{:S(2)}) %all-to-all-start.2) | async-done | bytes 3342368 | tf_op jit(solution)/shard_map/all_to_all | solution.py:118
  407.5 14.3 %shard_map.289 = (bf16[768,2176]{1,0:T(8,128)(2,1)}, bf16[768,352]{1,0:T(8,128)(2,1)}, bf16[768,352]{1,0:T(8,128)(2,1)}, bf16[768,352]{1,0:T(8,128)(2,1)}) custom-call(bf16[768,2176]{1,0:T(8,128)(2,1)} %bitcast.188, bf16[768,2048]{1,0:T(8,128)(2,1)} %bitcast.192, bf16[8,1056,256]{2,1,0:T(8,128)(2,1)} %all-to-all-done.4.slab_ref), custom_call_target="tpu_custom_call" | custom-call | tf_op jit(solution)/shard_map/pallas_call | solution.py:229
  421.8 11.7 %shard_map.290 = (bf16[768,2048]{1,0:T(8,128)(2,1)}, bf16[8,1056,256]{2,1,0:T(8,128)(2,1)}) custom-call(bf16[768,2176]{1,0:T(8,128)(2,1)} %bitcast.189, bf16[768,2048]{1,0:T(8,128)(2,1)} %bitcast.193, bf16[8,1056,256]{2,1,0:T(8,128)(2,1)} %all-to-all-done.4.slab_ref, bf16[768,352]{1,0:T(8,128)(2,1)} %get-tuple-element.27.da_ref, ...), custom_call_target="tpu_custom_call" | custom-call | tf_op jit(solution)/shard_map/pallas_call | solution.py:229
  447.0 51.3 %collective-permute-done.76 = bf16[2,1,1,1056,256]{4,3,2,1,0:T(8,128)(2,1)S(1)} collective-permute-done((bf16[2,1,1,1056,256]{4,3,2,1,0:T(8,128)(2,1)S(1)}, bf16[2,1,1,1056,256]{4,3,2,1,0:T(8,128)(2,1)S(1)}, u32[]{:S(2)}, u32[]{:S(2)}) %collective-permute-start.76) | collective-permute-done | bytes 1081376 | tf_op jit(solution)/shard_map/ppermute | solution.py:129
  516.0 41.6 %collective-permute-done.74 = bf16[1,1,1,1056,256]{4,3,2,1,0:T(8,128)(2,1)S(1)} collective-permute-done((bf16[1,1,1,1056,256]{4,3,2,1,0:T(8,128)(2,1)S(1)}, bf16[1,1,1,1056,256]{4,3,2,1,0:T(8,128)(2,1)S(1)}, u32[]{:S(2)}, u32[]{:S(2)}) %collective-permute-start.74) | collective-permute-done | bytes 540704 | tf_op jit(solution)/shard_map/ppermute | solution.py:129
  583.7 10.7 %collective-permute-done.42 = bf16[64,2176]{1,0:T(8,128)(2,1)S(1)} collective-permute-done((bf16[64,2176]{1,0:T(8,128)(2,1)S(1)}, bf16[64,2176]{1,0:T(8,128)(2,1)S(1)}, u32[]{:S(2)}, u32[]{:S(2)}) %collective-permute-start.42) | collective-permute-done | bytes 278560 | tf_op jit(solution)/shard_map/ppermute | solution.py:75
  601.6 9.6 %collective-permute-done.43 = bf16[64,2176]{1,0:T(8,128)(2,1)S(1)} collective-permute-done((bf16[64,2176]{1,0:T(8,128)(2,1)S(1)}, bf16[64,2176]{1,0:T(8,128)(2,1)S(1)}, u32[]{:S(2)}, u32[]{:S(2)}) %collective-permute-start.43) | collective-permute-done | bytes 278560 | tf_op jit(solution)/shard_map/ppermute | solution.py:75
  611.3 6.0 collective-permute-done.46
  617.5 11.0 %collective-permute-done.39 = bf16[128,2048]{1,0:T(8,128)(2,1)S(1)} collective-permute-done((bf16[128,2048]{1,0:T(8,128)(2,1)S(1)}, bf16[128,2048]{1,0:T(8,128)(2,1)S(1)}, u32[]{:S(2)}, u32[]{:S(2)}) %collective-permute-start.39) | collective-permute-done | bytes 524320 | tf_op jit(solution)/shard_map/ppermute | solution.py:75
  647.9 6.0 fusion.22
  661.0 10.5 %collective-permute-done.49 = bf16[64,2048]{1,0:T(8,128)(2,1)S(1)} collective-permute-done((bf16[64,2048]{1,0:T(8,128)(2,1)}, bf16[64,2048]{1,0:T(8,128)(2,1)S(1)}, u32[]{:S(2)}, u32[]{:S(2)}) %collective-permute-start.49) | collective-permute-done | bytes 262176 | tf_op jit(solution)/shard_map/ppermute | solution.py:75
  671.5 7.0 collective-permute-done.50
  769.7 8.4 collective-permute-done.55
  784.8 8.4 collective-permute-done.56
  808.4 9.6 %collective-permute-done.70 = bf16[2,1,1,512,256]{4,3,2,1,0:T(8,128)(2,1)S(1)} collective-permute-done((bf16[2,1,1,512,256]{4,3,2,1,0:T(8,128)(2,1)S(1)}, bf16[2,1,1,512,256]{4,3,2,1,0:T(8,128)(2,1)S(1)}, u32[]{:S(2)}, u32[]{:S(2)}) %collective-permute-start.70) | collective-permute-done | bytes 524320 | tf_op jit(solution)/shard_map/ppermute | solution.py:129
  819.5 8.8 %collective-permute-done.64 = bf16[2,1,1,256,640]{4,3,2,1,0:T(8,128)(2,1)S(1)} collective-permute-done((bf16[2,1,1,256,640]{4,3,2,1,0:T(8,128)(2,1)S(1)}, bf16[2,1,1,256,640]{4,3,2,1,0:T(8,128)(2,1)S(1)}, u32[]{:S(2)}, u32[]{:S(2)}) %collective-permute-start.64) | collective-permute-done | bytes 655392 | tf_op jit(solution)/shard_map/ppermute | solution.py:129
  (667 shorter events, 452.9 us)
Async XLA Ops:
  7.7 42.9 %collective-permute-start.1 = (bf16[64,2048]{1,0:T(8,128)(2,1)}, bf16[64,2048]{1,0:T(8,128)(2,1)}, u32[]{:S(2)}, u32[]{:S(2)}) collective-permute-start(bf16[64,2048]{1,0:T(8,128)(2,1)} %get-tuple-element.124), channel_id=1, source_target_pairs={{0,3},{1,0},{2,1},{3,2},{4,7},{5,4},{6,5},{7,6},{8,11},{9,8},{10,9... | collective-permute-start | bytes 786440 | tf_op jit(solution)/shard_map/ppermute | solution.py:75
  13.5 49.8 %collective-permute-start.12 = (bf16[1,1,1,256,768]{4,3,2,1,0:T(8,128)(2,1)}, bf16[1,1,1,256,768]{4,3,2,1,0:T(8,128)(2,1)}, u32[]{:S(2)}, u32[]{:S(2)}) collective-permute-start(bf16[1,1,1,256,768]{4,3,2,1,0:T(8,128)(2,1)} %bitcast.242), channel_id=1, source_target_pairs={{0,8},{4,12},{8,0},{12,4},{16,24},{20,28},{24,16},{28,20},{1,9},{5... | collective-permute-start | bytes 1179656 | tf_op jit(solution)/shard_map/ppermute | solution.py:129
  16.7 59.6 %collective-permute-start.30 = (bf16[128,2048]{1,0:T(8,128)(2,1)}, bf16[128,2048]{1,0:T(8,128)(2,1)}, u32[]{:S(2)}, u32[]{:S(2)}) collective-permute-start(bf16[128,2048]{1,0:T(8,128)(2,1)} %param.33), channel_id=1, source_target_pairs={{0,3},{1,0},{2,1},{3,2},{4,7},{5,4},{6,5},{7,6},{8,11},{9,8},{10,9... | collective-permute-start | bytes 1572872 | tf_op jit(solution)/shard_map/ppermute | solution.py:75
  35.0 54.4 %all-to-all-start.1 = ((bf16[4,64,640]{2,1,0:T(8,128)(2,1)}), bf16[4,64,640]{2,1,0:T(8,128)(2,1)}, u32[]{:S(2)}, u32[]{:S(2)}) async-start(bf16[4,64,640]{2,1,0:T(8,128)(2,1)} %broadcast_in_dim.43), calls=%async_computation.1 | async-start | bytes 655360 | tf_op jit(solution)/shard_map/all_to_all | solution.py:118
  76.4 79.4 %collective-permute-start.11 = (bf16[2,2,1,64,1024]{4,3,2,1,0:T(8,128)(2,1)}, bf16[2,2,1,64,1024]{4,3,2,1,0:T(8,128)(2,1)}, u32[]{:S(2)}, u32[]{:S(2)}) collective-permute-start(bf16[2,2,1,64,1024]{4,3,2,1,0:T(8,128)(2,1)} %pad_maximum_fusion.18), channel_id=1, source_target_pairs={{0,4},{4,0},{8,12},{12,8},{16,20},{20,16},{24,28},{28,24},{1,5},{5... | collective-permute-start | bytes 1572872 | tf_op jit(solution)/shard_map/ppermute | solution.py:129
  79.6 79.3 %collective-permute-start.13 = (bf16[1,2,1,256,768]{4,3,2,1,0:T(8,128)(2,1)}, bf16[1,2,1,256,768]{4,3,2,1,0:T(8,128)(2,1)}, u32[]{:S(2)}, u32[]{:S(2)}) collective-permute-start(bf16[1,2,1,256,768]{4,3,2,1,0:T(8,128)(2,1)} %pad_maximum_fusion.14), channel_id=1, source_target_pairs={{0,16},{4,20},{8,24},{12,28},{16,0},{20,4},{24,8},{28,12},{1,17},{... | collective-permute-start | bytes 2359304 | tf_op jit(solution)/shard_map/ppermute | solution.py:129
  89.5 220.0 %all-to-all-start.4 = ((bf16[8,1056,256]{2,1,0:T(8,128)(2,1)}), bf16[8,1056,256]{2,1,0:T(8,128)(2,1)}, u32[]{:S(2)}, u32[]{:S(2)}) async-start(bf16[8,1056,256]{2,1,0:T(8,128)(2,1)} %pad_maximum_fusion.2), calls=%async_computation.4 | async-start | bytes 8650752 | tf_op jit(solution)/shard_map/all_to_all | solution.py:118
  94.1 59.2 %collective-permute-start.6 = (bf16[1,1,1,4,64,640]{5,4,3,2,1,0:T(8,128)(2,1)}, bf16[1,1,1,4,64,640]{5,4,3,2,1,0:T(8,128)(2,1)S(1)}, u32[]{:S(2)}, u32[]{:S(2)}) collective-permute-start(bf16[1,1,1,4,64,640]{5,4,3,2,1,0:T(8,128)(2,1)} %bitcast.2), channel_id=1, source_target_pairs={{0,16},{4,20},{8,24},{12,28},{16,0},{20,4},{24,8},{28,12},{1,17},{... | collective-permute-start | bytes 983048 | tf_op jit(solution)/shard_map/ppermute | solution.py:129
  97.0 61.2 %collective-permute-start.31 = (bf16[128,2048]{1,0:T(8,128)(2,1)}, bf16[128,2048]{1,0:T(8,128)(2,1)S(1)}, u32[]{:S(2)}, u32[]{:S(2)}) collective-permute-start(bf16[128,2048]{1,0:T(8,128)(2,1)} %collective-permute-done.30), channel_id=1, source_target_pairs={{0,3},{1,0},{2,1},{3,2},{4,7},{5,4},{6,5},{7,6},{8,11},{9,8},{10,9... | collective-permute-start | bytes 1572872 | tf_op jit(solution)/shard_map/ppermute | solution.py:75
  99.4 97.5 %collective-permute-start.34 = (bf16[1,2,1,1056,256]{4,3,2,1,0:T(8,128)(2,1)S(1)}, bf16[1,2,1,1056,256]{4,3,2,1,0:T(8,128)(2,1)S(1)}, u32[]{:S(2)}, u32[]{:S(2)}) collective-permute-start(bf16[1,2,1,1056,256]{4,3,2,1,0:T(8,128)(2,1)S(1)} %copy-done.84), channel_id=1, source_target_pairs={{0,16},{4,20},{8,24},{12,28},{16,0},{20,4},{24,8},{28,12},{1,17},{... | collective-permute-start | bytes 3244040 | tf_op jit(solution)/shard_map/ppermute | solution.py:129
  153.2 94.9 %collective-permute-start.37 = (bf16[2,1,1,1056,256]{4,3,2,1,0:T(8,128)(2,1)}, bf16[2,1,1,1056,256]{4,3,2,1,0:T(8,128)(2,1)}, u32[]{:S(2)}, u32[]{:S(2)}) collective-permute-start(bf16[2,1,1,1056,256]{4,3,2,1,0:T(8,128)(2,1)} %pad_maximum_fusion.11), channel_id=1, source_target_pairs={{0,8},{4,12},{8,0},{12,4},{16,24},{20,28},{24,16},{28,20},{1,9},{5... | collective-permute-start | bytes 3244040 | tf_op jit(solution)/shard_map/ppermute | solution.py:129
  234.2 46.4 %collective-permute-start.35 = (bf16[2,2,1,1056,256]{4,3,2,1,0:T(8,128)(2,1)S(1)}, bf16[2,2,1,1056,256]{4,3,2,1,0:T(8,128)(2,1)S(1)}, u32[]{:S(2)}, u32[]{:S(2)}) collective-permute-start(bf16[2,2,1,1056,256]{4,3,2,1,0:T(8,128)(2,1)S(1)} %pad_maximum_fusion.5), channel_id=1, source_target_pairs={{0,4},{4,0},{8,12},{12,8},{16,20},{20,16},{24,28},{28,24},{1,5},{5... | collective-permute-start | bytes 6488072 | tf_op jit(solution)/shard_map/ppermute | solution.py:129
  309.5 50.9 %all-to-all-start.3 = ((bf16[8,96,2048]{2,1,0:T(8,128)(2,1)}), bf16[8,96,2048]{2,1,0:T(8,128)(2,1)S(1)}, u32[]{:S(2)}, u32[]{:S(2)}) async-start(bf16[8,96,2048]{2,1,0:T(8,128)(2,1)} %bitcast.220), calls=%async_computation.3 | async-start | bytes 6291456 | tf_op jit(solution)/shard_map/all_to_all | solution.py:118
  362.0 43.8 %all-to-all-start.2 = ((bf16[8,96,2176]{2,1,0:T(8,128)(2,1)}), bf16[8,96,2176]{2,1,0:T(8,128)(2,1)S(1)}, u32[]{:S(2)}, u32[]{:S(2)}) async-start(bf16[8,96,2176]{2,1,0:T(8,128)(2,1)} %bitcast.198), calls=%async_computation.2 | async-start | bytes 6684672 | tf_op jit(solution)/shard_map/all_to_all | solution.py:118
  368.9 73.1 %collective-permute-start.72 = (bf16[2,2,1,1056,256]{4,3,2,1,0:T(8,128)(2,1)}, bf16[2,2,1,1056,256]{4,3,2,1,0:T(8,128)(2,1)}, u32[]{:S(2)}, u32[]{:S(2)}) collective-permute-start(bf16[2,2,1,1056,256]{4,3,2,1,0:T(8,128)(2,1)} %constant_dynamic-slice_fusion.1), channel_id=1, source_target_pairs={{0,4},{4,0},{8,12},{12,8},{16,20},{20,16},{24,28},{28,24},{1,5},{5... | collective-permute-start | bytes 6488072 | tf_op jit(solution)/shard_map/ppermute | solution.py:129
  433.5 68.9 %all-to-all-start.5 = ((bf16[8,96,2048]{2,1,0:T(8,128)(2,1)}), bf16[8,96,2048]{2,1,0:T(8,128)(2,1)}, u32[]{:S(2)}, u32[]{:S(2)}) async-start(bf16[8,96,2048]{2,1,0:T(8,128)(2,1)} %bitcast.221), calls=%async_computation.5 | async-start | bytes 6291456 | tf_op jit(solution)/shard_map/all_to_all | solution.py:118
  440.1 58.2 %collective-permute-start.76 = (bf16[2,1,1,1056,256]{4,3,2,1,0:T(8,128)(2,1)S(1)}, bf16[2,1,1,1056,256]{4,3,2,1,0:T(8,128)(2,1)S(1)}, u32[]{:S(2)}, u32[]{:S(2)}) collective-permute-start(bf16[2,1,1,1056,256]{4,3,2,1,0:T(8,128)(2,1)S(1)} %dynamic-slice_convert_fusion), channel_id=1, source_target_pairs={{0,8},{4,12},{8,0},{12,4},{16,24},{20,28},{24,16},{28,20},{1,9},{5... | collective-permute-start | bytes 3244040 | tf_op jit(solution)/shard_map/ppermute | solution.py:129
  444.9 55.9 %collective-permute-start.73 = (bf16[1,2,1,1056,256]{4,3,2,1,0:T(8,128)(2,1)S(1)}, bf16[1,2,1,1056,256]{4,3,2,1,0:T(8,128)(2,1)S(1)}, u32[]{:S(2)}, u32[]{:S(2)}) collective-permute-start(bf16[1,2,1,1056,256]{4,3,2,1,0:T(8,128)(2,1)S(1)} %dynamic-slice_convert_fusion.1), channel_id=1, source_target_pairs={{0,16},{4,20},{8,24},{12,28},{16,0},{20,4},{24,8},{28,12},{1,17},{... | collective-permute-start | bytes 3244040 | tf_op jit(solution)/shard_map/ppermute | solution.py:129
  502.5 63.6 %all-to-all-start.6 = ((bf16[8,96,2176]{2,1,0:T(8,128)(2,1)}), bf16[8,96,2176]{2,1,0:T(8,128)(2,1)}, u32[]{:S(2)}, u32[]{:S(2)}) async-start(bf16[8,96,2176]{2,1,0:T(8,128)(2,1)} %bitcast.214), calls=%async_computation.6 | async-start | bytes 6684672 | tf_op jit(solution)/shard_map/all_to_all | solution.py:118
  508.4 49.1 %collective-permute-start.74 = (bf16[1,1,1,1056,256]{4,3,2,1,0:T(8,128)(2,1)S(1)}, bf16[1,1,1,1056,256]{4,3,2,1,0:T(8,128)(2,1)S(1)}, u32[]{:S(2)}, u32[]{:S(2)}) collective-permute-start(bf16[1,1,1,1056,256]{4,3,2,1,0:T(8,128)(2,1)S(1)} %dynamic-slice_convert_fusion.5), channel_id=1, source_target_pairs={{0,8},{4,12},{8,0},{12,4},{16,24},{20,28},{24,16},{28,20},{1,9},{5... | collective-permute-start | bytes 1622024 | tf_op jit(solution)/shard_map/ppermute | solution.py:129
  566.1 81.8 %all-to-all-start.9 = ((bf16[8,1056,256]{2,1,0:T(8,128)(2,1)}), bf16[8,1056,256]{2,1,0:T(8,128)(2,1)}, u32[]{:S(2)}, u32[]{:S(2)}) async-start(bf16[8,1056,256]{2,1,0:T(8,128)(2,1)} %get-tuple-element.35), calls=%async_computation.9 | async-start | bytes 8650752 | tf_op jit(solution)/shard_map/all_to_all | solution.py:118
  656.2 142.1 %collective-permute-start.41 = (bf16[128,2048]{1,0:T(8,128)(2,1)}, bf16[128,2048]{1,0:T(8,128)(2,1)}, u32[]{:S(2)}, u32[]{:S(2)}) collective-permute-start(bf16[128,2048]{1,0:T(8,128)(2,1)} %fusion.50), channel_id=1, source_target_pairs={{0,1},{1,2},{2,3},{3,0},{4,5},{5,6},{6,7},{7,4},{8,9},{9,10},{10,1... | collective-permute-start | bytes 1572872 | tf_op jit(solution)/shard_map/ppermute | solution.py:75
  725.2 76.3 %collective-permute-start.69 = (bf16[2,2,1,512,256]{4,3,2,1,0:T(8,128)(2,1)}, bf16[2,2,1,512,256]{4,3,2,1,0:T(8,128)(2,1)}, u32[]{:S(2)}, u32[]{:S(2)}) collective-permute-start(bf16[2,2,1,512,256]{4,3,2,1,0:T(8,128)(2,1)} %constant_dynamic-slice_fusion.2), channel_id=1, source_target_pairs={{0,4},{4,0},{8,12},{12,8},{16,20},{20,16},{24,28},{28,24},{1,5},{5... | collective-permute-start | bytes 3145736 | tf_op jit(solution)/shard_map/ppermute | solution.py:129
  760.5 44.2 %collective-permute-start.63 = (bf16[2,2,1,256,640]{4,3,2,1,0:T(8,128)(2,1)S(1)}, bf16[2,2,1,256,640]{4,3,2,1,0:T(8,128)(2,1)S(1)}, u32[]{:S(2)}, u32[]{:S(2)}) collective-permute-start(bf16[2,2,1,256,640]{4,3,2,1,0:T(8,128)(2,1)S(1)} %fusion.30), channel_id=1, source_target_pairs={{0,4},{4,0},{8,12},{12,8},{16,20},{20,16},{24,28},{28,24},{1,5},{5... | collective-permute-start | bytes 3932168 | tf_op jit(solution)/shard_map/ppermute | solution.py:129
  (200 other events, 2779.7 us)

commit v3 on v2

--- a/solution.py
+++ b/solution.py
@@ -15,6 +15,8 @@
 
 
 LANES = 128
+DP = "dp"
+TENSOR = "tensor"
 EPSILON = 1e-06
 NEGATIVE = -1e30
 
@@ -71,8 +73,8 @@
 
 
 def send_tensor(values, step):
-    count = lax.axis_size("tensor")
-    return lax.ppermute(values, "tensor", [(i, (i + step) % count) for i in range(count)])
+    count = lax.axis_size(TENSOR)
+    return lax.ppermute(values, TENSOR, [(i, (i + step) % count) for i in range(count)])
 
 
 def pieces_of(values, parts):
@@ -82,36 +84,26 @@
 
 def gather_tensor(own, parts=2):
     pieces = pieces_of(own, parts)
-    found = [list(pieces)]
-    for _ in range(1, lax.axis_size("tensor")):
+    found = list(pieces)
+    for _ in range(1, lax.axis_size(TENSOR)):
         pieces = [send_tensor(piece, -1) for piece in pieces]
-        found.append(list(pieces))
-    return jnp.concatenate([piece for row in found for piece in row], axis=0)
+        found += pieces
+    return found
 
 
 def scatter_tensor(share, parts=2):
-    count = lax.axis_size("tensor")
+    count = lax.axis_size(TENSOR)
     blocks = share.reshape((count, share.shape[0] // count) + share.shape[1:])
     sums = [piece.astype(jnp.bfloat16) for piece in pieces_of(blocks[count - 1], parts)]
     for step in range(1, count):
-        sums = [send_tensor(piece.astype(jnp.bfloat16), 1) for piece in sums]
+        sums = [send_tensor(piece, 1) for piece in sums]
         sums = [
             piece.astype(jnp.float32) + more.astype(jnp.float32)
             for piece, more in zip(sums, pieces_of(blocks[count - 1 - step], parts))
         ]
+        if step < count - 1:
+            sums = [piece.astype(jnp.bfloat16) for piece in sums]
     return jnp.concatenate(sums, axis=0)
-
-
-def with_column(rows, column):
-    high = column.astype(jnp.bfloat16)
-    low = (column - high.astype(jnp.float32)).astype(jnp.bfloat16)
-    return jnp.concatenate(
-        [rows, jnp.pad(jnp.stack([high, low], axis=1), ((0, 0), (0, LANES - 2)))], axis=1
-    )
-
-
-def column_of(rows, place):
-    return jnp.sum(rows[:, place : place + 2].astype(jnp.float32), axis=1)
 
 
 def exchange(values, axes):
@@ -119,26 +111,28 @@
 
 
 def dp_orders():
-    count = lax.axis_size("dp")
+    count = lax.axis_size(DP)
     masks = [1 << k for k in range(count.bit_length() - 1)]
     return (masks[1:] + masks[:1], masks[:0:-1] + masks[:1])
 
 
 def swap_dp(values, mask):
-    count = lax.axis_size("dp")
-    return lax.ppermute(values, "dp", [(i, i ^ mask) for i in range(count)])
+    count = lax.axis_size(DP)
+    return lax.ppermute(values, DP, [(i, i ^ mask) for i in range(count)])
 
 
 def axis_of(mask):
-    return lax.axis_size("dp").bit_length() - 1 - mask.bit_length()
-
-
-def gather_dp(own, order):
-    count = lax.axis_size("dp")
-    index = lax.axis_index("dp")
+    return lax.axis_size(DP).bit_length() - 1 - mask.bit_length()
+
+
+def gather_dp(own, order, apart=False):
+    count = lax.axis_size(DP)
+    index = lax.axis_index(DP)
     current = own.reshape((1,) * (count.bit_length() - 1) + own.shape)
-    for mask in order:
+    for step, mask in enumerate(order):
         other = swap_dp(current, mask)
+        if apart and step + 1 == len(order):
+            return [values.reshape((count // 2,) + own.shape) for values in (current, other)]
         high = (index & mask) > 0
         current = jnp.concatenate(
             [jnp.where(high, other, current), jnp.where(high, current, other)],
@@ -148,15 +142,20 @@
 
 
 def scatter_dp(blocks, order):
-    count = lax.axis_size("dp")
-    index = lax.axis_index("dp")
-    own = blocks.shape[1:]
-    current = blocks.reshape((2,) * (count.bit_length() - 1) + own)
+    count = lax.axis_size(DP)
+    index = lax.axis_index(DP)
+    bits = count.bit_length() - 1
+    pair = isinstance(blocks, (tuple, list))
+    own = blocks[0].shape[1:] if pair else blocks.shape[1:]
+    current = None if pair else blocks.reshape((2,) * bits + own)
     for mask in order[::-1]:
         high = ((index & mask) > 0).astype(jnp.int32)
         axis = axis_of(mask)
-        keep = lax.dynamic_slice_in_dim(current, high, 1, axis)
-        give = lax.dynamic_slice_in_dim(current, 1 - high, 1, axis).astype(jnp.bfloat16)
+        if current is None:
+            keep, give = [half.reshape((2,) * (bits - 1) + (1,) + own) for half in blocks]
+        else:
+            keep = lax.dynamic_slice_in_dim(current, high, 1, axis)
+            give = lax.dynamic_slice_in_dim(current, 1 - high, 1, axis).astype(jnp.bfloat16)
         got = swap_dp(give, mask)
         current = keep.astype(jnp.float32) + got.astype(jnp.float32)
     return current.reshape(own)
@@ -167,7 +166,7 @@
 
 
 def tall_blocks(values):
-    count = lax.axis_size("dp")
+    count = lax.axis_size(DP)
     values = values.reshape(values.shape[0], count, -1)
     return jnp.moveaxis(values, 1, 0).astype(jnp.bfloat16)
 
@@ -233,46 +232,76 @@
     )(*arguments)
 
 
-def shared_experts(hidden, grad, first, second, units):
+def mingle(pair, bit):
+    mine, theirs = pair
+    blocks = [jnp.where(bit > 0, theirs, mine), jnp.where(bit > 0, mine, theirs)]
+    return jnp.stack(blocks, axis=1).reshape((-1,) + mine.shape[1:])
+
+
+def part_by(blocks, bit):
+    even, odd = blocks[0::2], blocks[1::2]
+    return [jnp.where(bit > 0, odd, even), jnp.where(bit > 0, even, odd)]
+
+
+def shared_experts(hidden, grad, firsts, seconds, units, bit):
+    if firsts[0].shape[2] % LANES == 0:
+        return shared_kernel(hidden, grad, firsts, seconds, units, bit)
+    first, second = [mingle(pair, bit) for pair in (firsts, seconds)]
+    given, count = first.shape[0], lane_count(first)
+    pairs = [part_by(regroup(blocks, count), 0) for blocks in (first, second)]
+    out, back, *pairs = shared_kernel(hidden, grad, *pairs, units, jnp.int32(0))
+    pairs = [part_by(regroup(mingle(pair, 0), given), bit) for pair in pairs]
+    return out, back, *pairs
+
+
+def shared_kernel(hidden, grad, firsts, seconds, units, bit):
     narrow = jnp.bfloat16
     rows, width = hidden.shape
-    given = first.shape[0]
-    first, second = [regroup(blocks, lane_count(blocks)) for blocks in (first, second)]
-    count, _, part = first.shape
+    count, _, part = firsts[0].shape
     half = units // 2
 
-    def body(x_ref, g_ref, first_ref, second_ref, out_ref, back_ref, dfirst_ref, dsecond_ref,
-             gate_ref, up_ref, down_ref):
+    def body(bit_ref, x_ref, g_ref, *refs):
+        pairs, (out_ref, back_ref), results = refs[:4], refs[4:6], refs[6:10]
+        gate_ref, up_ref, down_ref = refs[10:]
+        mine = bit_ref[0]
         for j in range(count):
-            lanes = slice(j * part, (j + 1) * part)
-            gate_ref[:, lanes] = first_ref[j, :units]
-            up_ref[:, lanes] = second_ref[j, :units]
-            down_ref[:half, lanes] = first_ref[j, units:]
-            down_ref[half:, lanes] = second_ref[j, units:]
+            for place in range(2):
+                own = mine if place == 0 else 1 - mine
+                lanes = pl.ds(pl.multiple_of((2 * j + own) * part, LANES), part)
+                gate_ref[:, lanes] = pairs[place][j, :units]
+                up_ref[:, lanes] = pairs[2 + place][j, :units]
+                down_ref[:half, lanes] = pairs[place][j, units:]
+                down_ref[half:, lanes] = pairs[2 + place][j, units:]
         a = dot_of(x_ref[...], gate_ref[...], (1, 1))
         b = dot_of(x_ref[...], up_ref[...], (1, 1))
         u = dot_of(g_ref[...], down_ref[...], (1, 1))
         h, da, db = [v.astype(narrow) for v in swiglu_parts(a, b, u)]
         out_ref[...] = dot_of(h, down_ref[...], (1, 0)).astype(narrow)
         back_ref[...] = dot_of(da, gate_ref[...], (1, 0)) + dot_of(db, up_ref[...], (1, 0))
-        dgate = dot_of(da, x_ref[...], (0, 0)).astype(narrow)
-        dup = dot_of(db, x_ref[...], (0, 0)).astype(narrow)
-        ddown = dot_of(h, g_ref[...], (0, 0)).astype(narrow)
+        gate_ref[...] = dot_of(da, x_ref[...], (0, 0)).astype(narrow)
+        up_ref[...] = dot_of(db, x_ref[...], (0, 0)).astype(narrow)
+        down_ref[...] = dot_of(h, g_ref[...], (0, 0)).astype(narrow)
         for j in range(count):
-            lanes = slice(j * part, (j + 1) * part)
-            dfirst_ref[j, :units] = dgate[:, lanes]
-            dsecond_ref[j, :units] = dup[:, lanes]
-            dfirst_ref[j, units:] = ddown[:half, lanes]
-            dsecond_ref[j, units:] = ddown[half:, lanes]
-
-    wide_scratch = ((units, width), narrow)
-    out, back, dfirst, dsecond = call_kernel(
+            for place in range(2):
+                own = mine if place == 0 else 1 - mine
+                lanes = pl.ds(pl.multiple_of((2 * j + own) * part, LANES), part)
+                results[place][j, :units] = gate_ref[:, lanes]
+                results[2 + place][j, :units] = up_ref[:, lanes]
+                results[place][j, units:] = down_ref[:half, lanes]
+                results[2 + place][j, units:] = down_ref[half:, lanes]
+
+    blocks = (firsts[0].shape, narrow)
+    vmem = pl.BlockSpec(memory_space=pltpu.VMEM)
+    out, back, *results = pl.pallas_call(
         body,
-        [((rows, width), narrow), ((rows, width), jnp.float32), (first.shape, narrow), (second.shape, narrow)],
-        [wide_scratch] * 3,
-        hidden, grad, first, second,
-    )
-    return out, back, regroup(dfirst, given), regroup(dsecond, given)
+        in_specs=[pl.BlockSpec(memory_space=pltpu.SMEM)] + [vmem] * 6,
+        out_shape=[
+            jax.ShapeDtypeStruct(shape, dtype)
+            for shape, dtype in [((rows, width), narrow), ((rows, width), jnp.float32)] + [blocks] * 4
+        ],
+        scratch_shapes=[pltpu.VMEM((units, width), narrow)] * 3,
+    )(bit.reshape(1), hidden, grad, *firsts, *seconds)
+    return out, back, results[:2], results[2:]
 
 
 def load_slab(slab_ref, wide_ref, place, units):
@@ -308,10 +337,8 @@
         back_ref[:, :width] = (
             dot_of(da, gate_ref[...], (1, 0)) + dot_of(db, up_ref[...], (1, 0))
         ).astype(narrow)
-        lane = lax.broadcasted_iota(jnp.int32, (slots, LANES), 1)
         high = slot.astype(narrow).astype(jnp.float32)
-        column = jnp.where(lane == 0, high, jnp.where(lane == 1, slot - high, 0.0))
-        back_ref[:, width:] = column.astype(narrow)
+        back_ref[:, width:] = two_lanes(high, slot - high)
 
     inner = ((slots, units), narrow)
     return call_kernel(
@@ -346,6 +373,103 @@
         rows, grads, slabs, da, db, scaled,
     )
     return out, regroup(terms, given)
+
+
+def assemble(refs, whole_ref):
+    rows = refs[0].shape[0]
+    for i, ref in enumerate(refs):
+        whole_ref[i * rows : (i + 1) * rows] = ref[...]
+
+
+def joined(pieces):
+    def body(*refs):
+        assemble(refs[:-1], refs[-1])
+
+    shape = (len(pieces) * pieces[0].shape[0], pieces[0].shape[1])
+    return call_kernel(body, [(shape, pieces[0].dtype)], [], *pieces)[0]
+
+
+def normed_rows(pieces, gain):
+    def body(*refs):
+        gain_ref, whole_ref, hidden_ref = refs[-3:]
+        rows = refs[0].shape[0]
+        for i, ref in enumerate(refs[:-3]):
+            values = ref[...]
+            whole_ref[i * rows : (i + 1) * rows] = values
+            values = values.astype(jnp.float32)
+            hidden_ref[i * rows : (i + 1) * rows] = (
+                values * rms_scale(values) * gain_ref[...]
+            ).astype(jnp.bfloat16)
+
+    shape = (len(pieces) * pieces[0].shape[0], pieces[0].shape[1])
+    return call_kernel(body, [(shape, jnp.bfloat16)] * 2, [], *pieces, gain[None])
+
+
+def picked_rows(pieces, pick):
+    def body(*refs):
+        pick_ref, whole_ref, rows_ref = refs[-3:]
+        assemble(refs[:-3], whole_ref)
+        rows_ref[...] = dot_of(pick_ref[...], whole_ref[...], (0, 0)).astype(jnp.bfloat16)
+
+    width = pieces[0].shape[1]
+    shape = (len(pieces) * pieces[0].shape[0], width)
+    outs = [(shape, jnp.bfloat16), ((pick.shape[1], width), jnp.bfloat16)]
+    return call_kernel(body, outs, [], *pieces, pick)
+
+
+def expert_lanes(slots):
+    expert = lax.broadcasted_iota(jnp.int32, (slots, LANES), 0) // CAP
+    return lax.broadcasted_iota(jnp.int32, (slots, LANES), 1) == expert
+
+
+def token_rows(pieces, pick, router, chosen):
+    narrow = jnp.bfloat16
+    width = pieces[0].shape[1]
+    slots = pick.shape[1]
+
+    def body(*refs):
+        pick_ref, router_ref, chosen_ref, whole_ref, rows_ref = refs[-5:]
+        assemble(refs[:-5], whole_ref)
+        logits = dot_of(whole_ref[...], router_ref[...], (1, 0))
+        shifted = jnp.exp(logits - jnp.max(logits, axis=1, keepdims=True))
+        route = shifted / jnp.sum(shifted, axis=1, keepdims=True)
+        gate = jnp.where(chosen_ref[...] > 0, route[:, :ACTIVE], 0.0)
+        high = gate.astype(narrow)
+        low = (gate - high.astype(jnp.float32)).astype(narrow)
+        rows_ref[:, :width] = dot_of(pick_ref[...], whole_ref[...], (0, 0)).astype(narrow)
+        expert = lax.broadcasted_iota(jnp.int32, (slots, ACTIVE), 0) // CAP
+        own = lax.broadcasted_iota(jnp.int32, (slots, ACTIVE), 1) == expert
+        high, low = [
+            jnp.sum(jnp.where(own, dot_of(pick_ref[...], part, (0, 0)), 0.0), axis=1, keepdims=True)
+            for part in (high, low)
+        ]
+        rows_ref[:, width:] = two_lanes(high, low)
+
+    shape = (len(pieces) * pieces[0].shape[0], width)
+    outs = [(shape, narrow), ((slots, width + LANES), narrow)]
+    return call_kernel(body, outs, [], *pieces, pick, router, chosen)
+
+
+def two_lanes(high, low):
+    lane = lax.broadcasted_iota(jnp.int32, (high.shape[0], LANES), 1)
+    return jnp.where(lane == 0, high, jnp.where(lane == 1, low, 0.0)).astype(jnp.bfloat16)
+
+
+def combined_rows(pick, back, share):
+    narrow = jnp.bfloat16
+    rows, width = share.shape
+    slots = pick.shape[1]
+
+    def body(pick_ref, back_ref, share_ref, out_ref):
+        extra = back_ref[:, width:]
+        own = expert_lanes(slots)
+        spread = [jnp.where(own, extra[:, i : i + 1], 0.0).astype(narrow) for i in range(2)]
+        values = share_ref[...] + dot_of(pick_ref[...], back_ref[:, :width], (1, 0))
+        out_ref[:, :width] = values.astype(narrow)
+        values = dot_of(pick_ref[...], spread[0], (1, 0)) + dot_of(pick_ref[...], spread[1], (1, 0))
+        out_ref[:, width:] = values.astype(narrow)
+
+    return call_kernel(body, [((rows, width + LANES), narrow)], [], pick, back, share)[0]
 
 
 def block(
@@ -371,19 +495,19 @@
     narrow = jnp.bfloat16
     own_rows = block_in.shape[0]
     width = block_in.shape[1]
-    dp_count = lax.axis_size("dp")
-    tensor_count = lax.axis_size("tensor")
-    tensor_index = lax.axis_index("tensor")
+    dp_count = lax.axis_size(DP)
+    tensor_count = lax.axis_size(TENSOR)
+    tensor_index = lax.axis_index(TENSOR)
     group = own_rows * tensor_count
     owner_count = dp_count // ACTIVE
     slot_piece = CAP // owner_count
     slots = ACTIVE * CAP
-    both = ("dp", "tensor")
+    both = (DP, TENSOR)
     first_order, second_order = dp_orders()
 
-    all_in = gather_tensor(block_in)
+    in_pieces = gather_tensor(block_in)
     small = jnp.concatenate([kv_down_weight, router_weight], axis=1)
-    small = exchange(jnp.broadcast_to(small[None], (tensor_count,) + small.shape), "tensor")
+    small = exchange(jnp.broadcast_to(small[None], (tensor_count,) + small.shape), TENSOR)
     gains = jnp.concatenate([attn_norm_gain, ffn_norm_gain, latent_gain])
     gains = exchange(
         jnp.broadcast_to(gains[None], (dp_count * tensor_count, gains.shape[0])), both
@@ -393,35 +517,39 @@
     gain_two = gains[:, split_one : 2 * split_one].reshape(-1)
     gain_lat = gains[:, 2 * split_one :].reshape(-1)
 
-    query_full = gather_dp(query_weight, first_order).reshape(width, -1)
+    query_full = gather_dp(query_weight, first_order)
+    query_full = query_full.reshape(width, -1)
     small = gather_dp(small, second_order).reshape(width, -1)
     kv_up_full = gather_dp(kv_up_weight, second_order).reshape(LATENT, -1)
     kv_down = small[:, : LATENT + ROPE]
     router = small[:, LATENT + ROPE :]
-    output_full = wide_rows(gather_dp(output_weight, second_order))
-    grad_all = gather_tensor(out_grad, 1)
+    output_full = gather_dp(output_weight, second_order)
+    output_full = wide_rows(output_full)
+    grad_pieces = gather_tensor(out_grad, 1)
 
     shared_units = shared_down_weight.shape[0]
     half = shared_units // 2
+    packed = (
+        jnp.concatenate([shared_gate_weight.T, shared_down_weight[:half]]),
+        jnp.concatenate([shared_up_weight.T, shared_down_weight[half:]]),
+    )
     shared = (
-        gather_dp(jnp.concatenate([shared_gate_weight.T, shared_down_weight[:half]]), first_order),
-        gather_dp(jnp.concatenate([shared_up_weight.T, shared_down_weight[half:]]), second_order),
+        gather_dp(packed[0], first_order, apart=True),
+        gather_dp(packed[1], second_order, apart=True),
     )
     units = expert_down_weight.shape[1]
     slabs = jnp.concatenate(
-        [
-            jnp.swapaxes(expert_gate_weight, 1, 2),
-            jnp.swapaxes(expert_up_weight, 1, 2),
-            expert_down_weight,
-        ],
-        axis=1,
-    )
-    slabs = exchange(jnp.repeat(slabs, owner_count, axis=0), "dp")
+            [
+                jnp.swapaxes(expert_gate_weight, 1, 2),
+                jnp.swapaxes(expert_up_weight, 1, 2),
+                expert_down_weight,
+            ],
+            axis=1,
+    )
+    slabs = exchange(jnp.repeat(slabs, owner_count, axis=0), DP)
 
     heads = query_full.shape[1] // (NOPE + ROPE)
-    residual_all = all_in.astype(wide)
-    scale_all = rms_scale(residual_all)
-    hidden_one = (residual_all * scale_all * gain_one).astype(narrow)
+    all_in, hidden_one = normed_rows(in_pieces, gain_one)
     latent_in = matmul(hidden_one, kv_down).astype(narrow)
     compressed = latent_in[:, :LATENT].astype(wide)
     scale_lat = rms_scale(compressed)
@@ -449,7 +577,7 @@
     scale_two = rms_scale(after_attn)
     normed_two = after_attn * scale_two
     hidden_two_own = (normed_two * gain_two).astype(narrow)
-    hidden_two = gather_tensor(hidden_two_own)
+    hidden_pieces = gather_tensor(hidden_two_own)
 
     ids = jnp.concatenate([expert_ids, expert_ids], axis=0)
     ids = lax.dynamic_slice_in_dim(ids, tensor_index * own_rows, group, 0)
@@ -459,29 +587,24 @@
         :, :, None
     ]
     pick = places.astype(narrow).reshape(group, slots)
-    grad_in = left_dot(pick, grad_all).astype(narrow)
-    grad_here = exchange(grad_in.reshape(dp_count, slot_piece, width), "dp").reshape(-1, width)
-    route_prob = jax.nn.softmax(matmul(hidden_two, router), axis=-1)
-    gate = jnp.where(chosen, route_prob[:, :ACTIVE], 0.0)
-    weight = jnp.sum(jnp.where(places, gate[:, :, None], 0.0), axis=0).reshape(slots)
-    tokens_in = with_column(left_dot(pick, hidden_two).astype(narrow), weight)
-    rows_here = exchange(tokens_in.reshape(dp_count, slot_piece, -1), "dp")
+    grad_all, grad_in = picked_rows(grad_pieces, pick)
+    grad_here = exchange(grad_in.reshape(dp_count, slot_piece, width), DP).reshape(-1, width)
+    hidden_two, tokens_in = token_rows(hidden_pieces, pick, router, chosen.astype(jnp.int32))
+    rows_here = exchange(tokens_in.reshape(dp_count, slot_piece, -1), DP)
     rows_here = rows_here.reshape(slots, -1)
 
     moe_share, hidden_two_share, shared_first, shared_second = shared_experts(
-            hidden_two, grad_all, shared[0], shared[1], shared_units
+            hidden_two, grad_all, shared[0], shared[1], shared_units, lax.axis_index(DP) & 1
     )
 
     owned_back, owned_a_grad, owned_b_grad, owned_scaled = owned_first(rows_here, grad_here, slabs)
-    back_flat = exchange(owned_back.reshape(dp_count, slot_piece, -1), "dp")
+    back_flat = exchange(owned_back.reshape(dp_count, slot_piece, -1), DP)
     back_flat = back_flat.reshape(slots, -1)
-    per_slot = column_of(back_flat, width).reshape(1, ACTIVE, CAP)
-    back_flat = back_flat[:, :width]
     owned_out, terms = owned_second(
             rows_here, grad_here, slabs, owned_a_grad, owned_b_grad, owned_scaled
     )
-    routed_flat = exchange(owned_out.reshape(dp_count, slot_piece, width), "dp").reshape(-1, width)
-    terms = exchange(terms, "dp")
+    routed_flat = exchange(owned_out.reshape(dp_count, slot_piece, width), DP).reshape(-1, width)
+    terms = exchange(terms, DP)
     terms = terms.reshape((ACTIVE, owner_count) + terms.shape[1:])
 
     def summed(first):
@@ -491,11 +614,7 @@
     expert_up_wgrad = jnp.swapaxes(summed(units), 1, 2)
     expert_down_grad = summed(2 * units)
 
-    hidden_two_share = hidden_two_share + matmul(pick, back_flat)
-    gate_share = jnp.sum(jnp.where(places, per_slot, 0.0), axis=-1)
-    hidden_two_share = jnp.concatenate(
-            [hidden_two_share, jnp.pad(gate_share, ((0, 0), (0, LANES - ACTIVE)))], axis=1
-    )
+    hidden_two_share = combined_rows(pick, back_flat, hidden_two_share)
     hidden_two_grad = scatter_tensor(hidden_two_share)
     gate_grad = hidden_two_grad[:, width : width + ACTIVE]
     hidden_two_grad = hidden_two_grad[:, :width]
@@ -506,13 +625,13 @@
     logit_grad = (
         prob_own * (prob_grad - jnp.sum(prob_own * prob_grad, axis=-1, keepdims=True))
     ).astype(narrow)
-    router_grad = left_dot(hidden_two_own, logit_grad)
     hidden_two_grad = hidden_two_grad + right_dot(logit_grad, router)
     gain_two_grad = jnp.sum(hidden_two_grad * normed_two, axis=0)
     after_attn_grad = out_grad.astype(wide) + norm_back(
             hidden_two_grad * gain_two, normed_two, scale_two
     )
     residual_low = gather_tensor(after_attn_grad.astype(narrow))
+    residual_low = joined(residual_low)
     moe_share = moe_share.astype(wide) + matmul(pick, routed_flat)
     moe_own = scatter_tensor(moe_share, 1)
     block_out = (after_attn + moe_own).astype(narrow)
@@ -547,9 +666,10 @@
     normed_one = residual_in * scale_one
     input_grad = after_attn_grad + norm_back(hidden_one_grad * gain_one, normed_one, scale_one)
 
-    tall = jnp.concatenate(
-        [left_dot(hidden_one, latent_in_low), router_grad], axis=1
-    ).astype(narrow)
+    latent_wide = jnp.pad(latent_in_low, ((0, 0), (0, router.shape[1])))
+    logit_wide = jnp.pad(logit_grad, ((0, 0), (latent_in_low.shape[1], 0)))
+    tall = left_dot(hidden_one, latent_wide) + left_dot(hidden_two_own, logit_wide)
+    tall = tall.astype(narrow)
     tall = tall.reshape(dp_count, -1, tall.shape[1])
     shared_first = scatter_dp(shared_first, first_order)
     shared_second = scatter_dp(shared_second, second_order)
@@ -564,11 +684,14 @@
     kv_up_grad = kv_up_grad.astype(narrow).reshape(dp_count, -1, kv_up_grad.shape[1])
     kv_up_grad = scatter_dp(kv_up_grad, second_order)
     tall = scatter_dp(tall, second_order).astype(narrow)
-    tall = exchange(tall.reshape(tensor_count, -1, tall.shape[1]), "tensor")
+    tall = exchange(tall.reshape(tensor_count, -1, tall.shape[1]), TENSOR)
     tall = jnp.sum(tall.astype(wide), axis=0)
     kv_down_grad = tall[:, : LATENT + ROPE]
     router_grad = tall[:, LATENT + ROPE :]
-    gain_one_grad = jnp.sum(hidden_one_share * (residual_all * scale_all), axis=0)
+    residual_all = all_in.astype(wide)
+    gain_one_grad = jnp.sum(
+        hidden_one_share * (residual_all * rms_scale(residual_all)), axis=0
+    )
     devices = dp_count * tensor_count
     gain_grads = jnp.concatenate(
         [
@@ -601,40 +724,40 @@
 
 def solution(mesh):
     in_specs = (
-        P(("dp", "tensor"), None),
-        P(("dp", "tensor")),
-        P("dp", "tensor"),
-        P(("dp", "tensor"), None),
-        P(("dp", "tensor")),
-        P("dp", "tensor"),
-        P("tensor", "dp"),
-        P(("dp", "tensor")),
-        P(("dp", "tensor"), None),
-        P("dp", None),
-        P("dp", "tensor"),
-        P("dp", "tensor"),
-        P("tensor", "dp"),
-        P(None, "dp", "tensor"),
-        P(None, "dp", "tensor"),
-        P(None, "tensor", "dp"),
-        P(("dp", "tensor"), None),
+        P((DP, TENSOR), None),
+        P((DP, TENSOR)),
+        P(DP, TENSOR),
+        P((DP, TENSOR), None),
+        P((DP, TENSOR)),
+        P(DP, TENSOR),
+        P(TENSOR, DP),
+        P((DP, TENSOR)),
+        P((DP, TENSOR), None),
+        P(DP, None),
+        P(DP, TENSOR),
+        P(DP, TENSOR),
+        P(TENSOR, DP),
+        P(None, DP, TENSOR),
+        P(None, DP, TENSOR),
+        P(None, TENSOR, DP),
+        P((DP, TENSOR), None),
     )
     out_specs = (
-        P(("dp", "tensor"), None),
-        P(("dp", "tensor"), None),
-        P(("dp", "tensor")),
-        P("dp", "tensor"),
-        P(("dp", "tensor"), None),
-        P(("dp", "tensor")),
-        P("dp", "tensor"),
-        P("tensor", "dp"),
-        P(("dp", "tensor")),
-        P(("dp", "tensor"), None),
-        P("dp", "tensor"),
-        P("dp", "tensor"),
-        P("tensor", "dp"),
-        P(None, "dp", "tensor"),
-        P(None, "dp", "tensor"),
-        P(None, "tensor", "dp"),
+        P((DP, TENSOR), None),
+        P((DP, TENSOR), None),
+        P((DP, TENSOR)),
+        P(DP, TENSOR),
+        P((DP, TENSOR), None),
+        P((DP, TENSOR)),
+        P(DP, TENSOR),
+        P(TENSOR, DP),
+        P((DP, TENSOR)),
+        P((DP, TENSOR), None),
+        P(DP, TENSOR),
+        P(DP, TENSOR),
+        P(TENSOR, DP),
+        P(None, DP, TENSOR),
+        P(None, DP, TENSOR),
+        P(None, TENSOR, DP),
     )
     return jax.shard_map(block, mesh=mesh, in_specs=in_specs, out_specs=out_specs, check_vma=False)

time: 859 us -> 794 us (0.924)
  waiting for transfers between devices: 419 us -> 362 us
  Pallas kernels: 48.5 us -> 77.1 us
  local copies, waits for them, and re-layouts: 85.7 us -> 66.8 us
  matrix products: 68.2 us -> 56.7 us
    ppermute x78, waiting for transfers between devices: 387 us -> 314 us  [the longest x36 158 us: swap_dp(): return lax.ppermute(values, DP, [(i, i ^ mask) for i in range(count)])]
    pallas_call x0 -> x1, Pallas kernels: none -> 25 us  [shared_kernel(): pl.pallas_call(body, in_specs=[pl.BlockSpec(memory_space=pltpu.SMEM)] + [...]
    all_to_all x10, waiting for transfers between devices: 31.6 us -> 48.2 us  [exchange(): return lax.all_to_all(values, axes, split_axis=0, concat_axis=0, tiled=True)]
    dot_general x8 -> x6, matrix products: 26.1 us -> 15.7 us  [matmul(): return jnp.dot(left, right, preferred_element_type=jnp.float32)]
    concatenate x6 -> x0, local copies, waits for them, and re-layouts: 9.08 us -> none  [the longest x2 6.39 us: block(): jnp.concatenate([left_dot(hidden_one, latent_in_low), router_grad], axis=1)]
    unnamed x293 -> x258, local copies, waits for them, and re-layouts: 33.9 us -> 25.9 us
    pallas_call x3 -> x7, Pallas kernels: 48.5 us -> 52.1 us  [call_kernel(): pl.pallas_call(body, out_shape=[jax.ShapeDtypeStruct(shape, dtype) for sh...]
    dot_general x7 -> x5, matrix products: 17.9 us -> 14.5 us  [left_dot(): lax.dot_general(left, right, (((0,), (0,)), ((), ())), preferred_element_...]
  transfers between devices with their start and end apart: 88 -> 88, of which waited for: 44 -> 41; matrix products, arithmetic and copies ran while one was open for 27% -> 24% of each run, Pallas kernels for 6% -> 10%
where the time goes in v3:
time: 794 us; the launch traced here: 784 us
  waiting for transfers between devices  362 us (46%)
  starting transfers between devices  127 us (16%)
  other arithmetic  90.7 us (11%)
  Pallas kernels  77.1 us (10%)
  local copies, waits for them, and re-layouts  66.8 us (8%)
  matrix products  56.7 us (7%)
    ppermute x36, waiting for transfers between devices, swap_dp(): return lax.ppermute(values, DP, [(i, i ^ mask) for i in range(count)])  158 us
    ppermute x42, waiting for transfers between devices, send_tensor(): lax.ppermute(values, TENSOR, [(i, (i + step) % count) for i in range(coun...  157 us
    ppermute x42, starting transfers between devices, send_tensor(): lax.ppermute(values, TENSOR, [(i, (i + step) % count) for i in range(coun...  56.1 us
    pallas_call x7, Pallas kernels, call_kernel(): pl.pallas_call(body, out_shape=[jax.ShapeDtypeStruct(shape, dtype) for sh...  52.1 us
    all_to_all x10, waiting for transfers between devices, exchange(): return lax.all_to_all(values, axes, split_axis=0, concat_axis=0, tiled=True)  48.2 us
    all_to_all x10, starting transfers between devices, exchange(): return lax.all_to_all(values, axes, split_axis=0, concat_axis=0, tiled=True)  44.3 us
    ppermute x36, starting transfers between devices, swap_dp(): return lax.ppermute(values, DP, [(i, i ^ mask) for i in range(count)])  26.7 us
    unnamed x258, local copies, waits for them, and re-layouts  25.9 us
  transfers between devices with their start and end apart: 88, of which 41 were waited for; matrix products, arithmetic and copies ran while one was open for 24% of the time, Pallas kernels for 10%

profile of v3, /device:TPU:0, one launch (start us, length us, event | category | flops | bytes accessed | tf_op | source)
XLA Modules:
  0.0 783.8 jit_solution(1572453911795994950)
XLA Ops:
  42.2 13.8 %collective-permute-done.10 = bf16[2,1,1,64,1024]{4,3,2,1,0:T(8,128)(2,1)S(1)} collective-permute-done((bf16[2,1,1,64,1024]{4,3,2,1,0:T(8,128)(2,1)S(1)}, bf16[2,1,1,64,1024]{4,3,2,1,0:T(8,128)(2,1)S(1)}, u32[]{:S(2)}, u32[]{:S(2)}) %collective-permute-start.10) | collective-permute-done | bytes 262176 | tf_op jit(solution)/shard_map/ppermute | solution.py:121
  66.0 13.6 %collective-permute-done.2.refs_4_ = bf16[64,2048]{1,0:T(8,128)(2,1)} collective-permute-done((bf16[64,2048]{1,0:T(8,128)(2,1)}, bf16[64,2048]{1,0:T(8,128)(2,1)}, u32[]{:S(2)}, u32[]{:S(2)}) %collective-permute-start.2) | collective-permute-done | bytes 262176 | tf_op jit(solution)/shard_map/ppermute | solution.py:77
  107.0 60.8 %collective-permute-done.6 = bf16[1,1,1,4,64,640]{5,4,3,2,1,0:T(8,128)(2,1)} collective-permute-done((bf16[1,1,1,4,64,640]{5,4,3,2,1,0:T(8,128)(2,1)}, bf16[1,1,1,4,64,640]{5,4,3,2,1,0:T(8,128)(2,1)}, u32[]{:S(2)}, u32[]{:S(2)}) %collective-permute-start.6) | collective-permute-done | bytes 327712 | tf_op jit(solution)/shard_map/ppermute | solution.py:121
  175.3 11.0 %collective-permute-done.7 = bf16[2,1,1,4,64,640]{5,4,3,2,1,0:T(8,128)(2,1)S(1)} collective-permute-done((bf16[2,1,1,4,64,640]{5,4,3,2,1,0:T(8,128)(2,1)S(1)}, bf16[2,1,1,4,64,640]{5,4,3,2,1,0:T(8,128)(2,1)S(1)}, u32[]{:S(2)}, u32[]{:S(2)}) %collective-permute-start.7) | collective-permute-done | bytes 655392 | tf_op jit(solution)/shard_map/ppermute | solution.py:121
  237.1 7.1 collective-permute-done.18
  251.5 9.1 %collective-permute-done.19 = bf16[64,2048]{1,0:T(8,128)(2,1)S(1)} collective-permute-done((bf16[64,2048]{1,0:T(8,128)(2,1)S(1)}, bf16[64,2048]{1,0:T(8,128)(2,1)S(1)}, u32[]{:S(2)}, u32[]{:S(2)}) %collective-permute-start.19) | collective-permute-done | bytes 262176 | tf_op jit(solution)/shard_map/ppermute | solution.py:77
  271.0 6.1 collective-permute-done.20
  285.4 8.5 %collective-permute-done.24.refs_2_ = bf16[64,2048]{1,0:T(8,128)(2,1)S(1)} collective-permute-done((bf16[64,2048]{1,0:T(8,128)(2,1)S(1)}, bf16[64,2048]{1,0:T(8,128)(2,1)S(1)}, u32[]{:S(2)}, u32[]{:S(2)}) %collective-permute-start.24) | collective-permute-done | bytes 262176 | tf_op jit(solution)/shard_map/ppermute | solution.py:77
  310.6 10.5 %collective-permute-start.29 = (bf16[64,2048]{1,0:T(8,128)(2,1)S(1)}, bf16[64,2048]{1,0:T(8,128)(2,1)}, u32[]{:S(2)}, u32[]{:S(2)}) collective-permute-start(bf16[64,2048]{1,0:T(8,128)(2,1)S(1)} %collective-permute-done.27.refs_5_), channel_id=1, source_target_pairs={{0,3},{1,0},{2,1},{3,2},{4,7},{5,4},{6,5},{7,6},{8,11},{9,8},{10,9... | collective-permute-start | bytes 786440 | tf_op jit(solution)/shard_map/ppermute | solution.py:77
  325.6 6.6 shard_map.289
  332.2 25.0 %shard_map.291 = (bf16[512,2048]{1,0:T(8,128)(2,1)}, f32[512,2048]{1,0:T(8,128)}, bf16[4,1056,256]{2,1,0:T(8,128)(2,1)}, bf16[4,1056,256]{2,1,0:T(8,128)(2,1)}, ...) custom-call(s32[1]{0:T(128)} %bitcast.19.bit_ref, bf16[512,2048]{1,0:T(8,128)(2,1)} %get-tuple-element.35.x_ref, ...), custom_call_target="tpu_custom_call" | custom-call | tf_op jit(solution)/shard_map/pallas_call | solution.py:295
  378.1 25.0 %all-to-all-done.2 = bf16[8,96,2176]{2,1,0:T(8,128)(2,1)S(1)} async-done(((bf16[8,96,2176]{2,1,0:T(8,128)(2,1)}), bf16[8,96,2176]{2,1,0:T(8,128)(2,1)S(1)}, u32[]{:S(2)}, u32[]{:S(2)}) %all-to-all-start.2) | async-done | bytes 3342368 | tf_op jit(solution)/shard_map/all_to_all | solution.py:110
  404.9 14.3 %shard_map.292 = (bf16[768,2176]{1,0:T(8,128)(2,1)}, bf16[768,352]{1,0:T(8,128)(2,1)}, bf16[768,352]{1,0:T(8,128)(2,1)}, bf16[768,352]{1,0:T(8,128)(2,1)}) custom-call(bf16[768,2176]{1,0:T(8,128)(2,1)} %bitcast.197, bf16[768,2048]{1,0:T(8,128)(2,1)} %bitcast.201, bf16[8,1056,256]{2,1,0:T(8,128)(2,1)} %all-to-all-done.4.slab_ref), custom_call_target="tpu_custom_call" | custom-call | tf_op jit(solution)/shard_map/pallas_call | solution.py:228
  431.6 11.6 %shard_map.293 = (bf16[768,2048]{1,0:T(8,128)(2,1)}, bf16[8,1056,256]{2,1,0:T(8,128)(2,1)}) custom-call(bf16[768,2176]{1,0:T(8,128)(2,1)} %bitcast.198, bf16[768,2048]{1,0:T(8,128)(2,1)} %bitcast.202, bf16[8,1056,256]{2,1,0:T(8,128)(2,1)} %all-to-all-done.4.slab_ref, bf16[768,352]{1,0:T(8,128)(2,1)} %get-tuple-element.40.da_ref, ...), custom_call_target="tpu_custom_call" | custom-call | tf_op jit(solution)/shard_map/pallas_call | solution.py:228
  446.5 39.5 %collective-permute-done.73 = bf16[1,2,1,1056,256]{4,3,2,1,0:T(8,128)(2,1)} collective-permute-done((bf16[1,2,1,1056,256]{4,3,2,1,0:T(8,128)(2,1)}, bf16[1,2,1,1056,256]{4,3,2,1,0:T(8,128)(2,1)}, u32[]{:S(2)}, u32[]{:S(2)}) %collective-permute-start.73) | collective-permute-done | bytes 1081376 | tf_op jit(solution)/shard_map/ppermute | solution.py:121
  508.5 7.0 shard_map.294
  517.8 18.7 %all-to-all-done.5 = bf16[8,96,2048]{2,1,0:T(8,128)(2,1)} async-done(((bf16[8,96,2048]{2,1,0:T(8,128)(2,1)}), bf16[8,96,2048]{2,1,0:T(8,128)(2,1)}, u32[]{:S(2)}, u32[]{:S(2)}) %all-to-all-start.5) | async-done | bytes 3145760 | tf_op jit(solution)/shard_map/all_to_all | solution.py:110
  563.5 10.4 %collective-permute-done.39 = bf16[128,2048]{1,0:T(8,128)(2,1)S(1)} collective-permute-done((bf16[128,2048]{1,0:T(8,128)(2,1)S(1)}, bf16[128,2048]{1,0:T(8,128)(2,1)S(1)}, u32[]{:S(2)}, u32[]{:S(2)}) %collective-permute-start.39) | collective-permute-done | bytes 524320 | tf_op jit(solution)/shard_map/ppermute | solution.py:77
  593.6 9.0 %collective-permute-done.48.refs_2_ = bf16[64,2048]{1,0:T(8,128)(2,1)} collective-permute-done((bf16[64,2048]{1,0:T(8,128)(2,1)S(1)}, bf16[64,2048]{1,0:T(8,128)(2,1)}, u32[]{:S(2)}, u32[]{:S(2)}) %collective-permute-start.48) | collective-permute-done | bytes 262176 | tf_op jit(solution)/shard_map/ppermute | solution.py:77
  675.5 7.3 all-to-all-start.7
  705.2 8.2 %collective-permute-done.55 = bf16[64,2048]{1,0:T(8,128)(2,1)S(1)} collective-permute-done((bf16[64,2048]{1,0:T(8,128)(2,1)S(1)}, bf16[64,2048]{1,0:T(8,128)(2,1)S(1)}, u32[]{:S(2)}, u32[]{:S(2)}) %collective-permute-start.55) | collective-permute-done | bytes 262176 | tf_op jit(solution)/shard_map/ppermute | solution.py:77
  720.1 8.5 %collective-permute-done.56 = bf16[64,2048]{1,0:T(8,128)(2,1)S(1)} collective-permute-done((bf16[64,2048]{1,0:T(8,128)(2,1)S(1)}, bf16[64,2048]{1,0:T(8,128)(2,1)S(1)}, u32[]{:S(2)}, u32[]{:S(2)}) %collective-permute-start.56) | collective-permute-done | bytes 262176 | tf_op jit(solution)/shard_map/ppermute | solution.py:77
  743.0 10.4 %collective-permute-done.70 = bf16[2,1,1,512,256]{4,3,2,1,0:T(8,128)(2,1)S(1)} collective-permute-done((bf16[2,1,1,512,256]{4,3,2,1,0:T(8,128)(2,1)S(1)}, bf16[2,1,1,512,256]{4,3,2,1,0:T(8,128)(2,1)S(1)}, u32[]{:S(2)}, u32[]{:S(2)}) %collective-permute-start.70) | collective-permute-done | bytes 524320 | tf_op jit(solution)/shard_map/ppermute | solution.py:121
  754.9 8.8 %collective-permute-done.64 = bf16[2,1,1,256,640]{4,3,2,1,0:T(8,128)(2,1)S(1)} collective-permute-done((bf16[2,1,1,256,640]{4,3,2,1,0:T(8,128)(2,1)S(1)}, bf16[2,1,1,256,640]{4,3,2,1,0:T(8,128)(2,1)S(1)}, u32[]{:S(2)}, u32[]{:S(2)}) %collective-permute-start.64) | collective-permute-done | bytes 655392 | tf_op jit(solution)/shard_map/ppermute | solution.py:121
  (615 shorter events, 429.8 us)
Async XLA Ops:
  2.5 61.6 %collective-permute-start = (bf16[64,2048]{1,0:T(8,128)(2,1)}, bf16[64,2048]{1,0:T(8,128)(2,1)}, u32[]{:S(2)}, u32[]{:S(2)}) collective-permute-start(bf16[64,2048]{1,0:T(8,128)(2,1)} %get-tuple-element.131.refs_0_), channel_id=1, source_target_pairs={{0,3},{1,0},{2,1},{3,2},{4,7},{5,4},{6,5},{7,6},{8,11},{9,8},{10,9... | collective-permute-start | bytes 786440 | tf_op jit(solution)/shard_map/ppermute | solution.py:77
  7.6 57.1 %collective-permute-start.1 = (bf16[64,2048]{1,0:T(8,128)(2,1)}, bf16[64,2048]{1,0:T(8,128)(2,1)}, u32[]{:S(2)}, u32[]{:S(2)}) collective-permute-start(bf16[64,2048]{1,0:T(8,128)(2,1)} %get-tuple-element.130.refs_1_), channel_id=1, source_target_pairs={{0,3},{1,0},{2,1},{3,2},{4,7},{5,4},{6,5},{7,6},{8,11},{9,8},{10,9... | collective-permute-start | bytes 786440 | tf_op jit(solution)/shard_map/ppermute | solution.py:77
  13.3 45.2 %collective-permute-start.12 = (bf16[1,1,1,256,768]{4,3,2,1,0:T(8,128)(2,1)}, bf16[1,1,1,256,768]{4,3,2,1,0:T(8,128)(2,1)}, u32[]{:S(2)}, u32[]{:S(2)}) collective-permute-start(bf16[1,1,1,256,768]{4,3,2,1,0:T(8,128)(2,1)} %bitcast.247), channel_id=1, source_target_pairs={{0,8},{4,12},{8,0},{12,4},{16,24},{20,28},{24,16},{28,20},{1,9},{5... | collective-permute-start | bytes 1179656 | tf_op jit(solution)/shard_map/ppermute | solution.py:121
  31.7 57.5 %all-to-all-start.1 = ((bf16[4,64,640]{2,1,0:T(8,128)(2,1)}), bf16[4,64,640]{2,1,0:T(8,128)(2,1)}, u32[]{:S(2)}, u32[]{:S(2)}) async-start(bf16[4,64,640]{2,1,0:T(8,128)(2,1)} %broadcast_in_dim.19), calls=%async_computation.1 | async-start | bytes 655360 | tf_op jit(solution)/shard_map/all_to_all | solution.py:110
  79.5 89.5 %collective-permute-start.11 = (bf16[2,2,1,64,1024]{4,3,2,1,0:T(8,128)(2,1)}, bf16[2,2,1,64,1024]{4,3,2,1,0:T(8,128)(2,1)}, u32[]{:S(2)}, u32[]{:S(2)}) collective-permute-start(bf16[2,2,1,64,1024]{4,3,2,1,0:T(8,128)(2,1)} %pad_maximum_fusion.16), channel_id=1, source_target_pairs={{0,4},{4,0},{8,12},{12,8},{16,20},{20,16},{24,28},{28,24},{1,5},{5... | collective-permute-start | bytes 1572872 | tf_op jit(solution)/shard_map/ppermute | solution.py:121
  89.3 178.1 %all-to-all-start.4 = ((bf16[8,1056,256]{2,1,0:T(8,128)(2,1)}), bf16[8,1056,256]{2,1,0:T(8,128)(2,1)}, u32[]{:S(2)}, u32[]{:S(2)}) async-start(bf16[8,1056,256]{2,1,0:T(8,128)(2,1)} %pad_maximum_fusion), calls=%async_computation.4 | async-start | bytes 8650752 | tf_op jit(solution)/shard_map/all_to_all | solution.py:110
  93.9 77.4 %collective-permute-start.13 = (bf16[1,2,1,256,768]{4,3,2,1,0:T(8,128)(2,1)}, bf16[1,2,1,256,768]{4,3,2,1,0:T(8,128)(2,1)}, u32[]{:S(2)}, u32[]{:S(2)}) collective-permute-start(bf16[1,2,1,256,768]{4,3,2,1,0:T(8,128)(2,1)} %pad_maximum_fusion.12), channel_id=1, source_target_pairs={{0,16},{4,20},{8,24},{12,28},{16,0},{20,4},{24,8},{28,12},{1,17},{... | collective-permute-start | bytes 2359304 | tf_op jit(solution)/shard_map/ppermute | solution.py:121
  95.8 72.1 %collective-permute-start.6 = (bf16[1,1,1,4,64,640]{5,4,3,2,1,0:T(8,128)(2,1)}, bf16[1,1,1,4,64,640]{5,4,3,2,1,0:T(8,128)(2,1)}, u32[]{:S(2)}, u32[]{:S(2)}) collective-permute-start(bf16[1,1,1,4,64,640]{5,4,3,2,1,0:T(8,128)(2,1)} %bitcast.2), channel_id=1, source_target_pairs={{0,16},{4,20},{8,24},{12,28},{16,0},{20,4},{24,8},{28,12},{1,17},{... | collective-permute-start | bytes 983048 | tf_op jit(solution)/shard_map/ppermute | solution.py:121
  96.0 75.2 %collective-permute-start.31 = (bf16[128,2048]{1,0:T(8,128)(2,1)}, bf16[128,2048]{1,0:T(8,128)(2,1)}, u32[]{:S(2)}, u32[]{:S(2)}) collective-permute-start(bf16[128,2048]{1,0:T(8,128)(2,1)} %collective-permute-done.30.refs_1_), channel_id=1, source_target_pairs={{0,3},{1,0},{2,1},{3,2},{4,7},{5,4},{6,5},{7,6},{8,11},{9,8},{10,9... | collective-permute-start | bytes 1572872 | tf_op jit(solution)/shard_map/ppermute | solution.py:77
  104.2 91.6 %collective-permute-start.34 = (bf16[1,2,1,1056,256]{4,3,2,1,0:T(8,128)(2,1)}, bf16[1,2,1,1056,256]{4,3,2,1,0:T(8,128)(2,1)}, u32[]{:S(2)}, u32[]{:S(2)}) collective-permute-start(bf16[1,2,1,1056,256]{4,3,2,1,0:T(8,128)(2,1)} %pad_maximum_fusion.8), channel_id=1, source_target_pairs={{0,16},{4,20},{8,24},{12,28},{16,0},{20,4},{24,8},{28,12},{1,17},{... | collective-permute-start | bytes 3244040 | tf_op jit(solution)/shard_map/ppermute | solution.py:121
  186.3 63.8 %collective-permute-start.37 = (bf16[2,1,1,1056,256]{4,3,2,1,0:T(8,128)(2,1)}, bf16[2,1,1,1056,256]{4,3,2,1,0:T(8,128)(2,1)}, u32[]{:S(2)}, u32[]{:S(2)}) collective-permute-start(bf16[2,1,1,1056,256]{4,3,2,1,0:T(8,128)(2,1)} %pad_maximum_fusion.9), channel_id=1, source_target_pairs={{0,8},{4,12},{8,0},{12,4},{16,24},{20,28},{24,16},{28,20},{1,9},{5... | collective-permute-start | bytes 3244040 | tf_op jit(solution)/shard_map/ppermute | solution.py:121
  236.9 95.3 %collective-permute-start.35 = (bf16[2,2,1,1056,256]{4,3,2,1,0:T(8,128)(2,1)}, bf16[2,2,1,1056,256]{4,3,2,1,0:T(8,128)(2,1)}, u32[]{:S(2)}, u32[]{:S(2)}) collective-permute-start(bf16[2,2,1,1056,256]{4,3,2,1,0:T(8,128)(2,1)} %pad_maximum_fusion.3), channel_id=1, source_target_pairs={{0,4},{4,0},{8,12},{12,8},{16,20},{20,16},{24,28},{28,24},{1,5},{5... | collective-permute-start | bytes 6488072 | tf_op jit(solution)/shard_map/ppermute | solution.py:121
  267.3 64.9 %collective-permute-start.38 = (bf16[2,2,1,1056,256]{4,3,2,1,0:T(8,128)(2,1)}, bf16[2,2,1,1056,256]{4,3,2,1,0:T(8,128)(2,1)}, u32[]{:S(2)}, u32[]{:S(2)}) collective-permute-start(bf16[2,2,1,1056,256]{4,3,2,1,0:T(8,128)(2,1)} %pad_maximum_fusion.4), channel_id=1, source_target_pairs={{0,4},{4,0},{8,12},{12,8},{16,20},{20,16},{24,28},{28,24},{1,5},{5... | collective-permute-start | bytes 6488072 | tf_op jit(solution)/shard_map/ppermute | solution.py:121
  267.3 90.0 %all-to-all-start.3 = ((bf16[8,96,2048]{2,1,0:T(8,128)(2,1)}), bf16[8,96,2048]{2,1,0:T(8,128)(2,1)S(1)}, u32[]{:S(2)}, u32[]{:S(2)}) async-start(bf16[8,96,2048]{2,1,0:T(8,128)(2,1)} %bitcast.221), calls=%async_computation.3 | async-start | bytes 6291456 | tf_op jit(solution)/shard_map/all_to_all | solution.py:110
  362.6 60.6 %collective-permute-start.72 = (bf16[2,2,1,1056,256]{4,3,2,1,0:T(8,128)(2,1)}, bf16[2,2,1,1056,256]{4,3,2,1,0:T(8,128)(2,1)}, u32[]{:S(2)}, u32[]{:S(2)}) collective-permute-start(bf16[2,2,1,1056,256]{4,3,2,1,0:T(8,128)(2,1)} %bitcast.253), channel_id=1, source_target_pairs={{0,4},{4,0},{8,12},{12,8},{16,20},{20,16},{24,28},{28,24},{1,5},{5... | collective-permute-start | bytes 6488072 | tf_op jit(solution)/shard_map/ppermute | solution.py:121
  376.5 66.7 %collective-permute-start.76 = (bf16[2,1,1,1056,256]{4,3,2,1,0:T(8,128)(2,1)}, bf16[2,1,1,1056,256]{4,3,2,1,0:T(8,128)(2,1)}, u32[]{:S(2)}, u32[]{:S(2)}) collective-permute-start(bf16[2,1,1,1056,256]{4,3,2,1,0:T(8,128)(2,1)} %dynamic-slice_convert_fusion), channel_id=1, source_target_pairs={{0,8},{4,12},{8,0},{12,4},{16,24},{20,28},{24,16},{28,20},{1,9},{5... | collective-permute-start | bytes 3244040 | tf_op jit(solution)/shard_map/ppermute | solution.py:121
  419.2 70.9 %all-to-all-start.6 = ((bf16[8,96,2176]{2,1,0:T(8,128)(2,1)}), bf16[8,96,2176]{2,1,0:T(8,128)(2,1)S(1)}, u32[]{:S(2)}, u32[]{:S(2)}) async-start(bf16[8,96,2176]{2,1,0:T(8,128)(2,1)} %bitcast.216), calls=%async_computation.6 | async-start | bytes 6684672 | tf_op jit(solution)/shard_map/all_to_all | solution.py:110
  429.0 57.0 %collective-permute-start.73 = (bf16[1,2,1,1056,256]{4,3,2,1,0:T(8,128)(2,1)}, bf16[1,2,1,1056,256]{4,3,2,1,0:T(8,128)(2,1)}, u32[]{:S(2)}, u32[]{:S(2)}) collective-permute-start(bf16[1,2,1,1056,256]{4,3,2,1,0:T(8,128)(2,1)} %dynamic-slice_convert_fusion.1), channel_id=1, source_target_pairs={{0,16},{4,20},{8,24},{12,28},{16,0},{20,4},{24,8},{28,12},{1,17},{... | collective-permute-start | bytes 3244040 | tf_op jit(solution)/shard_map/ppermute | solution.py:121
  446.5 50.5 %collective-permute-start.77 = (bf16[1,1,1,1056,256]{4,3,2,1,0:T(8,128)(2,1)}, bf16[1,1,1,1056,256]{4,3,2,1,0:T(8,128)(2,1)}, u32[]{:S(2)}, u32[]{:S(2)}) collective-permute-start(bf16[1,1,1,1056,256]{4,3,2,1,0:T(8,128)(2,1)} %dynamic-slice_convert_fusion.4), channel_id=1, source_target_pairs={{0,16},{4,20},{8,24},{12,28},{16,0},{20,4},{24,8},{28,12},{1,17},{... | collective-permute-start | bytes 1622024 | tf_op jit(solution)/shard_map/ppermute | solution.py:121
  491.7 44.7 %all-to-all-start.5 = ((bf16[8,96,2048]{2,1,0:T(8,128)(2,1)}), bf16[8,96,2048]{2,1,0:T(8,128)(2,1)}, u32[]{:S(2)}, u32[]{:S(2)}) async-start(bf16[8,96,2048]{2,1,0:T(8,128)(2,1)} %bitcast.222), calls=%async_computation.5 | async-start | bytes 6291456 | tf_op jit(solution)/shard_map/all_to_all | solution.py:110
  536.4 72.1 %all-to-all-start.9 = ((bf16[8,1056,256]{2,1,0:T(8,128)(2,1)}), bf16[8,1056,256]{2,1,0:T(8,128)(2,1)}, u32[]{:S(2)}, u32[]{:S(2)}) async-start(bf16[8,1056,256]{2,1,0:T(8,128)(2,1)} %get-tuple-element.51), calls=%async_computation.9 | async-start | bytes 8650752 | tf_op jit(solution)/shard_map/all_to_all | solution.py:110
  574.8 44.7 %collective-permute-start.40 = (bf16[128,2048]{1,0:T(8,128)(2,1)}, bf16[128,2048]{1,0:T(8,128)(2,1)}, u32[]{:S(2)}, u32[]{:S(2)}) collective-permute-start(bf16[128,2048]{1,0:T(8,128)(2,1)} %fusion.42), channel_id=1, source_target_pairs={{0,1},{1,2},{2,3},{3,0},{4,5},{5,6},{6,7},{7,4},{8,9},{9,10},{10,1... | collective-permute-start | bytes 1572872 | tf_op jit(solution)/shard_map/ppermute | solution.py:77
  621.8 111.9 %collective-permute-start.41 = (bf16[128,2048]{1,0:T(8,128)(2,1)}, bf16[128,2048]{1,0:T(8,128)(2,1)}, u32[]{:S(2)}, u32[]{:S(2)}) collective-permute-start(bf16[128,2048]{1,0:T(8,128)(2,1)} %fusion.41), channel_id=1, source_target_pairs={{0,1},{1,2},{2,3},{3,0},{4,5},{5,6},{6,7},{7,4},{8,9},{9,10},{10,1... | collective-permute-start | bytes 1572872 | tf_op jit(solution)/shard_map/ppermute | solution.py:77
  661.4 75.4 %collective-permute-start.69 = (bf16[2,2,1,512,256]{4,3,2,1,0:T(8,128)(2,1)}, bf16[2,2,1,512,256]{4,3,2,1,0:T(8,128)(2,1)}, u32[]{:S(2)}, u32[]{:S(2)}) collective-permute-start(bf16[2,2,1,512,256]{4,3,2,1,0:T(8,128)(2,1)} %constant_dynamic-slice_fusion), channel_id=1, source_target_pairs={{0,4},{4,0},{8,12},{12,8},{16,20},{20,16},{24,28},{28,24},{1,5},{5... | collective-permute-start | bytes 3145736 | tf_op jit(solution)/shard_map/ppermute | solution.py:121
  (192 other events, 2447.4 us)

commit v4 on v3

--- a/solution.py
+++ b/solution.py
@@ -148,7 +148,7 @@
     pair = isinstance(blocks, (tuple, list))
     own = blocks[0].shape[1:] if pair else blocks.shape[1:]
     current = None if pair else blocks.reshape((2,) * bits + own)
-    for mask in order[::-1]:
+    for step, mask in enumerate(order[::-1]):
         high = ((index & mask) > 0).astype(jnp.int32)
         axis = axis_of(mask)
         if current is None:
@@ -158,6 +158,8 @@
             give = lax.dynamic_slice_in_dim(current, 1 - high, 1, axis).astype(jnp.bfloat16)
         got = swap_dp(give, mask)
         current = keep.astype(jnp.float32) + got.astype(jnp.float32)
+        if step + 1 < bits:
+            current = current.astype(jnp.bfloat16)
     return current.reshape(own)
 
 
@@ -304,6 +306,28 @@
     return out, back, results[:2], results[2:]
 
 
+def column_gradient(left, right, bit):
+    count = lax.axis_size(DP)
+    rows, width = left.shape[1], right.shape[1]
+    part = width // count
+    if part % LANES:
+        return part_by(tall_blocks(left_dot(left, right)), bit)
+
+    def body(bit_ref, left_ref, right_ref, keep_ref, give_ref, whole_ref):
+        whole_ref[...] = dot_of(left_ref[...], right_ref[...], (0, 0)).astype(jnp.bfloat16)
+        for j in range(count // 2):
+            for ref, own in ((keep_ref, bit_ref[0]), (give_ref, 1 - bit_ref[0])):
+                ref[j] = whole_ref[:, pl.ds(pl.multiple_of((2 * j + own) * part, LANES), part)]
+
+    vmem = pl.BlockSpec(memory_space=pltpu.VMEM)
+    return pl.pallas_call(
+        body,
+        in_specs=[pl.BlockSpec(memory_space=pltpu.SMEM), vmem, vmem],
+        out_shape=[jax.ShapeDtypeStruct((count // 2, rows, part), jnp.bfloat16)] * 2,
+        scratch_shapes=[pltpu.VMEM((rows, width), jnp.bfloat16)],
+    )(bit.reshape(1), left, right)
+
+
 def load_slab(slab_ref, wide_ref, place, units):
     part = slab_ref.shape[2]
     for j in range(slab_ref.shape[0]):
@@ -453,6 +477,15 @@
 def two_lanes(high, low):
     lane = lax.broadcasted_iota(jnp.int32, (high.shape[0], LANES), 1)
     return jnp.where(lane == 0, high, jnp.where(lane == 1, low, 0.0)).astype(jnp.bfloat16)
+
+
+def added_rows(pick, routed, share):
+    def body(pick_ref, routed_ref, share_ref, out_ref):
+        values = share_ref[...].astype(jnp.float32)
+        values = values + dot_of(pick_ref[...], routed_ref[...], (1, 0))
+        out_ref[...] = values.astype(jnp.bfloat16)
+
+    return call_kernel(body, [(share.shape, jnp.bfloat16)], [], pick, routed, share)[0]
 
 
 def combined_rows(pick, back, share):
@@ -632,12 +665,12 @@
     )
     residual_low = gather_tensor(after_attn_grad.astype(narrow))
     residual_low = joined(residual_low)
-    moe_share = moe_share.astype(wide) + matmul(pick, routed_flat)
+    moe_share = added_rows(pick, routed_flat, moe_share)
     moe_own = scatter_tensor(moe_share, 1)
     block_out = (after_attn + moe_own).astype(narrow)
 
     mixed_grad = right_dot(residual_low, output_full).astype(narrow).reshape(group, heads, VDIM)
-    output_grad = left_dot(mixed_flat, residual_low)
+    output_grad = column_gradient(mixed_flat, residual_low, lax.axis_index(DP) & 1)
     query_nope_grad, query_rope_grad, key_nope_grad, key_rope_grad, values_grad = attend_backward(
             query_nope, query_rope, key_nope, key_rope, values, mixed, mixed_grad, logsum, seen
     )
@@ -659,7 +692,7 @@
         .reshape(group, heads * (NOPE + ROPE))
     )
     hidden_one_share = right_dot(query_grad, query_full) + right_dot(latent_in_low, kv_down)
-    hidden_one_grad = scatter_tensor(hidden_one_share)
+    hidden_one_grad = scatter_tensor(hidden_one_share, 1)
     query_wgrad = left_dot(hidden_one, query_grad)
     kv_up_grad = left_dot(latent, keyvalue_grad)
     scale_one = rms_scale(residual_in)
@@ -678,7 +711,7 @@
         shared_second[:shared_units].T,
         jnp.concatenate([shared_first[shared_units:], shared_second[shared_units:]]),
     )
-    output_grad = scatter_dp(tall_blocks(output_grad), second_order)
+    output_grad = scatter_dp(output_grad, second_order)
     query_wgrad = query_wgrad.astype(narrow).reshape(dp_count, -1, query_wgrad.shape[1])
     query_wgrad = scatter_dp(query_wgrad, first_order)
     kv_up_grad = kv_up_grad.astype(narrow).reshape(dp_count, -1, kv_up_grad.shape[1])

time: 794 us -> 783 us (0.986)
  waiting for transfers between devices: 362 us -> 344 us
  Pallas kernels: 77.1 us -> 87.8 us
    convert_element_type x0 -> x12, other arithmetic: none -> 16.7 us  [scatter_dp(): current = current.astype(jnp.bfloat16)]
    all_to_all x10, waiting for transfers between devices: 48.2 us -> 34.1 us  [exchange(): return lax.all_to_all(values, axes, split_axis=0, concat_axis=0, tiled=True)]
    add x14 -> x2, other arithmetic: 15.9 us -> 2.42 us  [scatter_dp(): current = keep.astype(jnp.float32) + got.astype(jnp.float32)]
    unnamed x258 -> x252, local copies, waits for them, and re-layouts: 25.9 us -> 19 us
    pallas_call x7 -> x8, Pallas kernels: 52.1 us -> 58.1 us  [call_kernel(): pl.pallas_call(body, out_shape=[jax.ShapeDtypeStruct(shape, dtype) for sh...]
    ppermute x42 -> x39, waiting for transfers between devices: 157 us -> 159 us  [send_tensor(): lax.ppermute(values, TENSOR, [(i, (i + step) % count) for i in range(coun...]
    ppermute x42 -> x39, starting transfers between devices: 56.1 us -> 54.9 us  [send_tensor(): lax.ppermute(values, TENSOR, [(i, (i + step) % count) for i in range(coun...]
  transfers between devices with their start and end apart: 88 -> 85, of which waited for: 41 -> 39; matrix products, arithmetic and copies ran while one was open for 24% -> 24% of each run, Pallas kernels for 10% -> 11%
where the time goes in v4:
time: 783 us; the launch traced here: 773 us
  waiting for transfers between devices  344 us (44%)
  starting transfers between devices  129 us (16%)
  other arithmetic  93.7 us (12%)
  Pallas kernels  87.8 us (11%)
  local copies, waits for them, and re-layouts  62.9 us (8%)
  matrix products  52 us (7%)
    ppermute x39, waiting for transfers between devices, send_tensor(): lax.ppermute(values, TENSOR, [(i, (i + step) % count) for i in range(coun...  159 us
    ppermute x36, waiting for transfers between devices, swap_dp(): return lax.ppermute(values, DP, [(i, i ^ mask) for i in range(count)])  151 us
    pallas_call x8, Pallas kernels, call_kernel(): pl.pallas_call(body, out_shape=[jax.ShapeDtypeStruct(shape, dtype) for sh...  58.1 us
    ppermute x39, starting transfers between devices, send_tensor(): lax.ppermute(values, TENSOR, [(i, (i + step) % count) for i in range(coun...  54.9 us
    all_to_all x10, starting transfers between devices, exchange(): return lax.all_to_all(values, axes, split_axis=0, concat_axis=0, tiled=True)  45.4 us
    all_to_all x10, waiting for transfers between devices, exchange(): return lax.all_to_all(values, axes, split_axis=0, concat_axis=0, tiled=True)  34.1 us
    ppermute x36, starting transfers between devices, swap_dp(): return lax.ppermute(values, DP, [(i, i ^ mask) for i in range(count)])  28.8 us
    pallas_call x1, Pallas kernels, shared_kernel(): pl.pallas_call(body, in_specs=[pl.BlockSpec(memory_space=pltpu.SMEM)] + [...  25.2 us
  transfers between devices with their start and end apart: 85, of which 39 were waited for; matrix products, arithmetic and copies ran while one was open for 24% of the time, Pallas kernels for 11%

profile of v4, /device:TPU:0, one launch (start us, length us, event | category | flops | bytes accessed | tf_op | source)
XLA Modules:
  0.0 772.6 jit_solution(4492030036368341355)
XLA Ops:
  41.4 13.8 %collective-permute-done.10 = bf16[2,1,1,64,1024]{4,3,2,1,0:T(8,128)(2,1)S(1)} collective-permute-done((bf16[2,1,1,64,1024]{4,3,2,1,0:T(8,128)(2,1)S(1)}, bf16[2,1,1,64,1024]{4,3,2,1,0:T(8,128)(2,1)S(1)}, u32[]{:S(2)}, u32[]{:S(2)}) %collective-permute-start.10) | collective-permute-done | bytes 262176 | tf_op jit(solution)/shard_map/ppermute | solution.py:121
  65.1 13.6 %collective-permute-done.2.refs_4_ = bf16[64,2048]{1,0:T(8,128)(2,1)} collective-permute-done((bf16[64,2048]{1,0:T(8,128)(2,1)}, bf16[64,2048]{1,0:T(8,128)(2,1)}, u32[]{:S(2)}, u32[]{:S(2)}) %collective-permute-start.2) | collective-permute-done | bytes 262176 | tf_op jit(solution)/shard_map/ppermute | solution.py:77
  106.1 60.8 %collective-permute-done.6 = bf16[1,1,1,4,64,640]{5,4,3,2,1,0:T(8,128)(2,1)} collective-permute-done((bf16[1,1,1,4,64,640]{5,4,3,2,1,0:T(8,128)(2,1)}, bf16[1,1,1,4,64,640]{5,4,3,2,1,0:T(8,128)(2,1)}, u32[]{:S(2)}, u32[]{:S(2)}) %collective-permute-start.6) | collective-permute-done | bytes 327712 | tf_op jit(solution)/shard_map/ppermute | solution.py:121
  174.4 11.0 %collective-permute-done.7 = bf16[2,1,1,4,64,640]{5,4,3,2,1,0:T(8,128)(2,1)S(1)} collective-permute-done((bf16[2,1,1,4,64,640]{5,4,3,2,1,0:T(8,128)(2,1)S(1)}, bf16[2,1,1,4,64,640]{5,4,3,2,1,0:T(8,128)(2,1)S(1)}, u32[]{:S(2)}, u32[]{:S(2)}) %collective-permute-start.7) | collective-permute-done | bytes 655392 | tf_op jit(solution)/shard_map/ppermute | solution.py:121
  236.2 7.1 collective-permute-done.18
  250.6 9.1 %collective-permute-done.19 = bf16[64,2048]{1,0:T(8,128)(2,1)S(1)} collective-permute-done((bf16[64,2048]{1,0:T(8,128)(2,1)S(1)}, bf16[64,2048]{1,0:T(8,128)(2,1)S(1)}, u32[]{:S(2)}, u32[]{:S(2)}) %collective-permute-start.19) | collective-permute-done | bytes 262176 | tf_op jit(solution)/shard_map/ppermute | solution.py:77
  265.8 9.4 %collective-permute-done.20 = bf16[64,2048]{1,0:T(8,128)(2,1)S(1)} collective-permute-done((bf16[64,2048]{1,0:T(8,128)(2,1)S(1)}, bf16[64,2048]{1,0:T(8,128)(2,1)S(1)}, u32[]{:S(2)}, u32[]{:S(2)}) %collective-permute-start.20) | collective-permute-done | bytes 262176 | tf_op jit(solution)/shard_map/ppermute | solution.py:77
  286.5 9.1 %collective-permute-done.24.refs_2_ = bf16[64,2048]{1,0:T(8,128)(2,1)S(1)} collective-permute-done((bf16[64,2048]{1,0:T(8,128)(2,1)S(1)}, bf16[64,2048]{1,0:T(8,128)(2,1)S(1)}, u32[]{:S(2)}, u32[]{:S(2)}) %collective-permute-start.24) | collective-permute-done | bytes 262176 | tf_op jit(solution)/shard_map/ppermute | solution.py:77
  312.4 10.3 %collective-permute-start.29 = (bf16[64,2048]{1,0:T(8,128)(2,1)S(1)}, bf16[64,2048]{1,0:T(8,128)(2,1)}, u32[]{:S(2)}, u32[]{:S(2)}) collective-permute-start(bf16[64,2048]{1,0:T(8,128)(2,1)S(1)} %collective-permute-done.27.refs_5_), channel_id=1, source_target_pairs={{0,3},{1,0},{2,1},{3,2},{4,7},{5,4},{6,5},{7,6},{8,11},{9,8},{10,9... | collective-permute-start | bytes 786440 | tf_op jit(solution)/shard_map/ppermute | solution.py:77
  334.7 25.2 %shard_map.293 = (bf16[512,2048]{1,0:T(8,128)(2,1)}, f32[512,2048]{1,0:T(8,128)}, bf16[4,1056,256]{2,1,0:T(8,128)(2,1)}, bf16[4,1056,256]{2,1,0:T(8,128)(2,1)}, ...) custom-call(s32[1]{0:T(128)} %bitcast.33.bit_ref, bf16[512,2048]{1,0:T(8,128)(2,1)} %get-tuple-element.43.x_ref, ...), custom_call_target="tpu_custom_call" | custom-call | tf_op jit(solution)/shard_map/pallas_call | solution.py:297
  384.2 22.0 %all-to-all-done.2 = bf16[8,96,2176]{2,1,0:T(8,128)(2,1)S(1)} async-done(((bf16[8,96,2176]{2,1,0:T(8,128)(2,1)}), bf16[8,96,2176]{2,1,0:T(8,128)(2,1)S(1)}, u32[]{:S(2)}, u32[]{:S(2)}) %all-to-all-start.2) | async-done | bytes 3342368 | tf_op jit(solution)/shard_map/all_to_all | solution.py:110
  407.9 14.3 %shard_map.291 = (bf16[768,2176]{1,0:T(8,128)(2,1)}, bf16[768,352]{1,0:T(8,128)(2,1)}, bf16[768,352]{1,0:T(8,128)(2,1)}, bf16[768,352]{1,0:T(8,128)(2,1)}) custom-call(bf16[768,2176]{1,0:T(8,128)(2,1)} %bitcast.194, bf16[768,2048]{1,0:T(8,128)(2,1)} %bitcast.198, bf16[8,1056,256]{2,1,0:T(8,128)(2,1)} %all-to-all-done.4.slab_ref), custom_call_target="tpu_custom_call" | custom-call | tf_op jit(solution)/shard_map/pallas_call | solution.py:230
  431.6 11.9 %shard_map.292 = (bf16[768,2048]{1,0:T(8,128)(2,1)}, bf16[8,1056,256]{2,1,0:T(8,128)(2,1)}) custom-call(bf16[768,2176]{1,0:T(8,128)(2,1)} %bitcast.195, bf16[768,2048]{1,0:T(8,128)(2,1)} %bitcast.199, bf16[8,1056,256]{2,1,0:T(8,128)(2,1)} %all-to-all-done.4.slab_ref, bf16[768,352]{1,0:T(8,128)(2,1)} %get-tuple-element.39.da_ref, ...), custom_call_target="tpu_custom_call" | custom-call | tf_op jit(solution)/shard_map/pallas_call | solution.py:230
  445.7 43.1 %collective-permute-done.70 = bf16[1,2,1,1056,256]{4,3,2,1,0:T(8,128)(2,1)} collective-permute-done((bf16[1,2,1,1056,256]{4,3,2,1,0:T(8,128)(2,1)}, bf16[1,2,1,1056,256]{4,3,2,1,0:T(8,128)(2,1)}, u32[]{:S(2)}, u32[]{:S(2)}) %collective-permute-start.70) | collective-permute-done | bytes 1081376 | tf_op jit(solution)/shard_map/ppermute | solution.py:121
  492.1 7.5 collective-permute-done.74
  510.1 7.0 shard_map.295
  523.3 6.8 collective-permute-done.42
  538.1 7.5 all-to-all-done.5
  563.8 10.5 %collective-permute-done.39 = bf16[128,2048]{1,0:T(8,128)(2,1)S(1)} collective-permute-done((bf16[128,2048]{1,0:T(8,128)(2,1)S(1)}, bf16[128,2048]{1,0:T(8,128)(2,1)S(1)}, u32[]{:S(2)}, u32[]{:S(2)}) %collective-permute-start.39) | collective-permute-done | bytes 524320 | tf_op jit(solution)/shard_map/ppermute | solution.py:77
  674.6 7.5 all-to-all-start.7
  697.0 11.3 %collective-permute-done.54 = bf16[128,2048]{1,0:T(8,128)(2,1)} collective-permute-done((bf16[128,2048]{1,0:T(8,128)(2,1)}, bf16[128,2048]{1,0:T(8,128)(2,1)}, u32[]{:S(2)}, u32[]{:S(2)}) %collective-permute-start.54) | collective-permute-done | bytes 524320 | tf_op jit(solution)/shard_map/ppermute | solution.py:77
  716.2 10.5 %collective-permute-done.55 = bf16[128,2048]{1,0:T(8,128)(2,1)S(1)} collective-permute-done((bf16[128,2048]{1,0:T(8,128)(2,1)S(1)}, bf16[128,2048]{1,0:T(8,128)(2,1)S(1)}, u32[]{:S(2)}, u32[]{:S(2)}) %collective-permute-start.55) | collective-permute-done | bytes 524320 | tf_op jit(solution)/shard_map/ppermute | solution.py:77
  732.6 7.0 collective-permute-done.56
  744.6 10.4 %collective-permute-done.58 = bf16[1,2,1,256,768]{4,3,2,1,0:T(8,128)(2,1)S(1)} collective-permute-done((bf16[1,2,1,256,768]{4,3,2,1,0:T(8,128)(2,1)S(1)}, bf16[1,2,1,256,768]{4,3,2,1,0:T(8,128)(2,1)S(1)}, u32[]{:S(2)}, u32[]{:S(2)}) %collective-permute-start.58) | collective-permute-done | bytes 786464 | tf_op jit(solution)/shard_map/ppermute | solution.py:121
  (600 shorter events, 423.1 us)
Async XLA Ops:
  2.5 60.7 %collective-permute-start = (bf16[64,2048]{1,0:T(8,128)(2,1)}, bf16[64,2048]{1,0:T(8,128)(2,1)}, u32[]{:S(2)}, u32[]{:S(2)}) collective-permute-start(bf16[64,2048]{1,0:T(8,128)(2,1)} %get-tuple-element.125.refs_0_), channel_id=1, source_target_pairs={{0,3},{1,0},{2,1},{3,2},{4,7},{5,4},{6,5},{7,6},{8,11},{9,8},{10,9... | collective-permute-start | bytes 786440 | tf_op jit(solution)/shard_map/ppermute | solution.py:77
  7.6 56.2 %collective-permute-start.1 = (bf16[64,2048]{1,0:T(8,128)(2,1)}, bf16[64,2048]{1,0:T(8,128)(2,1)}, u32[]{:S(2)}, u32[]{:S(2)}) collective-permute-start(bf16[64,2048]{1,0:T(8,128)(2,1)} %get-tuple-element.124.refs_1_), channel_id=1, source_target_pairs={{0,3},{1,0},{2,1},{3,2},{4,7},{5,4},{6,5},{7,6},{8,11},{9,8},{10,9... | collective-permute-start | bytes 786440 | tf_op jit(solution)/shard_map/ppermute | solution.py:77
  13.3 44.3 %collective-permute-start.12 = (bf16[1,1,1,256,768]{4,3,2,1,0:T(8,128)(2,1)}, bf16[1,1,1,256,768]{4,3,2,1,0:T(8,128)(2,1)}, u32[]{:S(2)}, u32[]{:S(2)}) collective-permute-start(bf16[1,1,1,256,768]{4,3,2,1,0:T(8,128)(2,1)} %bitcast.241), channel_id=1, source_target_pairs={{0,8},{4,12},{8,0},{12,4},{16,24},{20,28},{24,16},{28,20},{1,9},{5... | collective-permute-start | bytes 1179656 | tf_op jit(solution)/shard_map/ppermute | solution.py:121
  30.8 57.5 %all-to-all-start.1 = ((bf16[4,64,640]{2,1,0:T(8,128)(2,1)}), bf16[4,64,640]{2,1,0:T(8,128)(2,1)}, u32[]{:S(2)}, u32[]{:S(2)}) async-start(bf16[4,64,640]{2,1,0:T(8,128)(2,1)} %broadcast_in_dim.19), calls=%async_computation.1 | async-start | bytes 655360 | tf_op jit(solution)/shard_map/all_to_all | solution.py:110
  78.6 89.5 %collective-permute-start.11 = (bf16[2,2,1,64,1024]{4,3,2,1,0:T(8,128)(2,1)}, bf16[2,2,1,64,1024]{4,3,2,1,0:T(8,128)(2,1)}, u32[]{:S(2)}, u32[]{:S(2)}) collective-permute-start(bf16[2,2,1,64,1024]{4,3,2,1,0:T(8,128)(2,1)} %pad_maximum_fusion.16), channel_id=1, source_target_pairs={{0,4},{4,0},{8,12},{12,8},{16,20},{20,16},{24,28},{28,24},{1,5},{5... | collective-permute-start | bytes 1572872 | tf_op jit(solution)/shard_map/ppermute | solution.py:121
  88.4 192.0 %all-to-all-start.4 = ((bf16[8,1056,256]{2,1,0:T(8,128)(2,1)}), bf16[8,1056,256]{2,1,0:T(8,128)(2,1)}, u32[]{:S(2)}, u32[]{:S(2)}) async-start(bf16[8,1056,256]{2,1,0:T(8,128)(2,1)} %pad_maximum_fusion), calls=%async_computation.4 | async-start | bytes 8650752 | tf_op jit(solution)/shard_map/all_to_all | solution.py:110
  92.9 77.4 %collective-permute-start.13 = (bf16[1,2,1,256,768]{4,3,2,1,0:T(8,128)(2,1)}, bf16[1,2,1,256,768]{4,3,2,1,0:T(8,128)(2,1)}, u32[]{:S(2)}, u32[]{:S(2)}) collective-permute-start(bf16[1,2,1,256,768]{4,3,2,1,0:T(8,128)(2,1)} %pad_maximum_fusion.12), channel_id=1, source_target_pairs={{0,16},{4,20},{8,24},{12,28},{16,0},{20,4},{24,8},{28,12},{1,17},{... | collective-permute-start | bytes 2359304 | tf_op jit(solution)/shard_map/ppermute | solution.py:121
  94.9 72.1 %collective-permute-start.6 = (bf16[1,1,1,4,64,640]{5,4,3,2,1,0:T(8,128)(2,1)}, bf16[1,1,1,4,64,640]{5,4,3,2,1,0:T(8,128)(2,1)}, u32[]{:S(2)}, u32[]{:S(2)}) collective-permute-start(bf16[1,1,1,4,64,640]{5,4,3,2,1,0:T(8,128)(2,1)} %bitcast.2), channel_id=1, source_target_pairs={{0,16},{4,20},{8,24},{12,28},{16,0},{20,4},{24,8},{28,12},{1,17},{... | collective-permute-start | bytes 983048 | tf_op jit(solution)/shard_map/ppermute | solution.py:121
  95.1 75.2 %collective-permute-start.31 = (bf16[128,2048]{1,0:T(8,128)(2,1)}, bf16[128,2048]{1,0:T(8,128)(2,1)}, u32[]{:S(2)}, u32[]{:S(2)}) collective-permute-start(bf16[128,2048]{1,0:T(8,128)(2,1)} %collective-permute-done.30.refs_1_), channel_id=1, source_target_pairs={{0,3},{1,0},{2,1},{3,2},{4,7},{5,4},{6,5},{7,6},{8,11},{9,8},{10,9... | collective-permute-start | bytes 1572872 | tf_op jit(solution)/shard_map/ppermute | solution.py:77
  103.3 91.5 %collective-permute-start.34 = (bf16[1,2,1,1056,256]{4,3,2,1,0:T(8,128)(2,1)}, bf16[1,2,1,1056,256]{4,3,2,1,0:T(8,128)(2,1)}, u32[]{:S(2)}, u32[]{:S(2)}) collective-permute-start(bf16[1,2,1,1056,256]{4,3,2,1,0:T(8,128)(2,1)} %pad_maximum_fusion.8), channel_id=1, source_target_pairs={{0,16},{4,20},{8,24},{12,28},{16,0},{20,4},{24,8},{28,12},{1,17},{... | collective-permute-start | bytes 3244040 | tf_op jit(solution)/shard_map/ppermute | solution.py:121
  185.4 63.8 %collective-permute-start.37 = (bf16[2,1,1,1056,256]{4,3,2,1,0:T(8,128)(2,1)}, bf16[2,1,1,1056,256]{4,3,2,1,0:T(8,128)(2,1)}, u32[]{:S(2)}, u32[]{:S(2)}) collective-permute-start(bf16[2,1,1,1056,256]{4,3,2,1,0:T(8,128)(2,1)} %pad_maximum_fusion.9), channel_id=1, source_target_pairs={{0,8},{4,12},{8,0},{12,4},{16,24},{20,28},{24,16},{28,20},{1,9},{5... | collective-permute-start | bytes 3244040 | tf_op jit(solution)/shard_map/ppermute | solution.py:121
  236.0 98.7 %collective-permute-start.35 = (bf16[2,2,1,1056,256]{4,3,2,1,0:T(8,128)(2,1)}, bf16[2,2,1,1056,256]{4,3,2,1,0:T(8,128)(2,1)}, u32[]{:S(2)}, u32[]{:S(2)}) collective-permute-start(bf16[2,2,1,1056,256]{4,3,2,1,0:T(8,128)(2,1)} %pad_maximum_fusion.3), channel_id=1, source_target_pairs={{0,4},{4,0},{8,12},{12,8},{16,20},{20,16},{24,28},{28,24},{1,5},{5... | collective-permute-start | bytes 6488072 | tf_op jit(solution)/shard_map/ppermute | solution.py:121
  265.8 68.9 %collective-permute-start.38 = (bf16[2,2,1,1056,256]{4,3,2,1,0:T(8,128)(2,1)}, bf16[2,2,1,1056,256]{4,3,2,1,0:T(8,128)(2,1)}, u32[]{:S(2)}, u32[]{:S(2)}) collective-permute-start(bf16[2,2,1,1056,256]{4,3,2,1,0:T(8,128)(2,1)} %pad_maximum_fusion.4), channel_id=1, source_target_pairs={{0,4},{4,0},{8,12},{12,8},{16,20},{20,16},{24,28},{28,24},{1,5},{5... | collective-permute-start | bytes 6488072 | tf_op jit(solution)/shard_map/ppermute | solution.py:121
  280.4 80.0 %all-to-all-start.3 = ((bf16[8,96,2048]{2,1,0:T(8,128)(2,1)}), bf16[8,96,2048]{2,1,0:T(8,128)(2,1)S(1)}, u32[]{:S(2)}, u32[]{:S(2)}) async-start(bf16[8,96,2048]{2,1,0:T(8,128)(2,1)} %bitcast.217), calls=%async_computation.3 | async-start | bytes 6291456 | tf_op jit(solution)/shard_map/all_to_all | solution.py:110
  362.1 44.1 %all-to-all-start.2 = ((bf16[8,96,2176]{2,1,0:T(8,128)(2,1)}), bf16[8,96,2176]{2,1,0:T(8,128)(2,1)S(1)}, u32[]{:S(2)}, u32[]{:S(2)}) async-start(bf16[8,96,2176]{2,1,0:T(8,128)(2,1)} %bitcast.215), calls=%async_computation.2 | async-start | bytes 6684672 | tf_op jit(solution)/shard_map/all_to_all | solution.py:110
  378.8 64.7 %collective-permute-start.73 = (bf16[2,1,1,1056,256]{4,3,2,1,0:T(8,128)(2,1)}, bf16[2,1,1,1056,256]{4,3,2,1,0:T(8,128)(2,1)}, u32[]{:S(2)}, u32[]{:S(2)}) collective-permute-start(bf16[2,1,1,1056,256]{4,3,2,1,0:T(8,128)(2,1)} %constant_dynamic-slice_fusion.1), channel_id=1, source_target_pairs={{0,8},{4,12},{8,0},{12,4},{16,24},{20,28},{24,16},{28,20},{1,9},{5... | collective-permute-start | bytes 3244040 | tf_op jit(solution)/shard_map/ppermute | solution.py:121
  422.2 79.4 %all-to-all-start.6 = ((bf16[8,96,2176]{2,1,0:T(8,128)(2,1)}), bf16[8,96,2176]{2,1,0:T(8,128)(2,1)S(1)}, u32[]{:S(2)}, u32[]{:S(2)}) async-start(bf16[8,96,2176]{2,1,0:T(8,128)(2,1)} %bitcast.216), calls=%async_computation.6 | async-start | bytes 6684672 | tf_op jit(solution)/shard_map/all_to_all | solution.py:110
  428.3 60.5 %collective-permute-start.70 = (bf16[1,2,1,1056,256]{4,3,2,1,0:T(8,128)(2,1)}, bf16[1,2,1,1056,256]{4,3,2,1,0:T(8,128)(2,1)}, u32[]{:S(2)}, u32[]{:S(2)}) collective-permute-start(bf16[1,2,1,1056,256]{4,3,2,1,0:T(8,128)(2,1)} %constant_dynamic-slice_fusion.3), channel_id=1, source_target_pairs={{0,16},{4,20},{8,24},{12,28},{16,0},{20,4},{24,8},{28,12},{1,17},{... | collective-permute-start | bytes 3244040 | tf_op jit(solution)/shard_map/ppermute | solution.py:121
  445.5 54.2 %collective-permute-start.74 = (bf16[1,1,1,1056,256]{4,3,2,1,0:T(8,128)(2,1)S(1)}, bf16[1,1,1,1056,256]{4,3,2,1,0:T(8,128)(2,1)S(1)}, u32[]{:S(2)}, u32[]{:S(2)}) collective-permute-start(bf16[1,1,1,1056,256]{4,3,2,1,0:T(8,128)(2,1)S(1)} %constant_dynamic-slice_fusion), channel_id=1, source_target_pairs={{0,16},{4,20},{8,24},{12,28},{16,0},{20,4},{24,8},{28,12},{1,17},{... | collective-permute-start | bytes 1622024 | tf_op jit(solution)/shard_map/ppermute | solution.py:121
  545.6 63.6 %all-to-all-start.9 = ((bf16[8,1056,256]{2,1,0:T(8,128)(2,1)}), bf16[8,1056,256]{2,1,0:T(8,128)(2,1)}, u32[]{:S(2)}, u32[]{:S(2)}) async-start(bf16[8,1056,256]{2,1,0:T(8,128)(2,1)} %get-tuple-element.55), calls=%async_computation.9 | async-start | bytes 8650752 | tf_op jit(solution)/shard_map/all_to_all | solution.py:110
  576.3 43.5 %collective-permute-start.40 = (bf16[128,2048]{1,0:T(8,128)(2,1)}, bf16[128,2048]{1,0:T(8,128)(2,1)}, u32[]{:S(2)}, u32[]{:S(2)}) collective-permute-start(bf16[128,2048]{1,0:T(8,128)(2,1)} %add_convert_fusion.11), channel_id=1, source_target_pairs={{0,1},{1,2},{2,3},{3,0},{4,5},{5,6},{6,7},{7,4},{8,9},{9,10},{10,1... | collective-permute-start | bytes 1572872 | tf_op jit(solution)/shard_map/ppermute | solution.py:77
  622.0 117.9 %collective-permute-start.41 = (bf16[128,2048]{1,0:T(8,128)(2,1)}, bf16[128,2048]{1,0:T(8,128)(2,1)}, u32[]{:S(2)}, u32[]{:S(2)}) collective-permute-start(bf16[128,2048]{1,0:T(8,128)(2,1)} %add_convert_fusion.10), channel_id=1, source_target_pairs={{0,1},{1,2},{2,3},{3,0},{4,5},{5,6},{6,7},{7,4},{8,9},{9,10},{10,1... | collective-permute-start | bytes 1572872 | tf_op jit(solution)/shard_map/ppermute | solution.py:77
  657.9 56.1 %collective-permute-start.66 = (bf16[2,2,1,512,256]{4,3,2,1,0:T(8,128)(2,1)}, bf16[2,2,1,512,256]{4,3,2,1,0:T(8,128)(2,1)}, u32[]{:S(2)}, u32[]{:S(2)}) collective-permute-start(bf16[2,2,1,512,256]{4,3,2,1,0:T(8,128)(2,1)} %bitcast.249), channel_id=1, source_target_pairs={{0,4},{4,0},{8,12},{12,8},{16,20},{20,16},{24,28},{28,24},{1,5},{5... | collective-permute-start | bytes 3145736 | tf_op jit(solution)/shard_map/ppermute | solution.py:121
  666.7 60.3 %collective-permute-start.60 = (bf16[2,2,1,256,640]{4,3,2,1,0:T(8,128)(2,1)}, bf16[2,2,1,256,640]{4,3,2,1,0:T(8,128)(2,1)}, u32[]{:S(2)}, u32[]{:S(2)}) collective-permute-start(bf16[2,2,1,256,640]{4,3,2,1,0:T(8,128)(2,1)} %constant_dynamic-slice_fusion.11), channel_id=1, source_target_pairs={{0,4},{4,0},{8,12},{12,8},{16,20},{20,16},{24,28},{28,24},{1,5},{5... | collective-permute-start | bytes 3932168 | tf_op jit(solution)/shard_map/ppermute | solution.py:121
  (186 other events, 2748.2 us)
